TPU v7x, 32 devices: a whole 2x2x4 slice. The times are simulated.
32 devices in a mesh: req: 2 (over core), ctx: 16 (over z, y, x).
Axes of the slice: x: 2, y: 2, z: 4, core: 2. Of those that a mesh axis runs over, the one named last changes fastest.
Arguments:
- queries: bfloat16 [32, 8192], P(('req', 'ctx')), parts along dimension 0, may hold values from -256 to 256
- new_kv: bfloat16 [32, 2, 1024], P(('req', 'ctx')), parts along dimension 0, may hold values from -12 to 12
- prefix_kv: bfloat16 [2, 16384, 2, 1024], P('req', 'ctx'), parts along dimension 0, may hold values from -4.5 to 4.5
- pool: bfloat16 [256, 16, 2, 1024], P(('req', 'ctx')), parts along dimension 0, may hold values from -12 to 12
- out_weight: bfloat16 [8192, 8192], P('ctx'), may hold values from -0.0625 to 0.0625
- parents: int32 [32], P('req'), parts along dimension 0, may hold values from 0 to 15, as said below
- tail_table: int32 [32, 4], P('req'), parts along dimension 0, may hold values from 0 to 127, as said below
- fresh_slots: int32 [32], P('req'), parts along dimension 0, may hold values from 0 to 127, as said below
- tail_lengths: int32 [32], P('req'), parts along dimension 0, may hold values from 1 to 63
Outputs:
- attn_out: float32 [32, 8192], P(('req', 'ctx')), parts along dimension 0
- new_pool: bfloat16 [256, 16, 2, 1024], P(('req', 'ctx')), parts along dimension 0
There are 2 independent parts, one for each index of `req`. A program takes and returns all parts, laid end to end along the dimension named above; an argument that names none is the same for every part. Nothing has to cross between parts.
Inputs may be any that keep to these rules, and one draw needn't show every extreme that they name: `parents`: row i's parent is a beam of the same request, from 16 * (i // 16) to that plus 16 - 1. `tail_table`: all entries are distinct pool blocks, none among the last 2 blocks of a device's 8. Distinct pool blocks; fresh_slots[i] is one of the last 2 blocks of the device that holds beam row i, that is of device i.
All inputs are finite; a program needn't handle non-finite values.
Results may differ from a plain program's by a relative error of at most 0.0055.
Values may be sent and summed in bfloat16 or wider, within the bound.
No kernel may reach another device: no remote copies, remote signals or barrier semaphores. Data moves between devices by JAX's collectives and lax.ppermute only.
A program may use at most 384 MiB of HBM per device.

v0:
```python
import jax
import jax.numpy as jnp
from jax import lax
from jax.sharding import PartitionSpec as P

HQ = 64
KVH = 8
HD = 128
CAP = 2


masked_score = -1e30


def narrow(values):
    return values.astype(jnp.bfloat16)


def local(
    queries, new_kv, prefix_kv, pool, out_weight, parents, tail_table, fresh_slots, tail_lengths
):
    devices = lax.axis_size("ctx")
    my_index = lax.axis_index("ctx")
    local_rows = queries.shape[0]
    row_total = local_rows * devices
    pool_dev = pool.shape[0]
    block_len = pool.shape[1]
    kv_width = pool.shape[3]
    requests = prefix_kv.shape[0]
    local_len = prefix_kv.shape[1]
    table_depth = tail_table.shape[1]
    capacity = CAP
    groups = HQ // KVH
    beam_count = row_total // requests
    scaling = HD ** (-0.5)
    flat_width = block_len * 2 * kv_width
    parent_len = tail_lengths[parents]
    parent_table = tail_table[parents]
    offset = parent_len % block_len
    source = jnp.take_along_axis(parent_table, (parent_len // block_len)[:, None], axis=1)[:, 0]
    target_dev = fresh_slots // pool_dev
    target_pos = fresh_slots % pool_dev - (pool_dev - capacity)
    position = jnp.arange(block_len, dtype=jnp.int32)
    row_ids = jnp.arange(row_total, dtype=jnp.int32)
    owns_source = source // pool_dev == my_index
    owns_row = row_ids // local_rows == my_index
    picked = pool[jnp.clip(source - my_index * pool_dev, 0, pool_dev - 1)]
    keep_old = owns_source[:, None] & (position[None, :] < offset[:, None])
    kept = jnp.where(keep_old[:, :, None, None], picked, jnp.zeros((), jnp.bfloat16))
    slot_range = jnp.arange(capacity, dtype=jnp.int32)
    bucket = target_dev * capacity + target_pos
    write_new = owns_row[:, None] & (position[None, :] == offset[:, None])
    token_full = lax.dynamic_update_slice_in_dim(
        jnp.zeros((row_total, 2, kv_width), jnp.bfloat16), new_kv, my_index * local_rows, 0
    )
    contrib = jnp.where(write_new[:, :, None, None], token_full[:, None], kept)
    outgoing = jnp.zeros((devices * capacity, flat_width), jnp.bfloat16)
    outgoing = outgoing.at[bucket].set(contrib.reshape(row_total, flat_width))
    filled = jnp.any(
        (target_dev[:, None] == my_index) & (target_pos[:, None] == slot_range[None, :]), axis=0
    )
    incoming = lax.all_to_all(outgoing, "ctx", split_axis=0, concat_axis=0, tiled=True)
    arrived = jnp.sum(incoming.reshape(devices, capacity, flat_width), axis=0, dtype=jnp.float32)
    arrived = arrived.astype(jnp.bfloat16).reshape(capacity, block_len, 2, kv_width)
    previous = pool[pool_dev - capacity :]
    new_pool = jnp.concatenate(
        [pool[: pool_dev - capacity], jnp.where(filled[:, None, None, None], arrived, previous)],
        axis=0,
    )
    everyone = lax.all_gather(queries, "ctx", axis=0, tiled=True)
    query_grid = everyone.reshape(requests, beam_count, KVH, groups, HD)
    pre_keys = prefix_kv[:, :, 0].reshape(requests, local_len, KVH, HD)
    pre_vals = prefix_kv[:, :, 1].reshape(requests, local_len, KVH, HD)
    pre_score = (
        jnp.einsum("rbkgd,rpkd->kgrbp", query_grid, pre_keys, preferred_element_type=jnp.float32)
        * scaling
    )
    pre_score = pre_score.reshape(KVH, groups, row_total, local_len)
    flat_query = everyone.reshape(row_total, KVH, groups, HD)
    pool_keys = pool[:, :, 0].reshape(pool_dev * block_len, KVH, HD)
    pool_vals = pool[:, :, 1].reshape(pool_dev * block_len, KVH, HD)
    tail_score = (
        jnp.einsum("ikgd,tkd->kgit", flat_query, pool_keys, preferred_element_type=jnp.float32)
        * scaling
    )
    slot_ids = my_index * pool_dev + jnp.arange(pool_dev, dtype=jnp.int32)
    matches = parent_table[:, :, None] == slot_ids[None, None, :]
    reach_limit = (
        parent_len[:, None] - jnp.arange(table_depth, dtype=jnp.int32)[None, :] * block_len
    )
    live_mask = jnp.any(
        matches[:, :, :, None] & (position[None, None, None, :] < reach_limit[:, :, None, None]),
        axis=1,
    )
    live_mask = live_mask.reshape(row_total, pool_dev * block_len)
    tail_score = jnp.where(live_mask[None, None], tail_score, masked_score)
    own_query = queries.reshape(local_rows, KVH, groups, HD)
    own_keys = new_kv[:, 0].reshape(local_rows, KVH, HD)
    own_score = (
        jnp.einsum("ikgd,ikd->kgi", own_query, own_keys, preferred_element_type=jnp.float32)
        * scaling
    )
    new_score = lax.dynamic_update_slice_in_dim(
        jnp.full((KVH, groups, row_total), masked_score, jnp.float32),
        own_score,
        my_index * local_rows,
        2,
    )
    value_full = lax.dynamic_update_slice_in_dim(
        jnp.zeros((row_total, kv_width), jnp.bfloat16), new_kv[:, 1], my_index * local_rows, 0
    )
    new_vals = value_full.reshape(row_total, KVH, HD)
    highest = jnp.maximum(jnp.maximum(pre_score.max(-1), tail_score.max(-1)), new_score)
    pre_exp = jnp.exp(pre_score - highest[..., None])
    tail_exp = jnp.exp(tail_score - highest[..., None])
    new_exp = jnp.exp(new_score - highest)
    totals = pre_exp.sum(-1) + tail_exp.sum(-1) + new_exp
    pre_weights = narrow(pre_exp).reshape(KVH, groups, requests, beam_count, local_len)
    pre_out = jnp.einsum(
        "kgrbp,rpkd->kgrbd", pre_weights, pre_vals, preferred_element_type=jnp.float32
    )
    part_out = pre_out.reshape(KVH, groups, row_total, HD)
    part_out = part_out + jnp.einsum(
        "kgit,tkd->kgid", narrow(tail_exp), pool_vals, preferred_element_type=jnp.float32
    )
    part_out = part_out + jnp.einsum(
        "kgi,ikd->kgid", narrow(new_exp), new_vals, preferred_element_type=jnp.float32
    )
    part_max = highest.reshape(HQ, row_total)
    part_sum = totals.reshape(HQ, row_total)
    part_out = part_out.reshape(HQ, row_total, HD)
    own_heads = HQ // devices
    received = (
        lax.all_to_all(part_max[None], "ctx", split_axis=1, concat_axis=0, tiled=True),
        lax.all_to_all(part_sum[None], "ctx", split_axis=1, concat_axis=0, tiled=True),
        lax.all_to_all(part_out[None], "ctx", split_axis=1, concat_axis=0, tiled=True),
    )
    head_max = jnp.max(received[0], axis=0)
    weights = jnp.exp(received[0] - head_max)
    head_sum = jnp.sum(received[1] * weights, axis=0)
    head_out = jnp.sum(received[2] * weights[..., None], axis=0)
    attended = (head_out / head_sum[..., None]).astype(jnp.bfloat16)
    flat_heads = attended.transpose(1, 0, 2).reshape(row_total, own_heads * HD)
    result = lax.psum_scatter(
        jnp.dot(flat_heads, out_weight, preferred_element_type=jnp.float32),
        "ctx",
        scatter_dimension=0,
        tiled=True,
    )
    return (result, new_pool)


def solution(mesh):
    in_specs = (
        P(("req", "ctx"), None),
        P(("req", "ctx"), None, None),
        P("req", "ctx", None, None),
        P(("req", "ctx"), None, None, None),
        P("ctx", None),
        P("req"),
        P("req", None),
        P("req"),
        P("req"),
    )
    out_specs = (P(("req", "ctx"), None), P(("req", "ctx"), None, None, None))
    return jax.shard_map(local, mesh=mesh, in_specs=in_specs, out_specs=out_specs, check_vma=False)
```

profile of v0, /device:TPU:0, one launch (start us, length us, event | category | flops | bytes accessed | tf_op | source)
XLA Modules:
  0.0 284.2 jit_solution(8541146533976965647)
XLA Ops:
  7.2 0.0 copy-start
  7.2 10.1 %fusion.39 = (bf16[1,1024,1,1024]{3,2,1,0:T(2,128)(2,1)}, bf16[1,1024,1,1024]{3,2,1,0:T(2,128)(2,1)}) fusion(bf16[1,1024,2,1024]{3,2,1,0:T(2,128)(2,1)} %param.11), kind=kLoop, calls=%fused_computation.113 | loop fusion | bytes 8388608 | tf_op jit(solution)/shard_map/slice | solution.py:73
  17.3 0.0 copy-start.8
  17.3 0.0 copy-start.1
  17.3 0.0 copy-start.11
  17.3 0.0 copy-start.9
  17.4 9.0 %copy.79 = bf16[1,1024,1,1024]{1,3,2,0:T(8,128)(2,1)S(1)} copy(bf16[1,1024,1,1024]{3,2,1,0:T(2,128)(2,1)} %get-tuple-element.13) | data formatting | bytes 4194304
  26.4 45.3 %all-gather = bf16[16,1,8192]{2,1,0:T(2,128)(2,1)S(1)} all-gather(bf16[1,1,8192]{2,1,0:T(2,128)(2,1)S(1)} %bitcast.144), channel_id=1, replica_groups=mesh['req'=2,'ctx'=16] {'ctx'}, dimensions={0}, use_global_device_ids=true | all-gather | bytes 278528 | tf_op jit(solution)/shard_map/all_gather | solution.py:70
  71.7 0.1 reduce.5
  71.8 1.6 reduce.3
  73.5 0.0 copy-start.4
  73.6 0.1 fusion.27
  73.7 0.1 copy.56
  73.8 2.2 slice_reduce_fusion
  76.0 0.8 copy.83
  76.8 0.0 copy-done
  76.8 0.7 gather_fusion.1
  77.4 0.1 broadcast_subtract_fusion
  77.5 0.1 iota_compare_fusion
  77.6 0.1 copy.53
  77.7 0.6 gather_fusion
  78.3 0.1 broadcast_compare_fusion
  78.4 0.1 and_reduce_fusion
  78.5 0.1 broadcast_in_dim.63
  78.6 2.8 bitcast_reduce_fusion
  81.4 1.4 fusion.40
  82.8 0.1 dynamic_update_slice.11
  82.9 0.6 convert_bitcast_fusion.1
  83.5 3.1 %fusion.1 = f32[8,8,16]{2,1,0:T(8,128)S(1)} fusion(f32[8,1024,16,8]{1,2,3,0:T(8,128)} %get-tuple-element.17, f32[8,8,16]{2,1,0:T(8,128)} %get-tuple-element.9), kind=kLoop, calls=%fused_computation.7 | loop fusion | flops 3144704 | bytes 4202496 | tf_op jit(solution)/shard_map/reduce_sum | solution.py:117
  86.6 1.2 fusion.14
  87.8 1.4 add_add_fusion
  89.2 3.5 %all-to-all-start.2 = ((f32[1,64,16]{2,0,1:T(1,128)}), f32[1,64,16]{2,0,1:T(1,128)S(1)}, u32[]{:S(2)}, u32[]{:S(2)}) async-start(f32[1,64,16]{2,0,1:T(1,128)} %bitcast.27), calls=%async_computation.2 | async-start | bytes 65536 | tf_op jit(solution)/shard_map/all_to_all | solution.py:135
  92.7 9.0 %copy.80 = bf16[1,1024,1,1024]{1,3,2,0:T(8,128)(2,1)S(1)} copy(bf16[1,1024,1,1024]{3,2,1,0:T(2,128)(2,1)} %get-tuple-element.12) | data formatting | bytes 4194304
  101.7 4.0 %fusion.5 = f32[8,8,16,128]{3,2,1,0:T(8,128)} fusion(bf16[1024,8,128,1]{0,2,3,1:T(8,128)(2,1)S(1)} %bitcast.131, f32[8,1024,16,8]{1,2,3,0:T(8,128)} %get-tuple-element.17, f32[8,8,16]{2,1,0:T(8,128)} %get-tuple-element.9), kind=kOutput, calls=%fused_computation.13 | convolution fusion | flops 271581184 | bytes 6819840 | tf_op jit(solution)/shard_map/kgrbp,rpkd->kgrbd/dot_general | solution.py:119
  105.8 0.1 dynamic_update_slice.12
  106.0 0.7 gather_fusion.3
  106.7 2.2 fusion.9
  108.9 0.1 fusion.31
  109.0 0.0 all-to-all-done.2
  109.0 6.9 %all-to-all-start.1 = ((f32[1,64,16]{2,0,1:T(1,128)}), f32[1,64,16]{2,0,1:T(1,128)S(1)}, u32[]{:S(2)}, u32[]{:S(2)}) async-start(f32[1,64,16]{2,0,1:T(1,128)} %bitcast.23), calls=%async_computation.1 | async-start | bytes 65536 | tf_op jit(solution)/shard_map/all_to_all | solution.py:134
  115.9 7.4 %all-to-all-done.1 = f32[1,64,16]{2,0,1:T(1,128)S(1)} async-done(((f32[1,64,16]{2,0,1:T(1,128)}), f32[1,64,16]{2,0,1:T(1,128)S(1)}, u32[]{:S(2)}, u32[]{:S(2)}) %all-to-all-start.1) | async-done | bytes 4128 | tf_op jit(solution)/shard_map/all_to_all | solution.py:134
  123.3 3.8 %all-to-all-start = ((f32[1,64,16,128]{3,2,0,1:T(8,128)}), f32[1,64,16,128]{3,2,0,1:T(8,128)S(1)}, u32[]{:S(2)}, u32[]{:S(2)}) async-start(f32[1,64,16,128]{3,2,0,1:T(8,128)} %bitcast.21), calls=%async_computation | async-start | bytes 1048576 | tf_op jit(solution)/shard_map/all_to_all | solution.py:136
  127.1 2.7 gather_fusion.2
  129.8 1.4 broadcast_select_fusion.1
  131.2 1.6 reshape.462
  132.9 3.4 %scatter_custom_fusion = bf16[32,32768]{1,0:T(8,128)(2,1)S(1)} fusion(s32[16]{0:T(128)S(1)} %get-tuple-element.6, bf16[16,32768]{1,0:T(8,128)(2,1)} %reshape.462, bf16[]{:T(256)} %constant.103.clone.1), kind=kCustom, calls=%fused_computation.23 | custom fusion | bytes 2097664 | tf_op jit(solution)/shard_map/scatter | solution.py:58
  136.2 2.7 all_to_all.39
  138.9 0.0 all-to-all-done
  138.9 6.8 %all-to-all-start.3 = ((bf16[16,2,32768]{2,1,0:T(2,128)(2,1)}), bf16[16,2,32768]{2,1,0:T(2,128)(2,1)S(1)}, u32[]{:S(2)}, u32[]{:S(2)}) async-start(bf16[16,2,32768]{2,1,0:T(2,128)(2,1)} %all_to_all.39), calls=%async_computation.3 | async-start | bytes 4194304 | tf_op jit(solution)/shard_map/all_to_all | solution.py:62
  145.8 0.0 all-reduce.3.cloned.1.call-start
  145.8 0.0 copy-done.7
  145.9 0.2 multiply_reduce_fusion
  146.1 0.0 copy-start.12
  146.1 5.4 %fusion.24 = f32[16,8192]{1,0:T(8,128)} fusion(bf16[512,8192]{1,0:T(8,128)(2,1)} %param.13, f32[16,4]{0,1:T(4,128)S(1)} %bitcast.146, f32[4,16,128]{2,1,0:T(8,128)S(1)} %multiply_reduce_fusion), kind=kOutput, calls=%fused_computation.50 | convolution fusion | flops 134234112 | bytes 8945920 | tf_op jit(solution)/shard_map/dot_general | solution.py:145
  151.5 0.0 all-reduce.3.cloned.1.call-update
  151.6 0.6 dynamic-slice
  152.2 0.1 and_reduce_fusion.1
  152.3 118.8 %all-reduce.3.cloned.1.call-done = f32[16,8192]{1,0:T(8,128)} async-done(((f32[16,8192]{1,0:T(8,128)}), f32[16,8192]{1,0:T(8,128)}) %all-reduce.3.cloned.1.call-update) | async-done | bytes 524304
  271.1 2.2 constant_dynamic-slice_fusion
  273.3 0.0 all-to-all-done.3
  273.3 2.2 reduce_sum.55
  275.5 0.1 reshape.424
  275.6 0.3 broadcast_select_fusion.2
  275.8 1.5 pad_maximum_fusion
  (46 shorter events, 0.4 us)
Async XLA Ops:
  7.2 69.6 %copy-start = (s32[16]{0:T(128)S(1)}, s32[16]{0:T(128)}, u32[]{:S(2)}) copy-start(s32[16]{0:T(128)} %param.17) | copy-start | bytes 196
  17.3 9.1 %copy-start.5 = (bf16[1,8192]{1,0:T(2,128)(2,1)S(1)}, bf16[1,8192]{1,0:T(2,128)(2,1)}, u32[]{:S(2)}) copy-start(bf16[1,8192]{1,0:T(2,128)(2,1)} %param.9) | copy-start | bytes 49156
  17.3 56.2 %copy-start.8 = (bf16[1,2,1024]{2,1,0:T(2,128)(2,1)S(1)}, bf16[1,2,1024]{2,1,0:T(2,128)(2,1)}, u32[]{:S(2)}) copy-start(bf16[1,2,1024]{2,1,0:T(2,128)(2,1)} %param.10) | copy-start | bytes 12292
  17.3 56.5 %copy-start.1 = (bf16[8,16,2,1024]{3,2,1,0:T(2,128)(2,1)S(1)}, bf16[8,16,2,1024]{3,2,1,0:T(2,128)(2,1)}, u32[]{:S(2)}) copy-start(bf16[8,16,2,1024]{3,2,1,0:T(2,128)(2,1)} %param.12) | copy-start | bytes 1572868
  17.3 59.4 %copy-start.11 = (s32[16]{0:T(128)S(1)}, s32[16]{0:T(128)}, u32[]{:S(2)}) copy-start(s32[16]{0:T(128)} %param.14) | copy-start | bytes 196
  17.3 60.3 %copy-start.9 = (s32[16,4]{0,1:T(4,128)S(1)}, s32[16,4]{0,1:T(4,128)}, u32[]{:S(2)}) copy-start(s32[16,4]{0,1:T(4,128)} %param.15) | copy-start | bytes 772
  73.5 7.8 %copy-start.4 = (bf16[2,8,64,128]{3,2,1,0:T(8,128)(2,1)}, bf16[2,8,64,128]{3,2,1,0:T(8,128)(2,1)S(1)}, u32[]{:S(2)}) copy-start(bf16[2,8,64,128]{3,2,1,0:T(8,128)(2,1)S(1)} %copy.82) | copy-start | bytes 786436
  89.2 19.8 %all-to-all-start.2 = ((f32[1,64,16]{2,0,1:T(1,128)}), f32[1,64,16]{2,0,1:T(1,128)S(1)}, u32[]{:S(2)}, u32[]{:S(2)}) async-start(f32[1,64,16]{2,0,1:T(1,128)} %bitcast.27), calls=%async_computation.2 | async-start | bytes 65536 | tf_op jit(solution)/shard_map/all_to_all | solution.py:135
  108.9 24.0 %copy-start.10 = (s32[16]{0:T(128)S(1)}, s32[16]{0:T(128)}, u32[]{:S(2)}) copy-start(s32[16]{0:T(128)} %param.16) | copy-start | bytes 196
  109.0 14.3 %copy-start.6 = (f32[1,64,16]{2,0,1:T(1,128)}, f32[1,64,16]{2,0,1:T(1,128)S(1)}, u32[]{:S(2)}) copy-start(f32[1,64,16]{2,0,1:T(1,128)S(1)} %all-to-all-done.2) | copy-start | bytes 12292
  109.0 14.3 %all-to-all-start.1 = ((f32[1,64,16]{2,0,1:T(1,128)}), f32[1,64,16]{2,0,1:T(1,128)S(1)}, u32[]{:S(2)}, u32[]{:S(2)}) async-start(f32[1,64,16]{2,0,1:T(1,128)} %bitcast.23), calls=%async_computation.1 | async-start | bytes 65536 | tf_op jit(solution)/shard_map/all_to_all | solution.py:134
  123.3 3.8 %copy-start.2 = (f32[1,64,16]{2,0,1:T(1,128)}, f32[1,64,16]{2,0,1:T(1,128)S(1)}, u32[]{:S(2)}) copy-start(f32[1,64,16]{2,0,1:T(1,128)S(1)} %all-to-all-done.1) | copy-start | bytes 12292
  123.3 15.6 %all-to-all-start = ((f32[1,64,16,128]{3,2,0,1:T(8,128)}), f32[1,64,16,128]{3,2,0,1:T(8,128)S(1)}, u32[]{:S(2)}, u32[]{:S(2)}) async-start(f32[1,64,16,128]{3,2,0,1:T(8,128)} %bitcast.21), calls=%async_computation | async-start | bytes 1048576 | tf_op jit(solution)/shard_map/all_to_all | solution.py:136
  138.9 6.9 %copy-start.3 = (f32[1,64,16]{2,0,1:T(1,128)S(1)}, f32[1,64,16]{2,0,1:T(1,128)}, u32[]{:S(2)}) copy-start(f32[1,64,16]{2,0,1:T(1,128)} %copy-done.2) | copy-start | bytes 12292
  138.9 6.9 %copy-start.7 = (f32[1,64,16]{2,0,1:T(1,128)S(1)}, f32[1,64,16]{2,0,1:T(1,128)}, u32[]{:S(2)}) copy-start(f32[1,64,16]{2,0,1:T(1,128)} %copy-done.6) | copy-start | bytes 12292
  138.9 134.4 %all-to-all-start.3 = ((bf16[16,2,32768]{2,1,0:T(2,128)(2,1)}), bf16[16,2,32768]{2,1,0:T(2,128)(2,1)S(1)}, u32[]{:S(2)}, u32[]{:S(2)}) async-start(bf16[16,2,32768]{2,1,0:T(2,128)(2,1)} %all_to_all.39), calls=%async_computation.3 | async-start | bytes 4194304 | tf_op jit(solution)/shard_map/all_to_all | solution.py:62
  145.8 125.3 %all-reduce.3.cloned.1.call-start = ((), (), s32[]{:S(2)}) async-start(), calls=%async_computation.4 | async-start | bytes 1048576
  146.1 5.5 %copy-start.12 = (u32[32]{0:T(128)S(1)}, u32[32]{0:T(128)}, u32[]{:S(2)}) copy-start(u32[32]{0:T(128)} %constant.134) | copy-start | bytes 388
  151.5 124.3 %slice-start = ((bf16[8,16,2,1024]{3,2,1,0:T(2,128)(2,1)}), bf16[6,16,2,1024]{3,2,1,0:T(2,128)(2,1)S(1)}, s32[]{:S(2)}) async-start(bf16[8,16,2,1024]{3,2,1,0:T(2,128)(2,1)} %param.12), calls=%async_computation.5 | async-start | bytes 786432 | tf_op jit(solution)/shard_map/slice | solution.py:67
Sparse Core Ops, SparseCore 0:
  152.3 118.7 all-reduce.2
where the time goes:
time: 285 us; the launch traced here: 284 us
  waiting for transfers between devices  126 us (44%)
  local copies, waits for them, and re-layouts  46.9 us (16%)
  blocking collectives  45.3 us (16%)
  starting transfers between devices  21 us (7%)
  matrix products  16 us (6%)
  between operations  14.5 us (5%)
  other arithmetic  14.3 us (5%)
    unnamed x2, waiting for transfers between devices  119 us
    all_gather x1, blocking collectives, local(): everyone = lax.all_gather(queries, 'ctx', axis=0, tiled=True)  45.3 us
    unnamed x36, local copies, waits for them, and re-layouts  21.8 us
    slice x1, local copies, waits for them, and re-layouts, local(): pre_vals = prefix_kv[:, :, 1].reshape(requests, local_len, KVH, HD)  10.1 us
    all_to_all x1, waiting for transfers between devices, local(): lax.all_to_all(part_max[None], 'ctx', split_axis=1, concat_axis=0, tiled=...  7.39 us
    all_to_all x1, starting transfers between devices, local(): lax.all_to_all(part_max[None], 'ctx', split_axis=1, concat_axis=0, tiled=...  6.89 us
    all_to_all x1, starting transfers between devices, local(): lax.all_to_all(outgoing, 'ctx', split_axis=0, concat_axis=0, tiled=True)  6.83 us
  transfers between devices with their start and end apart: 5, of which 2 were waited for; matrix products, arithmetic and copies ran while one was open for 12% of the time, Pallas kernels for 0%

commit v1 on v0

v1 whole, which is shorter than its diff:
```python
import functools
import math

import jax
import jax.numpy as jnp
from jax import lax
from jax.experimental import pallas as pl
from jax.experimental.pallas import tpu as pltpu
from jax.sharding import PartitionSpec as P

HQ = 64
KVH = 8
HD = 128
CAP = 2

STAT_ROWS = 16
VMEM_LIMIT = 48 << 20
masked_score = -1e30
bf16 = jnp.bfloat16
f32 = jnp.float32


def split_kv(source, head, scratch, keys, values):
    tokens = source.shape[0]
    pairs = source[:, :, head * HD : (head + 1) * HD].astype(f32)
    scratch[: 2 * tokens, :] = pairs.reshape(2 * tokens, HD)
    keys[...] = scratch[pl.ds(0, tokens, stride=2), :].astype(bf16)
    values[...] = scratch[pl.ds(1, tokens, stride=2), :].astype(bf16)


def unpack_kernel(prefix, pool, new_kv, keys, values, tail_keys, tail_values, scratch):
    for head in range(KVH):
        split_kv(prefix.at[0], head, scratch.at[head], keys.at[0, head], values.at[0, head])

    @pl.when((pl.program_id(0) == 0) & (pl.program_id(1) == 0))
    def _():
        blocks, block_len = pool.shape[:2]
        tokens = blocks * block_len
        for head in range(KVH):
            for block in range(blocks):
                at = pl.ds(block * block_len, block_len)
                split_kv(
                    pool.at[block],
                    head,
                    scratch.at[head],
                    tail_keys.at[head, at],
                    tail_values.at[head, at],
                )
            rows = new_kv.shape[0]
            first = tokens - CAP * block_len
            at = pl.ds(first, CAP * block_len)
            lanes = slice(head * HD, (head + 1) * HD)
            slot = lax.broadcasted_iota(jnp.int32, (CAP * block_len, HD), 0)
            key = tail_keys[head, at, :]
            value = tail_values[head, at, :]
            for row in range(rows):
                key = jnp.where(slot == row, new_kv[row, 0:1, lanes], key)
                value = jnp.where(slot == row, new_kv[row, 1:2, lanes], value)
            tail_keys[head, at, :] = key
            tail_values[head, at, :] = value


def unpack(prefix_kv, pool, new_kv):
    requests, length, _, width = prefix_kv.shape
    blocks, block_len = pool.shape[:2]
    tokens = blocks * block_len
    step = min(256, length)
    whole = lambda shape: pl.BlockSpec(shape, lambda r, i: (0,) * len(shape))
    return pl.pallas_call(
        unpack_kernel,
        name="unpack",
        grid=(requests, length // step),
        in_specs=[
            pl.BlockSpec((1, step, 2, width), lambda r, i: (r, i, 0, 0)),
            whole(pool.shape),
            whole(new_kv.shape),
        ],
        out_specs=[pl.BlockSpec((1, KVH, step, HD), lambda r, i: (r, 0, i, 0))] * 2
        + [whole((KVH, tokens, HD))] * 2,
        out_shape=[jax.ShapeDtypeStruct((requests, KVH, length, HD), bf16)] * 2
        + [jax.ShapeDtypeStruct((KVH, tokens, HD), bf16)] * 2,
        scratch_shapes=[pltpu.VMEM((KVH, 2 * step, HD), f32)],
        compiler_params=pltpu.CompilerParams(vmem_limit_bytes=VMEM_LIMIT),
        cost_estimate=pl.CostEstimate(
            flops=0, bytes_accessed=4 * prefix_kv.size, transcendentals=0
        ),
    )(prefix_kv, pool, new_kv)


def pieces(value):
    high = value.astype(bf16)
    rest = value - high.astype(f32)
    middle = rest.astype(bf16)
    low = (rest - middle.astype(f32)).astype(bf16)
    return high.astype(f32), middle.astype(f32), low.astype(f32)


def attend_kernel(query, keys, values, tail_keys, tail_values, bias, out):
    groups = HQ // KVH
    targets = out.shape[0]
    beams = query.shape[0]
    count = groups * beams
    share = count // targets
    factor = HD ** (-0.5) * math.log2(math.e)
    stacked = jnp.concatenate([query[:, j * HD : (j + 1) * HD] for j in range(groups)], axis=0)
    contract = (((1,), (1,)), ((), ()))
    score = lax.dot_general(stacked, keys[0, 0], contract, preferred_element_type=f32)
    tail = lax.dot_general(stacked, tail_keys[0], contract, preferred_element_type=f32)
    tail = tail + jnp.concatenate([bias[0]] * groups, axis=0)
    top = jnp.maximum(
        jnp.max(score, axis=1, keepdims=True), jnp.max(tail, axis=1, keepdims=True)
    )
    weight = jnp.exp2((score - top) * factor)
    tail_weight = jnp.exp2((tail - top) * factor)
    total = jnp.sum(weight, axis=1, keepdims=True) + jnp.sum(tail_weight, axis=1, keepdims=True)
    result = jnp.dot(weight.astype(bf16), values[0, 0], preferred_element_type=f32)
    result = result + jnp.dot(
        tail_weight.astype(bf16), tail_values[0], preferred_element_type=f32
    )
    lane = lax.broadcasted_iota(jnp.int32, (count, HD), 1)
    packed = jnp.zeros((count, HD), f32)
    for at, term in enumerate(pieces(top) + pieces(total)):
        packed = jnp.where(lane == at, term, packed)
    stats = jnp.concatenate(
        [packed[t * share : (t + 1) * share] for t in range(targets)]
        + [jnp.zeros((HD - count, HD), f32)] * (count < HD),
        axis=0,
    )
    stats = stats.T
    for t in range(targets):
        out[t, 0, :share, :] = result[t * share : (t + 1) * share].astype(bf16)
        mine = stats if t == 0 else pltpu.roll(stats, HD - t * share, 1)
        out[t, 0, share : share + STAT_ROWS, :] = mine[:STAT_ROWS].astype(bf16)


def attend(everyone, keys, values, tail_keys, tail_values, bias, devices):
    requests, _, length, _ = keys.shape
    tokens = tail_keys.shape[1]
    beams = everyone.shape[0] // requests
    groups = HQ // KVH
    targets = devices // KVH
    rows = groups // targets * beams + STAT_ROWS
    return pl.pallas_call(
        attend_kernel,
        name="attend",
        grid=(requests, KVH),
        in_specs=[
            pl.BlockSpec((beams, groups * HD), lambda r, g: (r, g)),
            pl.BlockSpec((1, 1, length, HD), lambda r, g: (r, g, 0, 0)),
            pl.BlockSpec((1, 1, length, HD), lambda r, g: (r, g, 0, 0)),
            pl.BlockSpec((1, tokens, HD), lambda r, g: (g, 0, 0)),
            pl.BlockSpec((1, tokens, HD), lambda r, g: (g, 0, 0)),
            pl.BlockSpec((1, beams, tokens), lambda r, g: (r, 0, 0)),
        ],
        out_specs=pl.BlockSpec((targets, 1, rows, HD), lambda r, g: (g, r, 0, 0)),
        out_shape=jax.ShapeDtypeStruct((devices, requests, rows, HD), bf16),
        compiler_params=pltpu.CompilerParams(vmem_limit_bytes=VMEM_LIMIT),
        cost_estimate=pl.CostEstimate(
            flops=4 * everyone.size * length,
            bytes_accessed=4 * keys.size,
            transcendentals=everyone.size * length // HD,
        ),
    )(everyone, keys, values, tail_keys, tail_values, bias)


def project_kernel(partial, weight, out, attended, scratch):
    devices, requests, rows, _ = partial.shape
    share = rows - STAT_ROWS
    beams = out.shape[0] // requests
    own = share // beams
    factor = HD ** (-0.5) * math.log2(math.e)

    @pl.when(pl.program_id(0) == 0)
    def _():
        for r in range(requests):
            stats = [partial[p, r, share:rows, :].astype(f32) for p in range(devices)]
            tops = jnp.concatenate([s[0:1] + s[1:2] + s[2:3] for s in stats], axis=0)
            sums = jnp.concatenate([s[3:4] + s[4:5] + s[5:6] for s in stats], axis=0)
            scale = jnp.exp2((tops - jnp.max(tops, axis=0, keepdims=True)) * factor)
            scale = scale / jnp.sum(scale * sums, axis=0, keepdims=True)
            if devices < HD:
                scale = jnp.concatenate([scale, jnp.zeros((HD - devices, HD), f32)], axis=0)
            scale = scale.T
            total = jnp.zeros((share, HD), f32)
            for p in range(devices):
                total = total + partial[p, r, :share, :].astype(f32) * scale[:share, p : p + 1]
            for h in range(own):
                attended[r * beams : (r + 1) * beams, h * HD : (h + 1) * HD] = total[
                    h * beams : (h + 1) * beams
                ].astype(bf16)

    product = jnp.dot(attended[...], weight[...], preferred_element_type=f32)
    row_total = out.shape[0]
    chunks = weight.shape[1] // HD
    for c in range(chunks):
        scratch[pl.ds(c, row_total, stride=chunks), :] = product[:, c * HD : (c + 1) * HD]
    for row in range(row_total):
        out[row] = scratch[row * chunks : (row + 1) * chunks, :].astype(bf16)


def project(partial, weight, row_total):
    devices, requests, rows, _ = partial.shape
    depth, width = weight.shape
    step = min(2048, width)
    chunks = step // HD
    return pl.pallas_call(
        project_kernel,
        name="project",
        grid=(width // step,),
        in_specs=[
            pl.BlockSpec(partial.shape, lambda n: (0, 0, 0, 0)),
            pl.BlockSpec((depth, step), lambda n: (0, n)),
        ],
        out_specs=pl.BlockSpec((row_total, chunks, HD), lambda n: (0, n, 0)),
        out_shape=jax.ShapeDtypeStruct((row_total, width // HD, HD), bf16),
        scratch_shapes=[
            pltpu.VMEM((row_total, depth), bf16),
            pltpu.VMEM((row_total * chunks, HD), f32),
        ],
        compiler_params=pltpu.CompilerParams(vmem_limit_bytes=VMEM_LIMIT),
        cost_estimate=pl.CostEstimate(
            flops=2 * row_total * depth * width, bytes_accessed=2 * weight.size, transcendentals=0
        ),
    )(partial, weight)


def exchange(array):
    return lax.all_to_all(array, "ctx", split_axis=0, concat_axis=0, tiled=True)


def local(
    queries, new_kv, prefix_kv, pool, out_weight, parents, tail_table, fresh_slots, tail_lengths
):
    devices = lax.axis_size("ctx")
    my_index = lax.axis_index("ctx")
    local_rows = queries.shape[0]
    row_total = local_rows * devices
    pool_dev, block_len, _, kv_width = pool.shape
    requests = prefix_kv.shape[0]
    table_depth = tail_table.shape[1]
    beams = row_total // requests
    old_dev = pool_dev - CAP
    tokens = pool_dev * block_len

    width = queries.shape[1]
    outgoing = jnp.broadcast_to(queries[None], (devices, local_rows, width))
    everyone = exchange(outgoing).reshape(row_total, width)

    token_parts = min(devices, block_len)
    width_parts = devices // token_parts
    piece = (block_len // token_parts, 2, kv_width // width_parts)
    spread = pool[:old_dev].reshape(
        old_dev, token_parts, piece[0], 2, width_parts, piece[2]
    ).transpose(1, 4, 0, 2, 3, 5)
    spread = exchange(spread.reshape((devices, old_dev) + piece))

    keys, values, tail_keys, tail_values = unpack(prefix_kv, pool, new_kv)

    parent_len = tail_lengths[parents]
    parent_table = tail_table[parents]
    offset = parent_len % block_len
    source = jnp.take_along_axis(parent_table, (parent_len // block_len)[:, None], axis=1)[:, 0]
    slot = lax.broadcasted_iota(jnp.int32, (1, 1, pool_dev), 2) + my_index * pool_dev
    depth = lax.broadcasted_iota(jnp.int32, (1, table_depth, 1), 1)
    matches = parent_table[:, :, None] == slot
    reach = jnp.sum(
        jnp.where(matches, parent_len[:, None, None] - depth * block_len, 0), axis=1
    )
    position = jnp.arange(tokens, dtype=jnp.int32)
    live = position[None, :] % block_len < jnp.repeat(reach, block_len, axis=1)
    row_ids = jnp.arange(row_total, dtype=jnp.int32)
    own_slot = row_ids - my_index * local_rows
    own = (own_slot >= 0) & (own_slot < local_rows)
    live = live | (own[:, None] & (position[None, :] == old_dev * block_len + own_slot[:, None]))
    bias = jnp.where(live, 0.0, masked_score).astype(f32).reshape(requests, beams, tokens)

    partial = attend(everyone, keys, values, tail_keys, tail_values, bias, devices)
    partial = exchange(partial)

    picked = spread.reshape((devices * old_dev,) + piece)[
        source // pool_dev * old_dev + source % pool_dev
    ]
    block = exchange(picked.reshape((devices, local_rows) + piece))

    products = exchange(project(partial, out_weight, row_total).reshape(
        devices, local_rows * (out_weight.shape[1] // HD), HD
    ))
    result = jnp.sum(products.astype(f32), axis=0).reshape(local_rows, out_weight.shape[1])

    block = block.reshape((token_parts, width_parts, local_rows) + piece)
    block = block.transpose(2, 0, 3, 4, 1, 5).reshape(local_rows, block_len, 2, kv_width)
    own_offset = lax.dynamic_slice_in_dim(offset, my_index * local_rows, local_rows)
    own_fresh = lax.dynamic_slice_in_dim(fresh_slots, my_index * local_rows, local_rows)
    at = jnp.arange(block_len, dtype=jnp.int32)[None, :, None, None]
    limit = own_offset[:, None, None, None]
    copied = jnp.where(
        at < limit, block, jnp.where(at == limit, new_kv[:, None], jnp.zeros((), bf16))
    )
    new_pool = pool
    for row in range(local_rows):
        new_pool = lax.dynamic_update_slice_in_dim(
            new_pool, copied[row : row + 1], own_fresh[row] - my_index * pool_dev, 0
        )
    return (result, new_pool)


def solution(mesh):
    in_specs = (
        P(("req", "ctx"), None),
        P(("req", "ctx"), None, None),
        P("req", "ctx", None, None),
        P(("req", "ctx"), None, None, None),
        P("ctx", None),
        P("req"),
        P("req", None),
        P("req"),
        P("req"),
    )
    out_specs = (P(("req", "ctx"), None), P(("req", "ctx"), None, None, None))
    return jax.shard_map(local, mesh=mesh, in_specs=in_specs, out_specs=out_specs, check_vma=False)
```

time: 285 us -> 91 us (0.32)
  waiting for transfers between devices: 126 us -> 19.7 us
  blocking collectives: 45.3 us -> 0 us
  local copies, waits for them, and re-layouts: 46.9 us -> 15.6 us
  Pallas kernels: 0 us -> 18.1 us
  matrix products: 16 us -> 0 us
  between operations: 14.5 us -> 1.49 us
  other arithmetic: 14.3 us -> 5.57 us
  starting transfers between devices: 21 us -> 29.6 us
    unnamed x2 -> x0, waiting for transfers between devices: 119 us -> none
    all_gather x1 -> x0, blocking collectives: 45.3 us -> none  [local(): everyone = lax.all_gather(queries, 'ctx', axis=0, tiled=True)]
    pallas_call x0 -> x3, Pallas kernels: none -> 18.1 us  [the longest x1 6.6 us: unpack(): pl.pallas_call(unpack_kernel, name='unpack', grid=(requests, length // st...]
    dot_general x6 -> x0, matrix products: 16 us -> none  [the longest x1 5.43 us: local(): jnp.dot(flat_heads, out_weight, preferred_element_type=jnp.float32)]
    unnamed x36 -> x18, local copies, waits for them, and re-layouts: 21.8 us -> 7.96 us
    all_to_all x4 -> x5, waiting for transfers between devices: 7.4 us -> 19.7 us  [exchange(): return lax.all_to_all(array, 'ctx', split_axis=0, concat_axis=0, tiled=True)]
    slice x4 -> x0, local copies, waits for them, and re-layouts: 12.3 us -> none  [the longest x1 10.1 us: local(): pre_vals = prefix_kv[:, :, 1].reshape(requests, local_len, KVH, HD)]
    all_to_all x4 -> x5, starting transfers between devices: 21 us -> 29.6 us  [exchange(): return lax.all_to_all(array, 'ctx', split_axis=0, concat_axis=0, tiled=True)]
  transfers between devices with their start and end apart: 5 -> 5, of which waited for: 2 -> 4; matrix products, arithmetic and copies ran while one was open for 12% -> 13% of each run, Pallas kernels for 0% -> 20%
where the time goes in v1:
time: 91 us; the launch traced here: 90 us
  starting transfers between devices  29.6 us (33%)
  waiting for transfers between devices  19.7 us (22%)
  Pallas kernels  18.1 us (20%)
  local copies, waits for them, and re-layouts  15.6 us (17%)
  other arithmetic  5.57 us (6%)
  between operations  1.49 us (2%)
    all_to_all x5, starting transfers between devices, exchange(): return lax.all_to_all(array, 'ctx', split_axis=0, concat_axis=0, tiled=True)  29.6 us
    all_to_all x5, waiting for transfers between devices, exchange(): return lax.all_to_all(array, 'ctx', split_axis=0, concat_axis=0, tiled=True)  19.7 us
    unnamed x18, local copies, waits for them, and re-layouts  7.96 us
    pallas_call x1, Pallas kernels, unpack(): pl.pallas_call(unpack_kernel, name='unpack', grid=(requests, length // st...  6.6 us
    pallas_call x1, Pallas kernels, project(): pl.pallas_call(project_kernel, name='project', grid=(width // step,), in_...  5.85 us
    pallas_call x1, Pallas kernels, attend(): pl.pallas_call(attend_kernel, name='attend', grid=(requests, KVH), in_spe...  5.67 us
    gather x1, local copies, waits for them, and re-layouts, local(): spread.reshape((devices * old_dev,) + piece)  2.3 us
    broadcast_in_dim x1, other arithmetic, local(): outgoing = jnp.broadcast_to(queries[None], (devices, local_rows, width))  2.25 us
  transfers between devices with their start and end apart: 5, of which 4 were waited for; matrix products, arithmetic and copies ran while one was open for 13% of the time, Pallas kernels for 20%

profile of v1, /device:TPU:0, one launch (start us, length us, event | category | flops | bytes accessed | tf_op | source)
XLA Modules:
  0.0 90.0 jit_solution(1055166580123531706)
XLA Ops:
  0.6 0.0 copy-start
  0.6 0.0 copy-start.4
  0.7 1.1 %copy.32.pool = bf16[8,16,2,1024]{3,2,1,0:T(2,128)(2,1)S(1)} copy(bf16[8,16,2,1024]{3,2,1,0:T(2,128)(2,1)} %param.12) | data formatting | bytes 1048576
  1.7 0.8 reduce
  2.6 0.4 broadcast_in_dim.77
  3.0 0.5 broadcast.655
  3.5 2.3 %reduce.1 = bf16[16,8192]{1,0:T(8,128)(2,1)S(1)} reduce(bf16[16,1,8192]{2,1,0:T(2,128)(2,1)S(1)} %broadcast_in_dim.77, bf16[]{:T(256)} %broadcast.655), dimensions={1}, to_apply=%broadcast_in_dim.77.reduce_sub_computation | reduce | bytes 524290 | tf_op jit(solution)/shard_map/broadcast_in_dim | solution.py:246
  5.7 0.9 reshape.497
  6.6 8.3 %all-to-all-start = ((bf16[16,2,4096]{2,1,0:T(2,128)(2,1)}), bf16[16,2,4096]{2,1,0:T(2,128)(2,1)S(1)}, u32[]{:S(2)}, u32[]{:S(2)}) async-start(bf16[16,2,4096]{2,1,0:T(2,128)(2,1)} %reshape.497), calls=%async_computation | async-start | bytes 524288 | tf_op jit(solution)/shard_map/all_to_all | solution.py:228
  15.0 0.7 compare_select_fusion.3
  15.7 0.0 copy-done
  15.7 0.7 gather_fusion.1
  16.3 0.1 broadcast_subtract_fusion
  16.4 0.8 copy.20
  17.2 0.6 gather_fusion
  17.7 0.1 copy.21
  17.8 0.1 select_reduce_fusion
  17.9 1.0 %copy_bitcast_fusion = bf16[16,6,1,2,1024]{4,3,1,2,0:T(2,128)(2,1)} fusion(bf16[8,16,2,1024]{3,2,1,0:T(2,128)(2,1)S(1)} %copy.32.pool), kind=kLoop, calls=%fused_computation.5 | loop fusion | bytes 786432 | tf_op jit(solution)/shard_map/reshape | solution.py:255
  18.9 5.9 %all-to-all-done = bf16[16,2,4096]{2,1,0:T(2,128)(2,1)S(1)} async-done(((bf16[16,2,4096]{2,1,0:T(2,128)(2,1)}), bf16[16,2,4096]{2,1,0:T(2,128)(2,1)S(1)}, u32[]{:S(2)}, u32[]{:S(2)}) %all-to-all-start) | async-done | bytes 262176 | tf_op jit(solution)/shard_map/all_to_all | solution.py:228
  24.8 4.2 %all-to-all-start.3 = ((bf16[16,6,1,2,1024]{4,3,1,2,0:T(2,128)(2,1)}), bf16[16,6,1,2,1024]{4,3,1,2,0:T(2,128)(2,1)}, u32[]{:S(2)}, u32[]{:S(2)}) async-start(bf16[16,6,1,2,1024]{4,3,1,2,0:T(2,128)(2,1)} %copy_bitcast_fusion), calls=%async_computation.3 | async-start | bytes 786432 | tf_op jit(solution)/shard_map/all_to_all | solution.py:228
  29.1 0.1 copy.22
  29.1 0.1 broadcast_in_dim.81
  29.2 0.1 reshape.452
  29.3 0.0 copy-done.4
  29.3 6.6 %unpack.1 = (bf16[1,8,1024,128]{3,2,1,0:T(8,128)(2,1)S(1)}, bf16[1,8,1024,128]{3,2,1,0:T(8,128)(2,1)S(1)}, bf16[8,128,128]{2,1,0:T(8,128)(2,1)S(1)}, bf16[8,128,128]{2,1,0:T(8,128)(2,1)S(1)}) custom-call(bf16[1,1024,2,1024]{3,2,1,0:T(2,128)(2,1)} %prefix.1, bf16[8,16,2,1024]{3,2,1,0:T(2,128)(2,1)S(1)} %copy.32.pool, bf16[1,2,1024]{2,1,0:T(2,128)(2,1)S(1)} %copy-done.4), custom_call_target="tpu_custom_call" | custom-call | bytes 8388608 | tf_op jit(solution)/shard_map/unpack/pallas_call | solution.py:69
  35.9 0.0 copy-start.2
  35.9 1.3 %copy-done.2 = bf16[1,8,1024,128]{3,2,1,0:T(8,128)(2,1)} copy-done((bf16[1,8,1024,128]{3,2,1,0:T(8,128)(2,1)}, bf16[1,8,1024,128]{3,2,1,0:T(8,128)(2,1)S(1)}, u32[]{:S(2)}) %copy-start.2) | copy-done | bytes 2097176
  37.3 0.0 copy-start.5
  37.3 0.1 fusion.3.bias
  37.4 1.0 %reshape.498 = bf16[16,1,8192]{2,1,0:T(2,128)(2,1)} reshape(bf16[16,2,4096]{2,1,0:T(2,128)(2,1)S(1)} %all-to-all-done) | data formatting | bytes 524288
  38.4 1.3 %copy.29 = bf16[16,1,8192]{2,0,1:T(8,128)(2,1)S(1)} copy(bf16[16,1,8192]{2,1,0:T(2,128)(2,1)} %reshape.498) | data formatting | bytes 524288
  39.7 0.0 copy-start.3
  39.7 1.6 %copy-done.3 = bf16[1,8,1024,128]{3,2,1,0:T(8,128)(2,1)S(1)} copy-done((bf16[1,8,1024,128]{3,2,1,0:T(8,128)(2,1)S(1)}, bf16[1,8,1024,128]{3,2,1,0:T(8,128)(2,1)}, u32[]{:S(2)}) %copy-start.3) | copy-done | bytes 2097176
  41.3 5.7 %attend.1 = bf16[16,1,80,128]{3,2,1,0:T(8,128)(2,1)} custom-call(bf16[16,8192]{1,0:T(8,128)(2,1)S(1)} %bitcast.51, bf16[1,8,1024,128]{3,2,1,0:T(8,128)(2,1)S(1)} %get-tuple-element.6.keys, bf16[1,8,1024,128]{3,2,1,0:T(8,128)(2,1)S(1)} %copy-done.3, bf16[8,128,128]{2,1,0:T(8,128)(2,1)S(1)} %get-tuple-element.8.tail_keys, ...), custom_call_target="tpu_custom_call" | custom-call | flops 536870912 | bytes 4194304 | tf_op jit(solution)/shard_map/attend/pallas_call | solution.py:143
  47.0 0.0 all-to-all-done.3
  47.0 6.8 %all-to-all-start.1 = ((bf16[16,1,80,128]{3,2,1,0:T(8,128)(2,1)}), bf16[16,1,80,128]{3,2,1,0:T(8,128)(2,1)S(1)}, u32[]{:S(2)}, u32[]{:S(2)}) async-start(bf16[16,1,80,128]{3,2,1,0:T(8,128)(2,1)} %attend.1), calls=%async_computation.1 | async-start | bytes 655360 | tf_op jit(solution)/shard_map/all_to_all | solution.py:228
  53.8 0.7 gather_fusion.3
  54.5 2.3 %gather_fusion.2 = bf16[16,2,1024]{2,1,0:T(2,128)(2,1)} fusion(bf16[96,2,1024]{2,1,0:T(2,128)(2,1)} %bitcast.5, s32[1024]{0:T(1024)S(1)} %pad_clamp_fusion), kind=kCustom, calls=%fused_computation.2 | custom fusion | bytes 131136 | tf_op jit(solution)/shard_map/gather | solution.py:280
  56.8 6.3 %all-to-all-done.1.partial = bf16[16,1,80,128]{3,2,1,0:T(8,128)(2,1)S(1)} async-done(((bf16[16,1,80,128]{3,2,1,0:T(8,128)(2,1)}), bf16[16,1,80,128]{3,2,1,0:T(8,128)(2,1)S(1)}, u32[]{:S(2)}, u32[]{:S(2)}) %all-to-all-start.1) | async-done | bytes 327712 | tf_op jit(solution)/shard_map/all_to_all | solution.py:228
  63.1 3.7 %all-to-all-start.4 = ((bf16[16,1,1,2,1024]{4,3,2,1,0:T(2,128)(2,1)}), bf16[16,1,1,2,1024]{4,3,2,1,0:T(2,128)(2,1)S(1)}, u32[]{:S(2)}, u32[]{:S(2)}) async-start(bf16[16,1,1,2,1024]{4,3,2,1,0:T(2,128)(2,1)} %bitcast.13), calls=%async_computation.4 | async-start | bytes 131072 | tf_op jit(solution)/shard_map/all_to_all | solution.py:228
  66.9 0.0 copy-done.5
  66.9 0.6 dynamic_slice.7
  68.1 5.8 %project.1 = bf16[16,64,128]{2,1,0:T(8,128)(2,1)} custom-call(bf16[16,1,80,128]{3,2,1,0:T(8,128)(2,1)S(1)} %all-to-all-done.1.partial, bf16[512,8192]{1,0:T(8,128)(2,1)} %weight.1), custom_call_target="tpu_custom_call" | custom-call | flops 134217728 | bytes 8388608 | tf_op jit(solution)/shard_map/project/pallas_call | solution.py:206
  74.0 0.4 all-to-all-done.4
  74.4 6.5 %all-to-all-start.2 = ((bf16[16,64,128]{2,1,0:T(8,128)(2,1)}), bf16[16,64,128]{2,1,0:T(8,128)(2,1)S(1)}, u32[]{:S(2)}, u32[]{:S(2)}) async-start(bf16[16,64,128]{2,1,0:T(8,128)(2,1)} %project.1), calls=%async_computation.2 | async-start | bytes 524288 | tf_op jit(solution)/shard_map/all_to_all | solution.py:228
  80.9 0.6 dynamic_slice.6
  81.5 0.6 iota_compare_fusion.1
  82.1 0.2 fusion
  82.3 0.0 copy-start.1
  82.3 7.1 %all-to-all-done.2 = bf16[16,64,128]{2,1,0:T(8,128)(2,1)S(1)} async-done(((bf16[16,64,128]{2,1,0:T(8,128)(2,1)}), bf16[16,64,128]{2,1,0:T(8,128)(2,1)S(1)}, u32[]{:S(2)}, u32[]{:S(2)}) %all-to-all-start.2) | async-done | bytes 262176 | tf_op jit(solution)/shard_map/all_to_all | solution.py:228
  89.4 0.7 convert_reduce_fusion
  90.0 0.0 copy-done.1
  (13 shorter events, 0.1 us)
Async XLA Ops:
  0.6 15.0 %copy-start = (s32[16]{0:T(128)S(1)}, s32[16]{0:T(128)}, u32[]{:S(2)}) copy-start(s32[16]{0:T(128)} %param.17) | copy-start | bytes 196
  0.6 28.7 %copy-start.4 = (bf16[1,2,1024]{2,1,0:T(2,128)(2,1)S(1)}, bf16[1,2,1024]{2,1,0:T(2,128)(2,1)}, u32[]{:S(2)}) copy-start(bf16[1,2,1024]{2,1,0:T(2,128)(2,1)} %new_kv.1) | copy-start | bytes 12292
  6.6 18.2 %all-to-all-start = ((bf16[16,2,4096]{2,1,0:T(2,128)(2,1)}), bf16[16,2,4096]{2,1,0:T(2,128)(2,1)S(1)}, u32[]{:S(2)}, u32[]{:S(2)}) async-start(bf16[16,2,4096]{2,1,0:T(2,128)(2,1)} %reshape.497), calls=%async_computation | async-start | bytes 524288 | tf_op jit(solution)/shard_map/all_to_all | solution.py:228
  24.8 22.1 %all-to-all-start.3 = ((bf16[16,6,1,2,1024]{4,3,1,2,0:T(2,128)(2,1)}), bf16[16,6,1,2,1024]{4,3,1,2,0:T(2,128)(2,1)}, u32[]{:S(2)}, u32[]{:S(2)}) async-start(bf16[16,6,1,2,1024]{4,3,1,2,0:T(2,128)(2,1)} %copy_bitcast_fusion), calls=%async_computation.3 | async-start | bytes 786432 | tf_op jit(solution)/shard_map/all_to_all | solution.py:228
  35.9 1.4 %copy-start.2 = (bf16[1,8,1024,128]{3,2,1,0:T(8,128)(2,1)}, bf16[1,8,1024,128]{3,2,1,0:T(8,128)(2,1)S(1)}, u32[]{:S(2)}) copy-start(bf16[1,8,1024,128]{3,2,1,0:T(8,128)(2,1)S(1)} %get-tuple-element.7.values) | copy-start | bytes 6291460
  37.3 29.6 %copy-start.5 = (s32[16]{0:T(128)S(1)}, s32[16]{0:T(128)}, u32[]{:S(2)}) copy-start(s32[16]{0:T(128)} %param.16) | copy-start | bytes 196
  39.7 1.6 %copy-start.3 = (bf16[1,8,1024,128]{3,2,1,0:T(8,128)(2,1)S(1)}, bf16[1,8,1024,128]{3,2,1,0:T(8,128)(2,1)}, u32[]{:S(2)}) copy-start(bf16[1,8,1024,128]{3,2,1,0:T(8,128)(2,1)} %copy-done.2) | copy-start | bytes 6291460
  47.0 16.2 %all-to-all-start.1 = ((bf16[16,1,80,128]{3,2,1,0:T(8,128)(2,1)}), bf16[16,1,80,128]{3,2,1,0:T(8,128)(2,1)S(1)}, u32[]{:S(2)}, u32[]{:S(2)}) async-start(bf16[16,1,80,128]{3,2,1,0:T(8,128)(2,1)} %attend.1), calls=%async_computation.1 | async-start | bytes 655360 | tf_op jit(solution)/shard_map/all_to_all | solution.py:228
  63.1 11.3 %all-to-all-start.4 = ((bf16[16,1,1,2,1024]{4,3,2,1,0:T(2,128)(2,1)}), bf16[16,1,1,2,1024]{4,3,2,1,0:T(2,128)(2,1)S(1)}, u32[]{:S(2)}, u32[]{:S(2)}) async-start(bf16[16,1,1,2,1024]{4,3,2,1,0:T(2,128)(2,1)} %bitcast.13), calls=%async_computation.4 | async-start | bytes 131072 | tf_op jit(solution)/shard_map/all_to_all | solution.py:228
  74.4 15.0 %all-to-all-start.2 = ((bf16[16,64,128]{2,1,0:T(8,128)(2,1)}), bf16[16,64,128]{2,1,0:T(8,128)(2,1)S(1)}, u32[]{:S(2)}, u32[]{:S(2)}) async-start(bf16[16,64,128]{2,1,0:T(8,128)(2,1)} %project.1), calls=%async_computation.2 | async-start | bytes 524288 | tf_op jit(solution)/shard_map/all_to_all | solution.py:228
  82.3 7.7 %copy-start.1 = (bf16[8,16,2,1024]{3,2,1,0:T(2,128)(2,1)}, bf16[8,16,2,1024]{3,2,1,0:T(2,128)(2,1)S(1)}, u32[]{:S(2)}) copy-start(bf16[8,16,2,1024]{3,2,1,0:T(2,128)(2,1)S(1)} %fusion) | copy-start | bytes 1572868

commit v2 on v1

--- a/solution.py
+++ b/solution.py
@@ -14,10 +14,145 @@
 CAP = 2
 
 STAT_ROWS = 16
-VMEM_LIMIT = 48 << 20
+VMEM_LIMIT = 20 << 20
 masked_score = -1e30
 bf16 = jnp.bfloat16
 f32 = jnp.float32
+
+
+def broadcast_kernel(query, out, scratch):
+    devices, rows = out.shape[:2]
+    heads = query.shape[1] // HD
+    for row in range(rows):
+        for head in range(heads):
+            scratch[head : head + 1, :] = query[row : row + 1, head * HD : (head + 1) * HD].astype(
+                f32
+            )
+        value = scratch[...].astype(bf16)
+        for device in range(devices):
+            out[device, row] = value
+
+
+def broadcast(queries, devices):
+    rows, width = queries.shape
+    return pl.pallas_call(
+        broadcast_kernel,
+        name="broadcast",
+        in_specs=[pl.BlockSpec(memory_space=pltpu.VMEM)],
+        out_specs=pl.BlockSpec(memory_space=pltpu.VMEM),
+        out_shape=jax.ShapeDtypeStruct((devices, rows, width // HD, HD), bf16),
+        scratch_shapes=[pltpu.VMEM((width // HD, HD), f32)],
+    )(queries)
+
+
+def source_of(row, parents, table, lengths, block_len):
+    parent = parents[row]
+    length = lengths[parent]
+    return length, table[parent, length // block_len]
+
+
+def place_of(stage, source, mine, pool_dev):
+    return (source // pool_dev ^ mine) & ((1 << stage) - 1)
+
+
+def fetch_block(stage, me, source, dest, part, rows, pool, arrived, target, sem):
+    pool_dev = pool.shape[0]
+    place = place_of(stage, source, me, pool_dev)
+
+    @pl.when(place == 0)
+    def _():
+        pltpu.make_async_copy(pool.at[source % pool_dev], target, sem).start()
+
+    for bit in range(stage):
+
+        @pl.when((place >> bit) == 1)
+        def _():
+            at = (dest >> (bit + 1)) * rows + part
+            pltpu.make_async_copy(arrived[bit].at[at], target, sem).start()
+
+
+def pick_kernel(stage, rows, me_ref, parents, table, lengths, pool, *refs):
+    arrived, (out, sem) = refs[:stage], refs[stage:]
+    me = me_ref[0]
+    count = out.shape[0]
+    flipped = me & ((1 << (stage + 1)) - 1) ^ (1 << stage)
+
+    def begin(at, carry):
+        dest = (at // rows << (stage + 1)) | flipped
+        part = at % rows
+        _, source = source_of(dest * rows + part, parents, table, lengths, pool.shape[1])
+        fetch_block(stage, me, source, dest, part, rows, pool, arrived, out.at[at], sem.at[at])
+        return carry
+
+    def finish(at, carry):
+        pltpu.make_async_copy(pool.at[0], out.at[at], sem.at[at]).wait()
+        return carry
+
+    lax.fori_loop(0, count, begin, 0)
+    lax.fori_loop(0, count, finish, 0)
+
+
+def pick(stage, devices, rows, meta, pool, arrived):
+    count = (devices >> (stage + 1)) * rows
+    block = pool.shape[1:]
+    smem = pl.BlockSpec(memory_space=pltpu.SMEM)
+    return pl.pallas_call(
+        functools.partial(pick_kernel, stage, rows),
+        name=f"pick{stage}",
+        in_specs=[smem] * 4 + [pl.BlockSpec(memory_space=pl.ANY)] * (1 + stage),
+        out_specs=pl.BlockSpec(memory_space=pltpu.VMEM),
+        out_shape=jax.ShapeDtypeStruct((count,) + block, bf16),
+        scratch_shapes=[pltpu.SemaphoreType.DMA((count,))],
+        compiler_params=pltpu.CompilerParams(vmem_limit_bytes=VMEM_LIMIT),
+        cost_estimate=pl.CostEstimate(
+            flops=0, bytes_accessed=4 * count * math.prod(block), transcendentals=0
+        ),
+    )(*meta, pool, *arrived)
+
+
+def place_kernel(stages, rows, me_ref, parents, table, lengths, fresh, new_kv, pool, *refs):
+    arrived, (out, sem) = refs[:stages], refs[stages:]
+    me = me_ref[0]
+    pool_dev, block_len = pool.shape[:2]
+    whole = pltpu.make_async_copy(pool, out, sem)
+    whole.start()
+    whole.wait()
+    for part in range(rows):
+        row = me * rows + part
+        length, source = source_of(row, parents, table, lengths, block_len)
+        slot = fresh[row] - me * pool_dev
+        fetch_block(stages, me, source, me, part, rows, pool, arrived, out.at[slot], sem)
+        pltpu.make_async_copy(pool.at[0], out.at[slot], sem).wait()
+        offset = length % block_len
+
+        def token(at, carry):
+            @pl.when(at == offset)
+            def _():
+                out[slot, at] = new_kv[part]
+
+            @pl.when(at > offset)
+            def _():
+                out[slot, at] = jnp.zeros(out.shape[2:], bf16)
+
+            return carry
+
+        lax.fori_loop(0, block_len, token, 0)
+
+
+def place(stages, rows, meta, fresh, new_kv, pool, arrived):
+    smem = pl.BlockSpec(memory_space=pltpu.SMEM)
+    return pl.pallas_call(
+        functools.partial(place_kernel, stages, rows),
+        name="place",
+        in_specs=[smem] * 5
+        + [pl.BlockSpec(memory_space=pltpu.VMEM)]
+        + [pl.BlockSpec(memory_space=pl.ANY)] * (1 + stages),
+        out_specs=pl.BlockSpec(memory_space=pltpu.VMEM),
+        out_shape=jax.ShapeDtypeStruct(pool.shape, bf16),
+        scratch_shapes=[pltpu.SemaphoreType.DMA],
+        compiler_params=pltpu.CompilerParams(vmem_limit_bytes=VMEM_LIMIT),
+        cost_estimate=pl.CostEstimate(flops=0, bytes_accessed=4 * pool.size, transcendentals=0),
+    )(*meta, fresh, new_kv, pool, *arrived)
 
 
 def split_kv(source, head, scratch, keys, values):
@@ -28,14 +163,31 @@
     values[...] = scratch[pl.ds(1, tokens, stride=2), :].astype(bf16)
 
 
-def unpack_kernel(prefix, pool, new_kv, keys, values, tail_keys, tail_values, scratch):
+def unpack_kernel(
+    me_ref,
+    parents,
+    table,
+    lengths,
+    prefix,
+    pool,
+    new_kv,
+    keys,
+    values,
+    tail_keys,
+    tail_values,
+    bias,
+    scratch,
+):
     for head in range(KVH):
         split_kv(prefix.at[0], head, scratch.at[head], keys.at[0, head], values.at[0, head])
 
     @pl.when((pl.program_id(0) == 0) & (pl.program_id(1) == 0))
     def _():
+        me = me_ref[0]
         blocks, block_len = pool.shape[:2]
         tokens = blocks * block_len
+        rows = new_kv.shape[0]
+        first = tokens - CAP * block_len
         for head in range(KVH):
             for block in range(blocks):
                 at = pl.ds(block * block_len, block_len)
@@ -46,8 +198,6 @@
                     tail_keys.at[head, at],
                     tail_values.at[head, at],
                 )
-            rows = new_kv.shape[0]
-            first = tokens - CAP * block_len
             at = pl.ds(first, CAP * block_len)
             lanes = slice(head * HD, (head + 1) * HD)
             slot = lax.broadcasted_iota(jnp.int32, (CAP * block_len, HD), 0)
@@ -59,32 +209,53 @@
             tail_keys[head, at, :] = key
             tail_values[head, at, :] = value
 
-
-def unpack(prefix_kv, pool, new_kv):
+        lane = lax.broadcasted_iota(jnp.int32, (1, tokens), 1)
+
+        def mask(row, carry):
+            parent = parents[row]
+            length = lengths[parent]
+            reach = jnp.zeros((1, tokens), jnp.int32)
+            for depth in range(table.shape[1]):
+                block = table[parent, depth] - me * blocks
+                reach = jnp.where(lane // block_len == block, length - depth * block_len, reach)
+            own = row - me * rows
+            own = jnp.where((own >= 0) & (own < rows), own + first, -1)
+            live = (lane % block_len < reach) | (lane == own)
+            bias[pl.ds(row, 1), :] = jnp.where(live, 0.0, masked_score)
+            return carry
+
+        lax.fori_loop(0, bias.shape[0], mask, 0)
+
+
+def unpack(meta, prefix_kv, pool, new_kv, row_total):
     requests, length, _, width = prefix_kv.shape
     blocks, block_len = pool.shape[:2]
     tokens = blocks * block_len
     step = min(256, length)
+    smem = pl.BlockSpec(memory_space=pltpu.SMEM)
     whole = lambda shape: pl.BlockSpec(shape, lambda r, i: (0,) * len(shape))
     return pl.pallas_call(
         unpack_kernel,
         name="unpack",
         grid=(requests, length // step),
-        in_specs=[
+        in_specs=[smem] * 4
+        + [
             pl.BlockSpec((1, step, 2, width), lambda r, i: (r, i, 0, 0)),
             whole(pool.shape),
             whole(new_kv.shape),
         ],
         out_specs=[pl.BlockSpec((1, KVH, step, HD), lambda r, i: (r, 0, i, 0))] * 2
-        + [whole((KVH, tokens, HD))] * 2,
+        + [whole((KVH, tokens, HD))] * 2
+        + [whole((row_total, tokens))],
         out_shape=[jax.ShapeDtypeStruct((requests, KVH, length, HD), bf16)] * 2
-        + [jax.ShapeDtypeStruct((KVH, tokens, HD), bf16)] * 2,
+        + [jax.ShapeDtypeStruct((KVH, tokens, HD), bf16)] * 2
+        + [jax.ShapeDtypeStruct((row_total, tokens), f32)],
         scratch_shapes=[pltpu.VMEM((KVH, 2 * step, HD), f32)],
         compiler_params=pltpu.CompilerParams(vmem_limit_bytes=VMEM_LIMIT),
         cost_estimate=pl.CostEstimate(
             flops=0, bytes_accessed=4 * prefix_kv.size, transcendentals=0
         ),
-    )(prefix_kv, pool, new_kv)
+    )(*meta, prefix_kv, pool, new_kv)
 
 
 def pieces(value):
@@ -95,18 +266,27 @@
     return high.astype(f32), middle.astype(f32), low.astype(f32)
 
 
-def attend_kernel(query, keys, values, tail_keys, tail_values, bias, out):
+def attend_kernel(query, keys, values, tail_keys, tail_values, bias, out, wide, stacks):
     groups = HQ // KVH
     targets = out.shape[0]
     beams = query.shape[0]
     count = groups * beams
+
+    @pl.when(pl.program_id(1) == 0)
+    def _():
+        wide[...] = query[...].astype(f32).reshape(beams * HQ, HD)
+        for head in range(HQ):
+            stacks[head * beams : (head + 1) * beams, :] = wide[
+                pl.ds(head, beams, stride=HQ), :
+            ].astype(bf16)
+
     share = count // targets
     factor = HD ** (-0.5) * math.log2(math.e)
-    stacked = jnp.concatenate([query[:, j * HD : (j + 1) * HD] for j in range(groups)], axis=0)
+    stacked = stacks[pl.ds(pl.multiple_of(pl.program_id(1) * count, count), count), :]
     contract = (((1,), (1,)), ((), ()))
     score = lax.dot_general(stacked, keys[0, 0], contract, preferred_element_type=f32)
     tail = lax.dot_general(stacked, tail_keys[0], contract, preferred_element_type=f32)
-    tail = tail + jnp.concatenate([bias[0]] * groups, axis=0)
+    tail = tail + jnp.concatenate([bias[...]] * groups, axis=0)
     top = jnp.maximum(
         jnp.max(score, axis=1, keepdims=True), jnp.max(tail, axis=1, keepdims=True)
     )
@@ -145,15 +325,16 @@
         name="attend",
         grid=(requests, KVH),
         in_specs=[
-            pl.BlockSpec((beams, groups * HD), lambda r, g: (r, g)),
+            pl.BlockSpec((beams, HQ, HD), lambda r, g: (r, 0, 0)),
             pl.BlockSpec((1, 1, length, HD), lambda r, g: (r, g, 0, 0)),
             pl.BlockSpec((1, 1, length, HD), lambda r, g: (r, g, 0, 0)),
             pl.BlockSpec((1, tokens, HD), lambda r, g: (g, 0, 0)),
             pl.BlockSpec((1, tokens, HD), lambda r, g: (g, 0, 0)),
-            pl.BlockSpec((1, beams, tokens), lambda r, g: (r, 0, 0)),
+            pl.BlockSpec((beams, tokens), lambda r, g: (r, 0)),
         ],
         out_specs=pl.BlockSpec((targets, 1, rows, HD), lambda r, g: (g, r, 0, 0)),
         out_shape=jax.ShapeDtypeStruct((devices, requests, rows, HD), bf16),
+        scratch_shapes=[pltpu.VMEM((beams * HQ, HD), f32), pltpu.VMEM((beams * HQ, HD), bf16)],
         compiler_params=pltpu.CompilerParams(vmem_limit_bytes=VMEM_LIMIT),
         cost_estimate=pl.CostEstimate(
             flops=4 * everyone.size * length,
@@ -232,75 +413,26 @@
     queries, new_kv, prefix_kv, pool, out_weight, parents, tail_table, fresh_slots, tail_lengths
 ):
     devices = lax.axis_size("ctx")
-    my_index = lax.axis_index("ctx")
-    local_rows = queries.shape[0]
-    row_total = local_rows * devices
-    pool_dev, block_len, _, kv_width = pool.shape
-    requests = prefix_kv.shape[0]
-    table_depth = tail_table.shape[1]
-    beams = row_total // requests
-    old_dev = pool_dev - CAP
-    tokens = pool_dev * block_len
-
-    width = queries.shape[1]
-    outgoing = jnp.broadcast_to(queries[None], (devices, local_rows, width))
-    everyone = exchange(outgoing).reshape(row_total, width)
-
-    token_parts = min(devices, block_len)
-    width_parts = devices // token_parts
-    piece = (block_len // token_parts, 2, kv_width // width_parts)
-    spread = pool[:old_dev].reshape(
-        old_dev, token_parts, piece[0], 2, width_parts, piece[2]
-    ).transpose(1, 4, 0, 2, 3, 5)
-    spread = exchange(spread.reshape((devices, old_dev) + piece))
-
-    keys, values, tail_keys, tail_values = unpack(prefix_kv, pool, new_kv)
-
-    parent_len = tail_lengths[parents]
-    parent_table = tail_table[parents]
-    offset = parent_len % block_len
-    source = jnp.take_along_axis(parent_table, (parent_len // block_len)[:, None], axis=1)[:, 0]
-    slot = lax.broadcasted_iota(jnp.int32, (1, 1, pool_dev), 2) + my_index * pool_dev
-    depth = lax.broadcasted_iota(jnp.int32, (1, table_depth, 1), 1)
-    matches = parent_table[:, :, None] == slot
-    reach = jnp.sum(
-        jnp.where(matches, parent_len[:, None, None] - depth * block_len, 0), axis=1
-    )
-    position = jnp.arange(tokens, dtype=jnp.int32)
-    live = position[None, :] % block_len < jnp.repeat(reach, block_len, axis=1)
-    row_ids = jnp.arange(row_total, dtype=jnp.int32)
-    own_slot = row_ids - my_index * local_rows
-    own = (own_slot >= 0) & (own_slot < local_rows)
-    live = live | (own[:, None] & (position[None, :] == old_dev * block_len + own_slot[:, None]))
-    bias = jnp.where(live, 0.0, masked_score).astype(f32).reshape(requests, beams, tokens)
-
-    partial = attend(everyone, keys, values, tail_keys, tail_values, bias, devices)
-    partial = exchange(partial)
-
-    picked = spread.reshape((devices * old_dev,) + piece)[
-        source // pool_dev * old_dev + source % pool_dev
-    ]
-    block = exchange(picked.reshape((devices, local_rows) + piece))
-
-    products = exchange(project(partial, out_weight, row_total).reshape(
-        devices, local_rows * (out_weight.shape[1] // HD), HD
-    ))
-    result = jnp.sum(products.astype(f32), axis=0).reshape(local_rows, out_weight.shape[1])
-
-    block = block.reshape((token_parts, width_parts, local_rows) + piece)
-    block = block.transpose(2, 0, 3, 4, 1, 5).reshape(local_rows, block_len, 2, kv_width)
-    own_offset = lax.dynamic_slice_in_dim(offset, my_index * local_rows, local_rows)
-    own_fresh = lax.dynamic_slice_in_dim(fresh_slots, my_index * local_rows, local_rows)
-    at = jnp.arange(block_len, dtype=jnp.int32)[None, :, None, None]
-    limit = own_offset[:, None, None, None]
-    copied = jnp.where(
-        at < limit, block, jnp.where(at == limit, new_kv[:, None], jnp.zeros((), bf16))
-    )
-    new_pool = pool
-    for row in range(local_rows):
-        new_pool = lax.dynamic_update_slice_in_dim(
-            new_pool, copied[row : row + 1], own_fresh[row] - my_index * pool_dev, 0
-        )
+    rows = queries.shape[0]
+    row_total = rows * devices
+    width = out_weight.shape[1]
+    stages = devices.bit_length() - 1
+    meta = (lax.axis_index("ctx").reshape(1), parents, tail_table, tail_lengths)
+
+    everyone = exchange(broadcast(queries, devices)).reshape(row_total, HQ, HD)
+    keys, values, tail_keys, tail_values, bias = unpack(meta, prefix_kv, pool, new_kv, row_total)
+
+    arrived = []
+    for stage in range(stages):
+        chosen = pick(stage, devices, rows, meta, pool, arrived)
+        pairs = [(i, i ^ (1 << stage)) for i in range(devices)]
+        arrived.append(lax.ppermute(chosen, "ctx", pairs))
+
+    partial = exchange(attend(everyone, keys, values, tail_keys, tail_values, bias, devices))
+    products = project(partial, out_weight, row_total)
+    products = exchange(products.reshape(devices, rows * (width // HD), HD))
+    result = jnp.sum(products.astype(f32), axis=0).reshape(rows, width)
+    new_pool = place(stages, rows, meta, fresh_slots, new_kv, pool, arrived)
     return (result, new_pool)
 
 

time: 91 us -> 85.6 us (0.941)
  Pallas kernels: 18.1 us -> 23.6 us
  other arithmetic: 5.57 us -> 0.66 us
  local copies, waits for them, and re-layouts: 15.6 us -> 12.3 us
  starting transfers between devices: 29.6 us -> 27.1 us
    ppermute x0 -> x4, waiting for transfers between devices: none -> 13.3 us  [local(): arrived.append(lax.ppermute(chosen, 'ctx', pairs))]
    all_to_all x5 -> x3, waiting for transfers between devices: 19.7 us -> 7.05 us  [exchange(): return lax.all_to_all(array, 'ctx', split_axis=0, concat_axis=0, tiled=True)]
    all_to_all x5 -> x3, starting transfers between devices: 29.6 us -> 18.9 us  [exchange(): return lax.all_to_all(array, 'ctx', split_axis=0, concat_axis=0, tiled=True)]
    ppermute x0 -> x4, starting transfers between devices: none -> 8.22 us  [local(): arrived.append(lax.ppermute(chosen, 'ctx', pairs))]
    pallas_call x0 -> x6, Pallas kernels: none -> 8.14 us  [the longest x4 4.72 us: pick(): pl.pallas_call(functools.partial(pick_kernel, stage, rows), name=f'pick{s...]
    unnamed x18 -> x27, local copies, waits for them, and re-layouts: 7.96 us -> 12.3 us
    gather x5 -> x0, local copies, waits for them, and re-layouts: 4.26 us -> none  [the longest x1 2.3 us: local(): spread.reshape((devices * old_dev,) + piece)]
    pallas_call x1, Pallas kernels: 5.85 us -> 3.3 us  [project(): pl.pallas_call(project_kernel, name='project', grid=(width // step,), in_...]
  transfers between devices with their start and end apart: 5 -> 7, of which waited for: 4 -> 4; matrix products, arithmetic and copies ran while one was open for 13% -> 1% of each run, Pallas kernels for 20% -> 19%
where the time goes in v2:
time: 85.6 us; the launch traced here: 84.9 us
  starting transfers between devices  27.1 us (32%)
  Pallas kernels  23.6 us (28%)
  waiting for transfers between devices  20.4 us (24%)
  local copies, waits for them, and re-layouts  12.3 us (14%)
    all_to_all x3, starting transfers between devices, exchange(): return lax.all_to_all(array, 'ctx', split_axis=0, concat_axis=0, tiled=True)  18.9 us
    ppermute x4, waiting for transfers between devices, local(): arrived.append(lax.ppermute(chosen, 'ctx', pairs))  13.3 us
    unnamed x27, local copies, waits for them, and re-layouts  12.3 us
    ppermute x4, starting transfers between devices, local(): arrived.append(lax.ppermute(chosen, 'ctx', pairs))  8.22 us
    all_to_all x3, waiting for transfers between devices, exchange(): return lax.all_to_all(array, 'ctx', split_axis=0, concat_axis=0, tiled=True)  7.05 us
    pallas_call x1, Pallas kernels, unpack(): pl.pallas_call(unpack_kernel, name='unpack', grid=(requests, length // st...  6.25 us
    pallas_call x1, Pallas kernels, attend(): pl.pallas_call(attend_kernel, name='attend', grid=(requests, KVH), in_spe...  5.96 us
    pallas_call x4, Pallas kernels, pick(): pl.pallas_call(functools.partial(pick_kernel, stage, rows), name=f'pick{s...  4.72 us
  transfers between devices with their start and end apart: 7, of which 4 were waited for; matrix products, arithmetic and copies ran while one was open for 1% of the time, Pallas kernels for 19%

profile of v2, /device:TPU:0, one launch (start us, length us, event | category | flops | bytes accessed | tf_op | source)
XLA Modules:
  0.0 84.9 jit_solution(6527138150138473719)
XLA Ops:
  0.6 1.5 %broadcast.1 = bf16[16,1,64,128]{3,2,1,0:T(8,128)(2,1)} custom-call(bf16[1,8192]{1,0:T(2,128)(2,1)} %query.1), custom_call_target="tpu_custom_call" | custom-call | tf_op jit(solution)/shard_map/broadcast/pallas_call | solution.py:38
  2.1 8.3 %all-to-all-start = ((bf16[16,1,64,128]{3,2,1,0:T(8,128)(2,1)}), bf16[16,1,64,128]{3,2,1,0:T(8,128)(2,1)S(1)}, u32[]{:S(2)}, u32[]{:S(2)}) async-start(bf16[16,1,64,128]{3,2,1,0:T(8,128)(2,1)} %broadcast.1), calls=%async_computation | async-start | bytes 524288 | tf_op jit(solution)/shard_map/all_to_all | solution.py:409
  10.5 0.8 copy.18.table
  11.3 0.0 copy-start
  11.3 1.0 %copy-done = bf16[8,16,2,1024]{3,2,1,0:T(2,128)(2,1)S(1)} copy-done((bf16[8,16,2,1024]{3,2,1,0:T(2,128)(2,1)S(1)}, bf16[8,16,2,1024]{3,2,1,0:T(2,128)(2,1)}, u32[]{:S(2)}) %copy-start) | copy-done | bytes 524312
  12.3 0.0 copy-start.3
  12.3 2.2 %copy-done.3 = bf16[1,1024,2,1024]{3,2,1,0:T(2,128)(2,1)S(1)} copy-done((bf16[1,1024,2,1024]{3,2,1,0:T(2,128)(2,1)S(1)}, bf16[1,1024,2,1024]{3,2,1,0:T(2,128)(2,1)}, u32[]{:S(2)}) %copy-start.3) | copy-done | bytes 4194328
  14.5 0.0 copy-start.6
  14.5 0.7 copy-done.6
  15.1 0.0 copy-start.8
  15.1 0.7 copy-done.8
  15.8 0.0 copy-start.10
  15.8 0.7 copy-done.10
  16.5 0.0 copy-start.1
  16.5 0.0 copy-start.7
  16.5 0.0 copy-start.9
  16.5 6.2 %unpack.1 = (bf16[1,8,1024,128]{3,2,1,0:T(8,128)(2,1)S(1)}, bf16[1,8,1024,128]{3,2,1,0:T(8,128)(2,1)S(1)}, bf16[8,128,128]{2,1,0:T(8,128)(2,1)S(1)}, bf16[8,128,128]{2,1,0:T(8,128)(2,1)S(1)}, f32[16,128]{1,0:T(8,128)S(1)}) custom-call(s32[1]{0:T(128)} %bitcast.1.me_ref, s32[16]{0:T(128)S(1)} %copy-done.6, s32[16,4]{1,0:T(8,128)S(1)} %copy.18.table, ...), custom_call_target="tpu_custom_call" | custom-call | bytes 8388608 | tf_op jit(solution)/shard_map/unpack/pallas_call | solution.py:237
  22.7 0.0 copy-start.4
  22.8 1.3 %copy-done.4 = bf16[1,8,1024,128]{3,2,1,0:T(8,128)(2,1)} copy-done((bf16[1,8,1024,128]{3,2,1,0:T(8,128)(2,1)}, bf16[1,8,1024,128]{3,2,1,0:T(8,128)(2,1)S(1)}, u32[]{:S(2)}) %copy-start.4) | copy-done | bytes 2097176
  24.1 0.0 all-to-all-done
  24.1 0.0 copy-start.5
  24.1 1.6 %copy-done.5 = bf16[1,8,1024,128]{3,2,1,0:T(8,128)(2,1)S(1)} copy-done((bf16[1,8,1024,128]{3,2,1,0:T(8,128)(2,1)S(1)}, bf16[1,8,1024,128]{3,2,1,0:T(8,128)(2,1)}, u32[]{:S(2)}) %copy-start.5) | copy-done | bytes 2097176
  25.7 6.0 %attend.1 = bf16[16,1,80,128]{3,2,1,0:T(8,128)(2,1)} custom-call(bf16[16,64,128]{2,1,0:T(8,128)(2,1)S(1)} %bitcast.3, bf16[1,8,1024,128]{3,2,1,0:T(8,128)(2,1)S(1)} %get-tuple-element.7.keys, bf16[1,8,1024,128]{3,2,1,0:T(8,128)(2,1)S(1)} %copy-done.5, bf16[8,128,128]{2,1,0:T(8,128)(2,1)S(1)} %get-tuple-element.9.tail_keys, ...), custom_call_target="tpu_custom_call" | custom-call | flops 536870912 | bytes 4194304 | tf_op jit(solution)/shard_map/attend/pallas_call | solution.py:323
  31.6 6.9 %all-to-all-start.1 = ((bf16[16,1,80,128]{3,2,1,0:T(8,128)(2,1)}), bf16[16,1,80,128]{3,2,1,0:T(8,128)(2,1)S(1)}, u32[]{:S(2)}, u32[]{:S(2)}) async-start(bf16[16,1,80,128]{3,2,1,0:T(8,128)(2,1)} %attend.1), calls=%async_computation.1 | async-start | bytes 655360 | tf_op jit(solution)/shard_map/all_to_all | solution.py:409
  38.5 0.0 copy-done.1
  38.6 0.0 copy-done.7
  38.6 0.0 copy-done.9
  38.6 1.7 %pick0.1 = bf16[8,16,2,1024]{3,2,1,0:T(2,128)(2,1)S(1)} custom-call(s32[1]{0:T(128)} %bitcast.1.me_ref, s32[16]{0:T(128)S(1)} %copy-done.7, s32[16,4]{1,0:T(8,128)S(1)} %copy.18.table, s32[16]{0:T(128)S(1)} %copy-done.9, bf16[8,16,2,1024]{3,2,1,0:T(2,128)(2,1)S(1)} %copy-done.1), custom_call_target="tpu_custom_call" | custom-call | bytes 1048576 | tf_op jit(solution)/shard_map/pick0/pallas_call | solution.py:99
  40.3 2.0 %collective-permute-start = (bf16[8,16,2,1024]{3,2,1,0:T(2,128)(2,1)S(1)}, bf16[8,16,2,1024]{3,2,1,0:T(2,128)(2,1)S(1)}, u32[]{:S(2)}, u32[]{:S(2)}) collective-permute-start(bf16[8,16,2,1024]{3,2,1,0:T(2,128)(2,1)S(1)} %pick0.1), channel_id=1, source_target_pairs={{0,1},{1,0},{2,3},{3,2},{4,5},{5,4},{6,7},{7,6},{8,9},{9,8},{10,11... | collective-permute-start | bytes 1572872 | tf_op jit(solution)/shard_map/ppermute | solution.py:429
  42.3 7.0 %all-to-all-done.1.partial = bf16[16,1,80,128]{3,2,1,0:T(8,128)(2,1)S(1)} async-done(((bf16[16,1,80,128]{3,2,1,0:T(8,128)(2,1)}), bf16[16,1,80,128]{3,2,1,0:T(8,128)(2,1)S(1)}, u32[]{:S(2)}, u32[]{:S(2)}) %all-to-all-start.1) | async-done | bytes 327712 | tf_op jit(solution)/shard_map/all_to_all | solution.py:409
  49.3 0.0 copy-start.2
  49.3 3.4 %copy-done.2 = bf16[512,8192]{1,0:T(8,128)(2,1)S(1)} copy-done((bf16[512,8192]{1,0:T(8,128)(2,1)S(1)}, bf16[512,8192]{1,0:T(8,128)(2,1)}, u32[]{:S(2)}) %copy-start.2) | copy-done | bytes 8388632
  52.7 3.3 %project.1 = bf16[16,64,128]{2,1,0:T(8,128)(2,1)} custom-call(bf16[16,1,80,128]{3,2,1,0:T(8,128)(2,1)S(1)} %all-to-all-done.1.partial, bf16[512,8192]{1,0:T(8,128)(2,1)S(1)} %copy-done.2), custom_call_target="tpu_custom_call" | custom-call | flops 134217728 | bytes 8388608 | tf_op jit(solution)/shard_map/project/pallas_call | solution.py:387
  56.0 0.0 copy-start.11
  56.0 0.0 copy-start.12
  56.0 3.7 %all-to-all-start.2 = ((bf16[16,64,128]{2,1,0:T(8,128)(2,1)}), bf16[16,64,128]{2,1,0:T(8,128)(2,1)S(1)}, u32[]{:S(2)}, u32[]{:S(2)}) async-start(bf16[16,64,128]{2,1,0:T(8,128)(2,1)} %project.1), calls=%async_computation.2 | async-start | bytes 524288 | tf_op jit(solution)/shard_map/all_to_all | solution.py:409
  59.7 0.0 collective-permute-done.refs_0_
  59.7 1.2 %pick1.1 = bf16[4,16,2,1024]{3,2,1,0:T(2,128)(2,1)S(1)} custom-call(s32[1]{0:T(128)} %bitcast.1.me_ref, s32[16]{0:T(128)S(1)} %copy-done.7, s32[16,4]{1,0:T(8,128)S(1)} %copy.18.table, s32[16]{0:T(128)S(1)} %copy-done.9, bf16[8,16,2,1024]{3,2,1,0:T(2,128)(2,1)S(1)} %copy-done.1, bf16[8,16,2,1024]{3,2,1,0:T(2,128)(2,1)S(1)} %collective-permute-done.refs_0_), custom_call_target="tpu_custom_call" | custom-call | bytes 524288 | tf_op jit(solution)/shard_map/pick1/pallas_call | solution.py:99
  60.9 2.0 %collective-permute-start.1 = (bf16[4,16,2,1024]{3,2,1,0:T(2,128)(2,1)S(1)}, bf16[4,16,2,1024]{3,2,1,0:T(2,128)(2,1)S(1)}, u32[]{:S(2)}, u32[]{:S(2)}) collective-permute-start(bf16[4,16,2,1024]{3,2,1,0:T(2,128)(2,1)S(1)} %pick1.1), channel_id=1, source_target_pairs={{0,2},{1,3},{2,0},{3,1},{4,6},{5,7},{6,4},{7,5},{8,10},{9,11},{10,... | collective-permute-start | bytes 786440 | tf_op jit(solution)/shard_map/ppermute | solution.py:429
  62.9 7.3 %collective-permute-done.1.refs_1_ = bf16[4,16,2,1024]{3,2,1,0:T(2,128)(2,1)S(1)} collective-permute-done((bf16[4,16,2,1024]{3,2,1,0:T(2,128)(2,1)S(1)}, bf16[4,16,2,1024]{3,2,1,0:T(2,128)(2,1)S(1)}, u32[]{:S(2)}, u32[]{:S(2)}) %collective-permute-start.1) | collective-permute-done | bytes 262176 | tf_op jit(solution)/shard_map/ppermute | solution.py:429
  70.2 1.0 %pick2.1 = bf16[2,16,2,1024]{3,2,1,0:T(2,128)(2,1)S(1)} custom-call(s32[1]{0:T(128)} %bitcast.1.me_ref, s32[16]{0:T(128)S(1)} %copy-done.7, s32[16,4]{1,0:T(8,128)S(1)} %copy.18.table, s32[16]{0:T(128)S(1)} %copy-done.9, bf16[8,16,2,1024]{3,2,1,0:T(2,128)(2,1)S(1)} %copy-done.1, bf16[8,16,2,1024]{3,2,1,0:T(2,128)(2,1)S(1)} %collective-permute-done.refs_0_, ...), custom_call_target="tpu_custom_call" | custom-call | bytes 262144 | tf_op jit(solution)/shard_map/pick2/pallas_call | solution.py:99
  71.2 1.7 %collective-permute-start.2 = (bf16[2,16,2,1024]{3,2,1,0:T(2,128)(2,1)S(1)}, bf16[2,16,2,1024]{3,2,1,0:T(2,128)(2,1)S(1)}, u32[]{:S(2)}, u32[]{:S(2)}) collective-permute-start(bf16[2,16,2,1024]{3,2,1,0:T(2,128)(2,1)S(1)} %pick2.1), channel_id=1, source_target_pairs={{0,4},{1,5},{2,6},{3,7},{4,0},{5,1},{6,2},{7,3},{8,12},{9,13},{10,... | collective-permute-start | bytes 393224 | tf_op jit(solution)/shard_map/ppermute | solution.py:429
  72.9 3.3 %collective-permute-done.2.refs_2_ = bf16[2,16,2,1024]{3,2,1,0:T(2,128)(2,1)S(1)} collective-permute-done((bf16[2,16,2,1024]{3,2,1,0:T(2,128)(2,1)S(1)}, bf16[2,16,2,1024]{3,2,1,0:T(2,128)(2,1)S(1)}, u32[]{:S(2)}, u32[]{:S(2)}) %collective-permute-start.2) | collective-permute-done | bytes 131104 | tf_op jit(solution)/shard_map/ppermute | solution.py:429
  76.2 0.8 pick3.1
  77.1 2.6 %collective-permute-start.3 = (bf16[1,16,2,1024]{3,2,1,0:T(2,128)(2,1)S(1)}, bf16[1,16,2,1024]{3,2,1,0:T(2,128)(2,1)S(1)}, u32[]{:S(2)}, u32[]{:S(2)}) collective-permute-start(bf16[1,16,2,1024]{3,2,1,0:T(2,128)(2,1)S(1)} %pick3.1), channel_id=1, source_target_pairs={{0,8},{1,9},{2,10},{3,11},{4,12},{5,13},{6,14},{7,15},{8,0},{9,1},... | collective-permute-start | bytes 196616 | tf_op jit(solution)/shard_map/ppermute | solution.py:429
  79.6 2.7 %collective-permute-done.3.refs_3_ = bf16[1,16,2,1024]{3,2,1,0:T(2,128)(2,1)S(1)} collective-permute-done((bf16[1,16,2,1024]{3,2,1,0:T(2,128)(2,1)S(1)}, bf16[1,16,2,1024]{3,2,1,0:T(2,128)(2,1)S(1)}, u32[]{:S(2)}, u32[]{:S(2)}) %collective-permute-start.3) | collective-permute-done | bytes 65568 | tf_op jit(solution)/shard_map/ppermute | solution.py:429
  82.3 0.0 copy-done.11
  82.3 0.0 copy-done.12
  82.3 1.9 %place.1 = bf16[8,16,2,1024]{3,2,1,0:T(2,128)(2,1)} custom-call(s32[1]{0:T(128)} %bitcast.1.me_ref, s32[16]{0:T(128)S(1)} %copy-done.7, s32[16,4]{1,0:T(8,128)S(1)} %copy.18.table, s32[16]{0:T(128)S(1)} %copy-done.9, s32[16]{0:T(128)S(1)} %copy-done.12, bf16[1,2,1024]{2,1,0:T(2,128)(2,1)S(1)} %copy-done.11, bf16[8,16,2,1024]{3,2,1,0:T(2,128)(2,1)S(1)} %copy-done.1, ...), custom_call_target="tpu_custom_call" | custom-call | bytes 1048576 | tf_op jit(solution)/shard_map/place/pallas_call | solution.py:144
  84.2 0.0 all-to-all-done.2
  84.2 0.7 convert_reduce_fusion
Async XLA Ops:
  2.1 21.9 %all-to-all-start = ((bf16[16,1,64,128]{3,2,1,0:T(8,128)(2,1)}), bf16[16,1,64,128]{3,2,1,0:T(8,128)(2,1)S(1)}, u32[]{:S(2)}, u32[]{:S(2)}) async-start(bf16[16,1,64,128]{3,2,1,0:T(8,128)(2,1)} %broadcast.1), calls=%async_computation | async-start | bytes 524288 | tf_op jit(solution)/shard_map/all_to_all | solution.py:409
  11.3 1.0 %copy-start = (bf16[8,16,2,1024]{3,2,1,0:T(2,128)(2,1)S(1)}, bf16[8,16,2,1024]{3,2,1,0:T(2,128)(2,1)}, u32[]{:S(2)}) copy-start(bf16[8,16,2,1024]{3,2,1,0:T(2,128)(2,1)} %pool.11) | copy-start | bytes 1572868
  12.3 2.2 %copy-start.3 = (bf16[1,1024,2,1024]{3,2,1,0:T(2,128)(2,1)S(1)}, bf16[1,1024,2,1024]{3,2,1,0:T(2,128)(2,1)}, u32[]{:S(2)}) copy-start(bf16[1,1024,2,1024]{3,2,1,0:T(2,128)(2,1)} %prefix.1) | copy-start | bytes 12582916
  14.5 0.7 copy-start.6
  15.1 0.7 copy-start.8
  15.8 0.7 copy-start.10
  16.5 22.1 %copy-start.1 = (bf16[8,16,2,1024]{3,2,1,0:T(2,128)(2,1)S(1)}, bf16[8,16,2,1024]{3,2,1,0:T(2,128)(2,1)}, u32[]{:S(2)}) copy-start(bf16[8,16,2,1024]{3,2,1,0:T(2,128)(2,1)} %pool.11) | copy-start | bytes 1572868
  16.5 22.1 %copy-start.7 = (s32[16]{0:T(128)S(1)}, s32[16]{0:T(128)}, u32[]{:S(2)}) copy-start(s32[16]{0:T(128)} %parents.11) | copy-start | bytes 196
  16.5 22.1 %copy-start.9 = (s32[16]{0:T(128)S(1)}, s32[16]{0:T(128)}, u32[]{:S(2)}) copy-start(s32[16]{0:T(128)} %lengths.11) | copy-start | bytes 196
  22.7 1.3 %copy-start.4 = (bf16[1,8,1024,128]{3,2,1,0:T(8,128)(2,1)}, bf16[1,8,1024,128]{3,2,1,0:T(8,128)(2,1)S(1)}, u32[]{:S(2)}) copy-start(bf16[1,8,1024,128]{3,2,1,0:T(8,128)(2,1)S(1)} %get-tuple-element.8.values) | copy-start | bytes 6291460
  24.1 1.6 %copy-start.5 = (bf16[1,8,1024,128]{3,2,1,0:T(8,128)(2,1)S(1)}, bf16[1,8,1024,128]{3,2,1,0:T(8,128)(2,1)}, u32[]{:S(2)}) copy-start(bf16[1,8,1024,128]{3,2,1,0:T(8,128)(2,1)} %copy-done.4) | copy-start | bytes 6291460
  31.6 17.7 %all-to-all-start.1 = ((bf16[16,1,80,128]{3,2,1,0:T(8,128)(2,1)}), bf16[16,1,80,128]{3,2,1,0:T(8,128)(2,1)S(1)}, u32[]{:S(2)}, u32[]{:S(2)}) async-start(bf16[16,1,80,128]{3,2,1,0:T(8,128)(2,1)} %attend.1), calls=%async_computation.1 | async-start | bytes 655360 | tf_op jit(solution)/shard_map/all_to_all | solution.py:409
  40.3 19.4 %collective-permute-start = (bf16[8,16,2,1024]{3,2,1,0:T(2,128)(2,1)S(1)}, bf16[8,16,2,1024]{3,2,1,0:T(2,128)(2,1)S(1)}, u32[]{:S(2)}, u32[]{:S(2)}) collective-permute-start(bf16[8,16,2,1024]{3,2,1,0:T(2,128)(2,1)S(1)} %pick0.1), channel_id=1, source_target_pairs={{0,1},{1,0},{2,3},{3,2},{4,5},{5,4},{6,7},{7,6},{8,9},{9,8},{10,11... | collective-permute-start | bytes 1572872 | tf_op jit(solution)/shard_map/ppermute | solution.py:429
  49.3 3.4 %copy-start.2 = (bf16[512,8192]{1,0:T(8,128)(2,1)S(1)}, bf16[512,8192]{1,0:T(8,128)(2,1)}, u32[]{:S(2)}) copy-start(bf16[512,8192]{1,0:T(8,128)(2,1)} %weight.1) | copy-start | bytes 25165828
  56.0 26.3 %copy-start.11 = (bf16[1,2,1024]{2,1,0:T(2,128)(2,1)S(1)}, bf16[1,2,1024]{2,1,0:T(2,128)(2,1)}, u32[]{:S(2)}) copy-start(bf16[1,2,1024]{2,1,0:T(2,128)(2,1)} %new_kv.3) | copy-start | bytes 12292
  56.0 26.3 %copy-start.12 = (s32[16]{0:T(128)S(1)}, s32[16]{0:T(128)}, u32[]{:S(2)}) copy-start(s32[16]{0:T(128)} %fresh.1) | copy-start | bytes 196
  56.0 28.2 %all-to-all-start.2 = ((bf16[16,64,128]{2,1,0:T(8,128)(2,1)}), bf16[16,64,128]{2,1,0:T(8,128)(2,1)S(1)}, u32[]{:S(2)}, u32[]{:S(2)}) async-start(bf16[16,64,128]{2,1,0:T(8,128)(2,1)} %project.1), calls=%async_computation.2 | async-start | bytes 524288 | tf_op jit(solution)/shard_map/all_to_all | solution.py:409
  60.9 9.3 %collective-permute-start.1 = (bf16[4,16,2,1024]{3,2,1,0:T(2,128)(2,1)S(1)}, bf16[4,16,2,1024]{3,2,1,0:T(2,128)(2,1)S(1)}, u32[]{:S(2)}, u32[]{:S(2)}) collective-permute-start(bf16[4,16,2,1024]{3,2,1,0:T(2,128)(2,1)S(1)} %pick1.1), channel_id=1, source_target_pairs={{0,2},{1,3},{2,0},{3,1},{4,6},{5,7},{6,4},{7,5},{8,10},{9,11},{10,... | collective-permute-start | bytes 786440 | tf_op jit(solution)/shard_map/ppermute | solution.py:429
  71.2 5.0 %collective-permute-start.2 = (bf16[2,16,2,1024]{3,2,1,0:T(2,128)(2,1)S(1)}, bf16[2,16,2,1024]{3,2,1,0:T(2,128)(2,1)S(1)}, u32[]{:S(2)}, u32[]{:S(2)}) collective-permute-start(bf16[2,16,2,1024]{3,2,1,0:T(2,128)(2,1)S(1)} %pick2.1), channel_id=1, source_target_pairs={{0,4},{1,5},{2,6},{3,7},{4,0},{5,1},{6,2},{7,3},{8,12},{9,13},{10,... | collective-permute-start | bytes 393224 | tf_op jit(solution)/shard_map/ppermute | solution.py:429
  77.1 5.2 %collective-permute-start.3 = (bf16[1,16,2,1024]{3,2,1,0:T(2,128)(2,1)S(1)}, bf16[1,16,2,1024]{3,2,1,0:T(2,128)(2,1)S(1)}, u32[]{:S(2)}, u32[]{:S(2)}) collective-permute-start(bf16[1,16,2,1024]{3,2,1,0:T(2,128)(2,1)S(1)} %pick3.1), channel_id=1, source_target_pairs={{0,8},{1,9},{2,10},{3,11},{4,12},{5,13},{6,14},{7,15},{8,0},{9,1},... | collective-permute-start | bytes 196616 | tf_op jit(solution)/shard_map/ppermute | solution.py:429

commit v3 on v2

v3 whole, which is shorter than its diff:
```python
import functools
import math

import jax
import jax.numpy as jnp
from jax import lax
from jax.experimental import pallas as pl
from jax.experimental.pallas import tpu as pltpu
from jax.sharding import PartitionSpec as P


HQ = 64
KVH = 8
HD = 128
CAP = 2

STAT_ROWS = 16
AT_ONCE = 2
VMEM_LIMIT = 20 << 20
masked_score = -1e30
bf16 = jnp.bfloat16
f32 = jnp.float32


def in_hbm(array):
    return pltpu.with_memory_space_constraint(array, pltpu.HBM)


def rounds_of(devices):
    total = devices.bit_length() - 1
    return [(bit, min(2, total - bit)) for bit in range(0, total, 2)]


def channels_of(rounds):
    return [(first, mask) for first, bits in rounds for mask in range(1, 1 << bits)]


def load_meta(sources, targets, sem):
    copies = [pltpu.make_async_copy(s, t, sem.at[i]) for i, (s, t) in enumerate(zip(sources, targets))]
    for copy in copies:
        copy.start()
    return copies


def meta_scratch(meta):
    return [pltpu.SMEM(m.shape, jnp.int32) for m in meta] + [pltpu.SemaphoreType.DMA((len(meta),))]


def source_of(row, parents, table, lengths, block_len):
    parent = parents[row]
    length = lengths[parent]
    return length, table[length // block_len, parent]


def fetch_block(rounds, me, source, dest, part, rows, pool, arrived, target, sem):
    pool_dev = pool.shape[0]
    done = sum(bits for _, bits in rounds)
    moved = (source // pool_dev ^ me) & ((1 << done) - 1)

    @pl.when(moved == 0)
    def _():
        pltpu.make_async_copy(pool.at[source % pool_dev], target, sem).start()

    for (first, mask), ref in zip(channels_of(rounds), arrived):
        bits = dict(rounds)[first]

        @pl.when((moved >> first) == mask)
        def _():
            at = (dest >> (first + bits)) * rows + part
            pltpu.make_async_copy(ref.at[at], target, sem).start()


def begin_picks(rounds, now, rows, me, meta, pool, arrived, outs, sem):
    first, bits = now
    for mask in range(1, 1 << bits):
        out = outs[mask - 1]
        low = (me & ((1 << (first + bits)) - 1)) ^ (mask << first)

        def begin(at, carry):
            dest = (at // rows << (first + bits)) | low
            part = at % rows
            _, source = source_of(dest * rows + part, *meta, pool.shape[1])
            fetch_block(
                rounds, me, source, dest, part, rows, pool, arrived, out.at[at], sem.at[mask - 1, at]
            )
            return carry

        lax.fori_loop(0, out.shape[0], begin, 0)


def end_picks(pool, outs, sem):
    for index, out in enumerate(outs):

        def finish(at, carry):
            pltpu.make_async_copy(pool.at[0], out.at[at], sem.at[index, at]).wait()
            return carry

        lax.fori_loop(0, out.shape[0], finish, 0)


def ask_kernel(now, query, parents_in, table_in, lengths_in, pool, out, *refs):
    devices, rows = out.shape[:2]
    partners = (1 << now[1]) - 1
    outs, (wide, parents, table, lengths, meta_sem, sem) = refs[:partners], refs[partners:]
    me = lax.axis_index("ctx")
    meta = (parents, table, lengths)
    copies = load_meta((parents_in, table_in, lengths_in), meta, meta_sem)
    heads = query.shape[1] // HD
    for row in range(rows):
        for head in range(heads):
            wide[row, head : head + 1, :] = query[
                row : row + 1, head * HD : (head + 1) * HD
            ].astype(f32)
    for copy in copies:
        copy.wait()
    begin_picks([], now, rows, me, meta, pool, [], outs, sem)
    for row in range(rows):
        value = wide[row].astype(bf16)
        for device in range(devices):
            out[device, row] = value
    end_picks(pool, outs, sem)


def pick_shapes(now, devices, rows, pool):
    first, bits = now
    count = (devices >> (first + bits)) * rows
    partners = (1 << bits) - 1
    return [jax.ShapeDtypeStruct((count,) + pool.shape[1:], bf16)] * partners, (partners, count)


def ask(now, devices, queries, meta, pool):
    rows, width = queries.shape
    heads = width // HD
    shapes, semaphores = pick_shapes(now, devices, rows, pool)
    vmem, hbm = pl.BlockSpec(memory_space=pltpu.VMEM), pl.BlockSpec(memory_space=pltpu.HBM)
    return pl.pallas_call(
        functools.partial(ask_kernel, now),
        name="ask",
        in_specs=[vmem] + [hbm] * 4,
        out_specs=[vmem] * (1 + len(shapes)),
        out_shape=[jax.ShapeDtypeStruct((devices, rows, heads, HD), bf16)] + shapes,
        scratch_shapes=[pltpu.VMEM((rows, heads, HD), f32)]
        + meta_scratch(meta)
        + [pltpu.SemaphoreType.DMA(semaphores)],
        compiler_params=pltpu.CompilerParams(vmem_limit_bytes=VMEM_LIMIT),
    )(queries, *map(in_hbm, meta), in_hbm(pool))


def pick_kernel(rounds, now, rows, channels, parents_in, table_in, lengths_in, pool, *refs):
    partners = (1 << now[1]) - 1
    arrived, refs = refs[:channels], refs[channels:]
    outs, (parents, table, lengths, meta_sem, sem) = refs[:partners], refs[partners:]
    meta = (parents, table, lengths)
    for copy in load_meta((parents_in, table_in, lengths_in), meta, meta_sem):
        copy.wait()
    begin_picks(rounds, now, rows, lax.axis_index("ctx"), meta, pool, arrived, outs, sem)
    end_picks(pool, outs, sem)


def pick(rounds, now, devices, rows, meta, pool, arrived):
    shapes, semaphores = pick_shapes(now, devices, rows, pool)
    vmem, hbm = pl.BlockSpec(memory_space=pltpu.VMEM), pl.BlockSpec(memory_space=pltpu.HBM)
    return pl.pallas_call(
        functools.partial(pick_kernel, rounds, now, rows, len(arrived)),
        name="pick",
        in_specs=[hbm] * 4 + [pl.BlockSpec(memory_space=pl.ANY)] * len(arrived),
        out_specs=[vmem] * len(shapes),
        out_shape=shapes,
        scratch_shapes=meta_scratch(meta) + [pltpu.SemaphoreType.DMA(semaphores)],
        compiler_params=pltpu.CompilerParams(vmem_limit_bytes=VMEM_LIMIT),
        cost_estimate=pl.CostEstimate(flops=0, bytes_accessed=1 << 22, transcendentals=0),
    )(*map(in_hbm, meta), in_hbm(pool), *arrived)


def place_kernel(rounds, rows, parents_in, table_in, lengths_in, fresh_in, new_kv, pool, *refs):
    channels = len(channels_of(rounds))
    arrived, (out, parents, table, lengths, fresh, meta_sem, sem) = refs[:channels], refs[channels:]
    me = lax.axis_index("ctx")
    pool_dev, block_len = pool.shape[:2]
    whole = pltpu.make_async_copy(pool, out, sem)
    whole.start()
    sources = (parents_in, table_in, lengths_in, fresh_in)
    for copy in load_meta(sources, (parents, table, lengths, fresh), meta_sem):
        copy.wait()
    whole.wait()
    for part in range(rows):
        row = me * rows + part
        length, source = source_of(row, parents, table, lengths, block_len)
        slot = fresh[row] - me * pool_dev
        fetch_block(rounds, me, source, me, part, rows, pool, arrived, out.at[slot], sem)
        pltpu.make_async_copy(pool.at[0], out.at[slot], sem).wait()
        offset = length % block_len

        def token(at, carry):
            @pl.when(at == offset)
            def _():
                out[slot, at] = new_kv[part]

            @pl.when(at > offset)
            def _():
                out[slot, at] = jnp.zeros(out.shape[2:], bf16)

            return carry

        lax.fori_loop(0, block_len, token, 0)


def place(rounds, rows, meta, new_kv, pool, arrived):
    vmem, hbm = pl.BlockSpec(memory_space=pltpu.VMEM), pl.BlockSpec(memory_space=pltpu.HBM)
    return pl.pallas_call(
        functools.partial(place_kernel, rounds, rows),
        name="place",
        in_specs=[hbm] * 4 + [vmem, hbm] + [pl.BlockSpec(memory_space=pl.ANY)] * len(arrived),
        out_specs=vmem,
        out_shape=jax.ShapeDtypeStruct(pool.shape, bf16),
        scratch_shapes=meta_scratch(meta) + [pltpu.SemaphoreType.DMA],
        compiler_params=pltpu.CompilerParams(vmem_limit_bytes=VMEM_LIMIT),
        cost_estimate=pl.CostEstimate(flops=0, bytes_accessed=4 * pool.size, transcendentals=0),
    )(*map(in_hbm, meta), new_kv, in_hbm(pool), *arrived)


def split_kv(source, head, scratch, keys, values):
    tokens = source.shape[0]
    pairs = source[:, :, head * HD : (head + 1) * HD].astype(f32)
    scratch[: 2 * tokens, :] = pairs.reshape(2 * tokens, HD)
    keys[...] = scratch[pl.ds(0, tokens, stride=2), :].astype(bf16)
    values[...] = scratch[pl.ds(1, tokens, stride=2), :].astype(bf16)


def unpack_kernel(
    parents_in,
    table_in,
    lengths_in,
    prefix,
    pool,
    new_kv,
    keys,
    values,
    tail_keys,
    tail_values,
    bias,
    scratch,
    parents,
    table,
    lengths,
    meta_sem,
):
    sources, meta = (parents_in, table_in, lengths_in), (parents, table, lengths)
    first_step = (pl.program_id(0) == 0) & (pl.program_id(1) == 0)

    @pl.when(first_step)
    def _():
        load_meta(sources, meta, meta_sem)

    for head in range(KVH):
        split_kv(prefix.at[0], head, scratch.at[head], keys.at[0, head], values.at[0, head])

    @pl.when(first_step)
    def _():
        for index, (from_ref, to_ref) in enumerate(zip(sources, meta)):
            pltpu.make_async_copy(from_ref, to_ref, meta_sem.at[index]).wait()
        me = lax.axis_index("ctx")
        blocks, block_len = pool.shape[:2]
        tokens = blocks * block_len
        rows = new_kv.shape[0]
        first = tokens - CAP * block_len
        for head in range(KVH):
            for block in range(blocks):
                at = pl.ds(block * block_len, block_len)
                split_kv(
                    pool.at[block],
                    head,
                    scratch.at[head],
                    tail_keys.at[head, at],
                    tail_values.at[head, at],
                )
            at = pl.ds(first, CAP * block_len)
            lanes = slice(head * HD, (head + 1) * HD)
            slot = lax.broadcasted_iota(jnp.int32, (CAP * block_len, HD), 0)
            key = tail_keys[head, at, :]
            value = tail_values[head, at, :]
            for row in range(rows):
                key = jnp.where(slot == row, new_kv[row, 0:1, lanes], key)
                value = jnp.where(slot == row, new_kv[row, 1:2, lanes], value)
            tail_keys[head, at, :] = key
            tail_values[head, at, :] = value

        lane = lax.broadcasted_iota(jnp.int32, (1, tokens), 1)

        def mask(row, carry):
            parent = parents[row]
            length = lengths[parent]
            reach = jnp.zeros((1, tokens), jnp.int32)
            for depth in range(table.shape[0]):
                block = table[depth, parent] - me * blocks
                reach = jnp.where(lane // block_len == block, length - depth * block_len, reach)
            own = row - me * rows
            own = jnp.where((own >= 0) & (own < rows), own + first, -1)
            live = (lane % block_len < reach) | (lane == own)
            bias[pl.ds(row, 1), :] = jnp.where(live, 0.0, masked_score)
            return carry

        lax.fori_loop(0, bias.shape[0], mask, 0)


def unpack(meta, prefix_kv, pool, new_kv, row_total):
    requests, length, _, width = prefix_kv.shape
    blocks, block_len = pool.shape[:2]
    tokens = blocks * block_len
    step = min(256, length)
    hbm = pl.BlockSpec(memory_space=pltpu.HBM)
    whole = lambda shape: pl.BlockSpec(shape, lambda r, i: (0,) * len(shape))
    return pl.pallas_call(
        unpack_kernel,
        name="unpack",
        grid=(requests, length // step),
        in_specs=[hbm] * 3
        + [
            pl.BlockSpec((1, step, 2, width), lambda r, i: (r, i, 0, 0)),
            whole(pool.shape),
            whole(new_kv.shape),
        ],
        out_specs=[pl.BlockSpec((1, KVH, step, HD), lambda r, i: (r, 0, i, 0))] * 2
        + [whole((KVH, tokens, HD))] * 2
        + [whole((row_total, tokens))],
        out_shape=[pltpu.HBM((requests, KVH, length, HD), bf16)] * 2
        + [jax.ShapeDtypeStruct((KVH, tokens, HD), bf16)] * 2
        + [jax.ShapeDtypeStruct((row_total, tokens), f32)],
        scratch_shapes=[pltpu.VMEM((KVH, 2 * step, HD), f32)] + meta_scratch(meta),
        compiler_params=pltpu.CompilerParams(vmem_limit_bytes=VMEM_LIMIT),
        cost_estimate=pl.CostEstimate(
            flops=0, bytes_accessed=4 * prefix_kv.size, transcendentals=0
        ),
    )(*map(in_hbm, meta), in_hbm(prefix_kv), pool, new_kv)


def pieces(value):
    high = value.astype(bf16)
    rest = value - high.astype(f32)
    middle = rest.astype(bf16)
    low = (rest - middle.astype(f32)).astype(bf16)
    return high.astype(f32), middle.astype(f32), low.astype(f32)


def attend_kernel(
    query, keys, values, tail_keys, tail_values, bias, out, wide, stacks, key_buffer, value_buffer, sem
):
    groups = HQ // KVH
    targets = out.shape[0] // KVH
    beams = query.shape[0]
    count = groups * beams
    share = count // targets
    factor = HD ** (-0.5) * math.log2(math.e)
    contract = (((1,), (1,)), ((), ()))
    request = pl.program_id(0)

    def loads(head):
        return (
            pltpu.make_async_copy(keys.at[request, head], key_buffer.at[head], sem.at[0, head]),
            pltpu.make_async_copy(values.at[request, head], value_buffer.at[head], sem.at[1, head]),
        )

    for head in range(KVH):
        for copy in loads(head):
            copy.start()

    wide[...] = query[...].astype(f32).reshape(beams * HQ, HD)
    for head in range(HQ):
        stacks[head * beams : (head + 1) * beams, :] = wide[pl.ds(head, beams, stride=HQ), :].astype(
            bf16
        )
    mask = jnp.concatenate([bias[...]] * groups, axis=0)
    lane = lax.broadcasted_iota(jnp.int32, (count, HD), 1)

    def one(head):
        stacked = stacks[pl.ds(pl.multiple_of(head * count, count), count), :]
        score = lax.dot_general(stacked, key_buffer[head], contract, preferred_element_type=f32)
        tail = lax.dot_general(stacked, tail_keys[head], contract, preferred_element_type=f32)
        tail = tail + mask
        top = jnp.maximum(
            jnp.max(score, axis=1, keepdims=True), jnp.max(tail, axis=1, keepdims=True)
        )
        weight = jnp.exp2((score - top) * factor)
        tail_weight = jnp.exp2((tail - top) * factor)
        total = jnp.sum(weight, axis=1, keepdims=True) + jnp.sum(
            tail_weight, axis=1, keepdims=True
        )
        result = jnp.dot(weight.astype(bf16), value_buffer[head], preferred_element_type=f32)
        result = result + jnp.dot(
            tail_weight.astype(bf16), tail_values[head], preferred_element_type=f32
        )
        packed = jnp.zeros((count, HD), f32)
        for at, term in enumerate(pieces(top) + pieces(total)):
            packed = jnp.where(lane == at, term, packed)
        if count < HD:
            packed = jnp.concatenate([packed, jnp.zeros((HD - count, HD), f32)], axis=0)
        stats = packed.T
        for t in range(targets):
            at = head * targets + t
            out[at, 0, :share, :] = result[t * share : (t + 1) * share].astype(bf16)
            mine = stats if t == 0 else pltpu.roll(stats, HD - t * share, 1)
            out[at, 0, share : share + STAT_ROWS, :] = mine[:STAT_ROWS].astype(bf16)

    def some(step, carry):
        heads = [step * AT_ONCE + i for i in range(AT_ONCE)]
        for head in heads:
            for copy in loads(head):
                copy.wait()
        for head in heads:
            one(head)
        return carry

    lax.fori_loop(0, KVH // AT_ONCE, some, 0)


def attend(everyone, keys, values, tail_keys, tail_values, bias, devices):
    requests, _, length, _ = keys.shape
    tokens = tail_keys.shape[1]
    beams = everyone.shape[0] // requests
    groups = HQ // KVH
    targets = devices // KVH
    rows = groups // targets * beams + STAT_ROWS
    hbm = pl.BlockSpec(memory_space=pltpu.HBM)
    return pl.pallas_call(
        attend_kernel,
        name="attend",
        grid=(requests,),
        in_specs=[
            pl.BlockSpec((beams, HQ, HD), lambda r: (r, 0, 0)),
            hbm,
            hbm,
            pl.BlockSpec((KVH, tokens, HD), lambda r: (0, 0, 0)),
            pl.BlockSpec((KVH, tokens, HD), lambda r: (0, 0, 0)),
            pl.BlockSpec((beams, tokens), lambda r: (r, 0)),
        ],
        out_specs=pl.BlockSpec((devices, 1, rows, HD), lambda r: (0, r, 0, 0)),
        out_shape=jax.ShapeDtypeStruct((devices, requests, rows, HD), bf16),
        scratch_shapes=[
            pltpu.VMEM((beams * HQ, HD), f32),
            pltpu.VMEM((beams * HQ, HD), bf16),
            pltpu.VMEM((KVH, length, HD), bf16),
            pltpu.VMEM((KVH, length, HD), bf16),
            pltpu.SemaphoreType.DMA((2, KVH)),
        ],
        compiler_params=pltpu.CompilerParams(vmem_limit_bytes=VMEM_LIMIT),
        cost_estimate=pl.CostEstimate(
            flops=4 * everyone.size * length,
            bytes_accessed=4 * keys.size,
            transcendentals=everyone.size * length // HD,
        ),
    )(everyone, in_hbm(keys), in_hbm(values), tail_keys, tail_values, bias)


def project_kernel(partial, weight, out, attended, scratch, buffer, sem):
    devices, requests, rows, _ = partial.shape
    share = rows - STAT_ROWS
    row_total = out.shape[0]
    beams = row_total // requests
    own = share // beams
    chunks = out.shape[1]
    parts = sem.shape[0]
    step = weight.shape[1] // parts
    factor = HD ** (-0.5) * math.log2(math.e)

    def load(part):
        lanes = pl.ds(part * step, step)
        return pltpu.make_async_copy(weight.at[:, lanes], buffer.at[part], sem.at[part])

    for part in range(parts):
        load(part).start()

    for r in range(requests):
        stats = [partial[p, r, share:rows, :].astype(f32) for p in range(devices)]
        tops = jnp.concatenate([s[0:1] + s[1:2] + s[2:3] for s in stats], axis=0)
        sums = jnp.concatenate([s[3:4] + s[4:5] + s[5:6] for s in stats], axis=0)
        scale = jnp.exp2((tops - jnp.max(tops, axis=0, keepdims=True)) * factor)
        scale = scale / jnp.sum(scale * sums, axis=0, keepdims=True)
        if devices < HD:
            scale = jnp.concatenate([scale, jnp.zeros((HD - devices, HD), f32)], axis=0)
        scale = scale.T
        total = jnp.zeros((share, HD), f32)
        for p in range(devices):
            total = total + partial[p, r, :share, :].astype(f32) * scale[:share, p : p + 1]
        for h in range(own):
            attended[r * beams : (r + 1) * beams, h * HD : (h + 1) * HD] = total[
                h * beams : (h + 1) * beams
            ].astype(bf16)

    for part in range(parts):
        load(part).wait()
        product = jnp.dot(attended[...], buffer[part], preferred_element_type=f32)
        for c in range(step // HD):
            scratch[pl.ds(part * (step // HD) + c, row_total, stride=chunks), :] = product[
                :, c * HD : (c + 1) * HD
            ]
    for row in range(row_total):
        out[row] = scratch[row * chunks : (row + 1) * chunks, :].astype(bf16)


def project(partial, weight, row_total):
    depth, width = weight.shape
    parts = max(1, width // 1024)
    return pl.pallas_call(
        project_kernel,
        name="project",
        in_specs=[
            pl.BlockSpec(memory_space=pltpu.VMEM),
            pl.BlockSpec(memory_space=pltpu.HBM),
        ],
        out_specs=pl.BlockSpec(memory_space=pltpu.VMEM),
        out_shape=jax.ShapeDtypeStruct((row_total, width // HD, HD), bf16),
        scratch_shapes=[
            pltpu.VMEM((row_total, depth), bf16),
            pltpu.VMEM((row_total * (width // HD), HD), f32),
            pltpu.VMEM((parts, depth, width // parts), bf16),
            pltpu.SemaphoreType.DMA((parts,)),
        ],
        compiler_params=pltpu.CompilerParams(vmem_limit_bytes=VMEM_LIMIT),
        cost_estimate=pl.CostEstimate(
            flops=2 * row_total * depth * width, bytes_accessed=2 * weight.size, transcendentals=0
        ),
    )(partial, in_hbm(weight))


def exchange(array):
    return lax.all_to_all(array, "ctx", split_axis=0, concat_axis=0, tiled=True)


def local(
    queries, new_kv, prefix_kv, pool, out_weight, parents, tail_table, fresh_slots, tail_lengths
):
    devices = lax.axis_size("ctx")
    rows = queries.shape[0]
    row_total = rows * devices
    width = out_weight.shape[1]
    rounds = rounds_of(devices)
    meta = (parents, tail_table.T, tail_lengths)

    def move(index, blocks):
        first, _ = rounds[index]
        return [
            lax.ppermute(block, "ctx", [(i, i ^ ((at + 1) << first)) for i in range(devices)])
            for at, block in enumerate(blocks)
        ]

    wide, *blocks = ask(rounds[0], devices, queries, meta, pool)
    everyone = exchange(wide).reshape(row_total, HQ, HD)
    arrived = move(0, blocks)
    tokens = unpack(meta, prefix_kv, pool, new_kv, row_total)
    for index in range(1, len(rounds)):
        blocks = pick(rounds[:index], rounds[index], devices, rows, meta, pool, arrived)
        arrived = arrived + move(index, blocks)
    partial = attend(everyone, *tokens, devices)
    partial = exchange(partial)
    products = project(partial, out_weight, row_total)
    products = exchange(products.reshape(devices, rows * (width // HD), HD))
    result = jnp.sum(products.astype(f32), axis=0).reshape(rows, width)
    new_pool = place(rounds, rows, meta + (fresh_slots,), new_kv, pool, arrived)
    return (result, new_pool)


def solution(mesh):
    in_specs = (
        P(("req", "ctx"), None),
        P(("req", "ctx"), None, None),
        P("req", "ctx", None, None),
        P(("req", "ctx"), None, None, None),
        P("ctx", None),
        P("req"),
        P("req", None),
        P("req"),
        P("req"),
    )
    out_specs = (P(("req", "ctx"), None), P(("req", "ctx"), None, None, None))
    return jax.shard_map(local, mesh=mesh, in_specs=in_specs, out_specs=out_specs, check_vma=False)
```

time: 85.6 us -> 85.3 us (level)
  blocking collectives: 0 us -> 17.5 us
  local copies, waits for them, and re-layouts: 12.3 us -> 2.48 us
  starting transfers between devices: 27.1 us -> 20 us
  waiting for transfers between devices: 20.4 us -> 18.9 us
    all_to_all x0 -> x1, blocking collectives: none -> 17.5 us  [exchange(): return lax.all_to_all(array, 'ctx', split_axis=0, concat_axis=0, tiled=True)]
    unnamed x27 -> x8, local copies, waits for them, and re-layouts: 12.3 us -> 2.48 us
    all_to_all x3 -> x2, waiting for transfers between devices: 7.05 us -> 0.01 us  [exchange(): return lax.all_to_all(array, 'ctx', split_axis=0, concat_axis=0, tiled=True)]
    all_to_all x3 -> x2, starting transfers between devices: 18.9 us -> 11.9 us  [exchange(): return lax.all_to_all(array, 'ctx', split_axis=0, concat_axis=0, tiled=True)]
    ppermute x4 -> x6, waiting for transfers between devices: 13.3 us -> 18.9 us  [move(): lax.ppermute(block, 'ctx', [(i, i ^ at + 1 << first) for i in range(devic...]
    pallas_call x1, Pallas kernels: 6.25 us -> 8.17 us  [unpack(): pl.pallas_call(unpack_kernel, name='unpack', grid=(requests, length // st...]
    pallas_call x8 -> x5, Pallas kernels: 17.4 us -> 16.1 us  [the longest x1 5.5 us: attend(): pl.pallas_call(attend_kernel, name='attend', grid=(requests,), in_specs=[...]
    ppermute x4 -> x6, starting transfers between devices: 8.22 us -> 8.19 us  [move(): lax.ppermute(block, 'ctx', [(i, i ^ at + 1 << first) for i in range(devic...]
  transfers between devices with their start and end apart: 7 -> 8, of which waited for: 4 -> 6; matrix products, arithmetic and copies ran while one was open for 1% -> 0% of each run, Pallas kernels for 19% -> 14%
where the time goes in v3:
time: 85.3 us; the launch traced here: 84.6 us
  Pallas kernels  24.3 us (28%)
  starting transfers between devices  20 us (23%)
  waiting for transfers between devices  18.9 us (22%)
  blocking collectives  17.5 us (21%)
  local copies, waits for them, and re-layouts  2.48 us (3%)
    ppermute x6, waiting for transfers between devices, move(): lax.ppermute(block, 'ctx', [(i, i ^ at + 1 << first) for i in range(devic...  18.9 us
    all_to_all x1, blocking collectives, exchange(): return lax.all_to_all(array, 'ctx', split_axis=0, concat_axis=0, tiled=True)  17.5 us
    all_to_all x2, starting transfers between devices, exchange(): return lax.all_to_all(array, 'ctx', split_axis=0, concat_axis=0, tiled=True)  11.9 us
    ppermute x6, starting transfers between devices, move(): lax.ppermute(block, 'ctx', [(i, i ^ at + 1 << first) for i in range(devic...  8.19 us
    pallas_call x1, Pallas kernels, unpack(): pl.pallas_call(unpack_kernel, name='unpack', grid=(requests, length // st...  8.17 us
    pallas_call x1, Pallas kernels, attend(): pl.pallas_call(attend_kernel, name='attend', grid=(requests,), in_specs=[...  5.5 us
    pallas_call x1, Pallas kernels, project(): pl.pallas_call(project_kernel, name='project', in_specs=[pl.BlockSpec(mem...  4.5 us
    pallas_call x1, Pallas kernels, ask(): pl.pallas_call(functools.partial(ask_kernel, now), name='ask', in_specs=[...  2.82 us
  transfers between devices with their start and end apart: 8, of which 6 were waited for; matrix products, arithmetic and copies ran while one was open for 0% of the time, Pallas kernels for 14%

profile of v3, /device:TPU:0, one launch (start us, length us, event | category | flops | bytes accessed | tf_op | source)
XLA Modules:
  0.0 84.6 jit_solution(10096692802204807652)
XLA Ops:
  0.6 0.0 copy-start.1
  0.6 0.7 copy-done.1
  1.4 2.8 %ask.1 = (bf16[16,1,64,128]{3,2,1,0:T(8,128)(2,1)}, bf16[4,16,2,1024]{3,2,1,0:T(2,128)(2,1)S(1)}, bf16[4,16,2,1024]{3,2,1,0:T(2,128)(2,1)S(1)}, bf16[4,16,2,1024]{3,2,1,0:T(2,128)(2,1)S(1)}) custom-call(bf16[1,8192]{1,0:T(2,128)(2,1)S(1)} %copy-done.1, s32[16]{0:T(128)} %parents_in.7, s32[4,16]{1,0:T(4,128)} %bitcast.4, s32[16]{0:T(128)} %lengths_in.7, ...), custom_call_target="tpu_custom_call" | custom-call | tf_op jit(solution)/shard_map/ask/pallas_call | solution.py:136
  4.2 8.3 %all-to-all-start = ((bf16[16,1,64,128]{3,2,1,0:T(8,128)(2,1)}), bf16[16,1,64,128]{3,2,1,0:T(8,128)(2,1)S(1)}, u32[]{:S(2)}, u32[]{:S(2)}) async-start(bf16[16,1,64,128]{3,2,1,0:T(8,128)(2,1)} %get-tuple-element.14), calls=%async_computation | async-start | bytes 524288 | tf_op jit(solution)/shard_map/all_to_all | solution.py:526
  12.5 0.0 copy-start
  12.6 1.0 %copy-done = bf16[8,16,2,1024]{3,2,1,0:T(2,128)(2,1)S(1)} copy-done((bf16[8,16,2,1024]{3,2,1,0:T(2,128)(2,1)S(1)}, bf16[8,16,2,1024]{3,2,1,0:T(2,128)(2,1)}, u32[]{:S(2)}) %copy-start) | copy-done | bytes 524312
  13.6 0.0 copy-start.2
  13.6 0.7 copy-done.2
  14.3 8.2 %unpack.1 = (bf16[1,8,1024,128]{3,2,1,0:T(8,128)(2,1)}, bf16[1,8,1024,128]{3,2,1,0:T(8,128)(2,1)}, bf16[8,128,128]{2,1,0:T(8,128)(2,1)S(1)}, bf16[8,128,128]{2,1,0:T(8,128)(2,1)S(1)}, f32[16,128]{1,0:T(8,128)S(1)}) custom-call(s32[16]{0:T(128)} %parents_in.7, s32[4,16]{1,0:T(4,128)} %bitcast.5, s32[16]{0:T(128)} %lengths_in.7, ...), custom_call_target="tpu_custom_call" | custom-call | bytes 8388608 | tf_op jit(solution)/shard_map/unpack/pallas_call | solution.py:313
  22.5 0.0 all-to-all-done
  22.5 5.5 %attend.1 = bf16[16,1,80,128]{3,2,1,0:T(8,128)(2,1)S(1)} custom-call(bf16[16,64,128]{2,1,0:T(8,128)(2,1)S(1)} %bitcast.3, bf16[1,8,1024,128]{3,2,1,0:T(8,128)(2,1)} %get-tuple-element.15.keys, bf16[1,8,1024,128]{3,2,1,0:T(8,128)(2,1)} %get-tuple-element.16.values, bf16[8,128,128]{2,1,0:T(8,128)(2,1)S(1)} %get-tuple-element.17.tail_keys, ...), custom_call_target="tpu_custom_call" | custom-call | flops 536870912 | bytes 4194304 | tf_op jit(solution)/shard_map/attend/pallas_call | solution.py:424
  28.0 17.5 %all_to_all.15.partial = bf16[16,1,80,128]{3,2,1,0:T(8,128)(2,1)S(1)} all-to-all(bf16[16,1,80,128]{3,2,1,0:T(8,128)(2,1)S(1)} %attend.1), channel_id=1, replica_groups=mesh['req'=2,'ctx'=16] {'ctx'}, dimensions={0} | all-to-all | bytes 655360 | tf_op jit(solution)/shard_map/all_to_all | solution.py:526
  45.5 0.0 copy-start.3
  45.5 4.5 %project.1 = bf16[16,64,128]{2,1,0:T(8,128)(2,1)} custom-call(bf16[16,1,80,128]{3,2,1,0:T(8,128)(2,1)S(1)} %all_to_all.15.partial, bf16[512,8192]{1,0:T(8,128)(2,1)} %weight.1), custom_call_target="tpu_custom_call" | custom-call | flops 134217728 | bytes 8388608 | tf_op jit(solution)/shard_map/project/pallas_call | solution.py:503
  50.0 3.5 %all-to-all-start.2 = ((bf16[16,64,128]{2,1,0:T(8,128)(2,1)}), bf16[16,64,128]{2,1,0:T(8,128)(2,1)S(1)}, u32[]{:S(2)}, u32[]{:S(2)}) async-start(bf16[16,64,128]{2,1,0:T(8,128)(2,1)} %project.1), calls=%async_computation.2 | async-start | bytes 524288 | tf_op jit(solution)/shard_map/all_to_all | solution.py:526
  53.5 1.9 %collective-permute-start = (bf16[4,16,2,1024]{3,2,1,0:T(2,128)(2,1)S(1)}, bf16[4,16,2,1024]{3,2,1,0:T(2,128)(2,1)S(1)}, u32[]{:S(2)}, u32[]{:S(2)}) collective-permute-start(bf16[4,16,2,1024]{3,2,1,0:T(2,128)(2,1)S(1)} %get-tuple-element.20), channel_id=1, source_target_pairs={{0,1},{1,0},{2,3},{3,2},{4,5},{5,4},{6,7},{7,6},{8,9},{9,8},{10,11... | collective-permute-start | bytes 786440 | tf_op jit(solution)/shard_map/ppermute | solution.py:542
  55.4 1.5 %collective-permute-start.1 = (bf16[4,16,2,1024]{3,2,1,0:T(2,128)(2,1)S(1)}, bf16[4,16,2,1024]{3,2,1,0:T(2,128)(2,1)S(1)}, u32[]{:S(2)}, u32[]{:S(2)}) collective-permute-start(bf16[4,16,2,1024]{3,2,1,0:T(2,128)(2,1)S(1)} %get-tuple-element.21), channel_id=1, source_target_pairs={{0,2},{1,3},{2,0},{3,1},{4,6},{5,7},{6,4},{7,5},{8,10},{9,11},{10,... | collective-permute-start | bytes 786440 | tf_op jit(solution)/shard_map/ppermute | solution.py:542
  56.9 0.2 collective-permute-start.2
  57.1 8.2 %collective-permute-done.refs_0_ = bf16[4,16,2,1024]{3,2,1,0:T(2,128)(2,1)S(1)} collective-permute-done((bf16[4,16,2,1024]{3,2,1,0:T(2,128)(2,1)S(1)}, bf16[4,16,2,1024]{3,2,1,0:T(2,128)(2,1)S(1)}, u32[]{:S(2)}, u32[]{:S(2)}) %collective-permute-start) | collective-permute-done | bytes 262176 | tf_op jit(solution)/shard_map/ppermute | solution.py:542
  65.2 3.1 %collective-permute-done.1.refs_1_ = bf16[4,16,2,1024]{3,2,1,0:T(2,128)(2,1)S(1)} collective-permute-done((bf16[4,16,2,1024]{3,2,1,0:T(2,128)(2,1)S(1)}, bf16[4,16,2,1024]{3,2,1,0:T(2,128)(2,1)S(1)}, u32[]{:S(2)}, u32[]{:S(2)}) %collective-permute-start.1) | collective-permute-done | bytes 262176 | tf_op jit(solution)/shard_map/ppermute | solution.py:542
  68.4 1.5 %collective-permute-done.2.refs_2_ = bf16[4,16,2,1024]{3,2,1,0:T(2,128)(2,1)S(1)} collective-permute-done((bf16[4,16,2,1024]{3,2,1,0:T(2,128)(2,1)S(1)}, bf16[4,16,2,1024]{3,2,1,0:T(2,128)(2,1)S(1)}, u32[]{:S(2)}, u32[]{:S(2)}) %collective-permute-start.2) | collective-permute-done | bytes 262176 | tf_op jit(solution)/shard_map/ppermute | solution.py:542
  69.9 1.1 %pick.1 = (bf16[1,16,2,1024]{3,2,1,0:T(2,128)(2,1)S(1)}, bf16[1,16,2,1024]{3,2,1,0:T(2,128)(2,1)S(1)}, bf16[1,16,2,1024]{3,2,1,0:T(2,128)(2,1)S(1)}) custom-call(s32[16]{0:T(128)} %parents_in.7, s32[4,16]{1,0:T(4,128)} %bitcast.6, s32[16]{0:T(128)} %lengths_in.7, bf16[8,16,2,1024]{3,2,1,0:T(2,128)(2,1)} %pool.7, ...), custom_call_target="tpu_custom_call" | custom-call | bytes 4194304 | tf_op jit(solution)/shard_map/pick/pallas_call | solution.py:163
  71.0 2.0 %collective-permute-start.3 = (bf16[1,16,2,1024]{3,2,1,0:T(2,128)(2,1)S(1)}, bf16[1,16,2,1024]{3,2,1,0:T(2,128)(2,1)S(1)}, u32[]{:S(2)}, u32[]{:S(2)}) collective-permute-start(bf16[1,16,2,1024]{3,2,1,0:T(2,128)(2,1)S(1)} %get-tuple-element.23), channel_id=1, source_target_pairs={{0,4},{1,5},{2,6},{3,7},{4,0},{5,1},{6,2},{7,3},{8,12},{9,13},{10,... | collective-permute-start | bytes 196616 | tf_op jit(solution)/shard_map/ppermute | solution.py:542
  73.0 2.6 %collective-permute-start.4 = (bf16[1,16,2,1024]{3,2,1,0:T(2,128)(2,1)S(1)}, bf16[1,16,2,1024]{3,2,1,0:T(2,128)(2,1)S(1)}, u32[]{:S(2)}, u32[]{:S(2)}) collective-permute-start(bf16[1,16,2,1024]{3,2,1,0:T(2,128)(2,1)S(1)} %get-tuple-element.24), channel_id=1, source_target_pairs={{0,8},{1,9},{2,10},{3,11},{4,12},{5,13},{6,14},{7,15},{8,0},{9,1},... | collective-permute-start | bytes 196616 | tf_op jit(solution)/shard_map/ppermute | solution.py:542
  75.7 0.0 collective-permute-start.5
  75.7 0.4 collective-permute-done.3.refs_3_
  76.1 3.6 %collective-permute-done.4.refs_4_ = bf16[1,16,2,1024]{3,2,1,0:T(2,128)(2,1)S(1)} collective-permute-done((bf16[1,16,2,1024]{3,2,1,0:T(2,128)(2,1)S(1)}, bf16[1,16,2,1024]{3,2,1,0:T(2,128)(2,1)S(1)}, u32[]{:S(2)}, u32[]{:S(2)}) %collective-permute-start.4) | collective-permute-done | bytes 65568 | tf_op jit(solution)/shard_map/ppermute | solution.py:542
  79.6 2.1 %collective-permute-done.5.refs_5_ = bf16[1,16,2,1024]{3,2,1,0:T(2,128)(2,1)S(1)} collective-permute-done((bf16[1,16,2,1024]{3,2,1,0:T(2,128)(2,1)S(1)}, bf16[1,16,2,1024]{3,2,1,0:T(2,128)(2,1)S(1)}, u32[]{:S(2)}, u32[]{:S(2)}) %collective-permute-start.5) | collective-permute-done | bytes 65568 | tf_op jit(solution)/shard_map/ppermute | solution.py:542
  81.7 0.0 copy-done.3
  81.7 2.2 %place.1 = bf16[8,16,2,1024]{3,2,1,0:T(2,128)(2,1)} custom-call(s32[16]{0:T(128)} %parents_in.7, s32[4,16]{1,0:T(4,128)} %bitcast.7, s32[16]{0:T(128)} %lengths_in.7, s32[16]{0:T(128)} %fresh_in.1, bf16[1,2,1024]{2,1,0:T(2,128)(2,1)S(1)} %copy-done.3, bf16[8,16,2,1024]{3,2,1,0:T(2,128)(2,1)} %pool.7, ...), custom_call_target="tpu_custom_call" | custom-call | bytes 1048576 | tf_op jit(solution)/shard_map/place/pallas_call | solution.py:210
  83.9 0.0 all-to-all-done.2
  83.9 0.7 convert_reduce_fusion
Async XLA Ops:
  0.6 0.8 copy-start.1
  4.2 18.2 %all-to-all-start = ((bf16[16,1,64,128]{3,2,1,0:T(8,128)(2,1)}), bf16[16,1,64,128]{3,2,1,0:T(8,128)(2,1)S(1)}, u32[]{:S(2)}, u32[]{:S(2)}) async-start(bf16[16,1,64,128]{3,2,1,0:T(8,128)(2,1)} %get-tuple-element.14), calls=%async_computation | async-start | bytes 524288 | tf_op jit(solution)/shard_map/all_to_all | solution.py:526
  12.5 1.0 %copy-start = (bf16[8,16,2,1024]{3,2,1,0:T(2,128)(2,1)S(1)}, bf16[8,16,2,1024]{3,2,1,0:T(2,128)(2,1)}, u32[]{:S(2)}) copy-start(bf16[8,16,2,1024]{3,2,1,0:T(2,128)(2,1)} %pool.7) | copy-start | bytes 1572868
  13.6 0.7 copy-start.2
  45.5 36.3 %copy-start.3 = (bf16[1,2,1024]{2,1,0:T(2,128)(2,1)S(1)}, bf16[1,2,1024]{2,1,0:T(2,128)(2,1)}, u32[]{:S(2)}) copy-start(bf16[1,2,1024]{2,1,0:T(2,128)(2,1)} %new_kv.3) | copy-start | bytes 12292
  50.0 33.9 %all-to-all-start.2 = ((bf16[16,64,128]{2,1,0:T(8,128)(2,1)}), bf16[16,64,128]{2,1,0:T(8,128)(2,1)S(1)}, u32[]{:S(2)}, u32[]{:S(2)}) async-start(bf16[16,64,128]{2,1,0:T(8,128)(2,1)} %project.1), calls=%async_computation.2 | async-start | bytes 524288 | tf_op jit(solution)/shard_map/all_to_all | solution.py:526
  53.5 11.7 %collective-permute-start = (bf16[4,16,2,1024]{3,2,1,0:T(2,128)(2,1)S(1)}, bf16[4,16,2,1024]{3,2,1,0:T(2,128)(2,1)S(1)}, u32[]{:S(2)}, u32[]{:S(2)}) collective-permute-start(bf16[4,16,2,1024]{3,2,1,0:T(2,128)(2,1)S(1)} %get-tuple-element.20), channel_id=1, source_target_pairs={{0,1},{1,0},{2,3},{3,2},{4,5},{5,4},{6,7},{7,6},{8,9},{9,8},{10,11... | collective-permute-start | bytes 786440 | tf_op jit(solution)/shard_map/ppermute | solution.py:542
  55.4 13.0 %collective-permute-start.1 = (bf16[4,16,2,1024]{3,2,1,0:T(2,128)(2,1)S(1)}, bf16[4,16,2,1024]{3,2,1,0:T(2,128)(2,1)S(1)}, u32[]{:S(2)}, u32[]{:S(2)}) collective-permute-start(bf16[4,16,2,1024]{3,2,1,0:T(2,128)(2,1)S(1)} %get-tuple-element.21), channel_id=1, source_target_pairs={{0,2},{1,3},{2,0},{3,1},{4,6},{5,7},{6,4},{7,5},{8,10},{9,11},{10,... | collective-permute-start | bytes 786440 | tf_op jit(solution)/shard_map/ppermute | solution.py:542
  56.9 13.0 %collective-permute-start.2 = (bf16[4,16,2,1024]{3,2,1,0:T(2,128)(2,1)S(1)}, bf16[4,16,2,1024]{3,2,1,0:T(2,128)(2,1)S(1)}, u32[]{:S(2)}, u32[]{:S(2)}) collective-permute-start(bf16[4,16,2,1024]{3,2,1,0:T(2,128)(2,1)S(1)} %get-tuple-element.22), channel_id=1, source_target_pairs={{0,3},{1,2},{2,1},{3,0},{4,7},{5,6},{6,5},{7,4},{8,11},{9,10},{10,... | collective-permute-start | bytes 786440 | tf_op jit(solution)/shard_map/ppermute | solution.py:542
  71.0 5.0 %collective-permute-start.3 = (bf16[1,16,2,1024]{3,2,1,0:T(2,128)(2,1)S(1)}, bf16[1,16,2,1024]{3,2,1,0:T(2,128)(2,1)S(1)}, u32[]{:S(2)}, u32[]{:S(2)}) collective-permute-start(bf16[1,16,2,1024]{3,2,1,0:T(2,128)(2,1)S(1)} %get-tuple-element.23), channel_id=1, source_target_pairs={{0,4},{1,5},{2,6},{3,7},{4,0},{5,1},{6,2},{7,3},{8,12},{9,13},{10,... | collective-permute-start | bytes 196616 | tf_op jit(solution)/shard_map/ppermute | solution.py:542
  73.0 6.6 %collective-permute-start.4 = (bf16[1,16,2,1024]{3,2,1,0:T(2,128)(2,1)S(1)}, bf16[1,16,2,1024]{3,2,1,0:T(2,128)(2,1)S(1)}, u32[]{:S(2)}, u32[]{:S(2)}) collective-permute-start(bf16[1,16,2,1024]{3,2,1,0:T(2,128)(2,1)S(1)} %get-tuple-element.24), channel_id=1, source_target_pairs={{0,8},{1,9},{2,10},{3,11},{4,12},{5,13},{6,14},{7,15},{8,0},{9,1},... | collective-permute-start | bytes 196616 | tf_op jit(solution)/shard_map/ppermute | solution.py:542
  75.7 6.1 %collective-permute-start.5 = (bf16[1,16,2,1024]{3,2,1,0:T(2,128)(2,1)S(1)}, bf16[1,16,2,1024]{3,2,1,0:T(2,128)(2,1)S(1)}, u32[]{:S(2)}, u32[]{:S(2)}) collective-permute-start(bf16[1,16,2,1024]{3,2,1,0:T(2,128)(2,1)S(1)} %get-tuple-element.25), channel_id=1, source_target_pairs={{0,12},{1,13},{2,14},{3,15},{4,8},{5,9},{6,10},{7,11},{8,4},{9,5},... | collective-permute-start | bytes 196616 | tf_op jit(solution)/shard_map/ppermute | solution.py:542

commit v4 on v3

--- a/solution.py
+++ b/solution.py
@@ -14,7 +14,7 @@
 HD = 128
 CAP = 2
 
-STAT_ROWS = 16
+STAT_ROWS = 8
 AT_ONCE = 2
 VMEM_LIMIT = 20 << 20
 masked_score = -1e30
@@ -28,7 +28,7 @@
 
 def rounds_of(devices):
     total = devices.bit_length() - 1
-    return [(bit, min(2, total - bit)) for bit in range(0, total, 2)]
+    return [(0, 2)] + [(bit, 1) for bit in range(2, total)]
 
 
 def channels_of(rounds):
@@ -98,27 +98,30 @@
         lax.fori_loop(0, out.shape[0], finish, 0)
 
 
-def ask_kernel(now, query, parents_in, table_in, lengths_in, pool, out, *refs):
+def ask_kernel(query, out, wide):
     devices, rows = out.shape[:2]
-    partners = (1 << now[1]) - 1
-    outs, (wide, parents, table, lengths, meta_sem, sem) = refs[:partners], refs[partners:]
-    me = lax.axis_index("ctx")
-    meta = (parents, table, lengths)
-    copies = load_meta((parents_in, table_in, lengths_in), meta, meta_sem)
     heads = query.shape[1] // HD
     for row in range(rows):
         for head in range(heads):
-            wide[row, head : head + 1, :] = query[
-                row : row + 1, head * HD : (head + 1) * HD
-            ].astype(f32)
-    for copy in copies:
-        copy.wait()
-    begin_picks([], now, rows, me, meta, pool, [], outs, sem)
-    for row in range(rows):
-        value = wide[row].astype(bf16)
+            wide[head : head + 1, :] = query[row : row + 1, head * HD : (head + 1) * HD].astype(f32)
+        value = wide[...].astype(bf16)
         for device in range(devices):
             out[device, row] = value
-    end_picks(pool, outs, sem)
+
+
+def ask(queries, devices):
+    rows, width = queries.shape
+    heads = width // HD
+    vmem = pl.BlockSpec(memory_space=pltpu.VMEM)
+    return pl.pallas_call(
+        ask_kernel,
+        name="ask",
+        in_specs=[vmem],
+        out_specs=vmem,
+        out_shape=jax.ShapeDtypeStruct((devices, rows, heads, HD), bf16),
+        scratch_shapes=[pltpu.VMEM((heads, HD), f32)],
+        compiler_params=pltpu.CompilerParams(vmem_limit_bytes=VMEM_LIMIT),
+    )(queries)
 
 
 def pick_shapes(now, devices, rows, pool):
@@ -126,24 +129,6 @@
     count = (devices >> (first + bits)) * rows
     partners = (1 << bits) - 1
     return [jax.ShapeDtypeStruct((count,) + pool.shape[1:], bf16)] * partners, (partners, count)
-
-
-def ask(now, devices, queries, meta, pool):
-    rows, width = queries.shape
-    heads = width // HD
-    shapes, semaphores = pick_shapes(now, devices, rows, pool)
-    vmem, hbm = pl.BlockSpec(memory_space=pltpu.VMEM), pl.BlockSpec(memory_space=pltpu.HBM)
-    return pl.pallas_call(
-        functools.partial(ask_kernel, now),
-        name="ask",
-        in_specs=[vmem] + [hbm] * 4,
-        out_specs=[vmem] * (1 + len(shapes)),
-        out_shape=[jax.ShapeDtypeStruct((devices, rows, heads, HD), bf16)] + shapes,
-        scratch_shapes=[pltpu.VMEM((rows, heads, HD), f32)]
-        + meta_scratch(meta)
-        + [pltpu.SemaphoreType.DMA(semaphores)],
-        compiler_params=pltpu.CompilerParams(vmem_limit_bytes=VMEM_LIMIT),
-    )(queries, *map(in_hbm, meta), in_hbm(pool))
 
 
 def pick_kernel(rounds, now, rows, channels, parents_in, table_in, lengths_in, pool, *refs):
@@ -219,131 +204,34 @@
     )(*map(in_hbm, meta), new_kv, in_hbm(pool), *arrived)
 
 
-def split_kv(source, head, scratch, keys, values):
-    tokens = source.shape[0]
-    pairs = source[:, :, head * HD : (head + 1) * HD].astype(f32)
-    scratch[: 2 * tokens, :] = pairs.reshape(2 * tokens, HD)
-    keys[...] = scratch[pl.ds(0, tokens, stride=2), :].astype(bf16)
-    values[...] = scratch[pl.ds(1, tokens, stride=2), :].astype(bf16)
-
-
-def unpack_kernel(
+def pieces(value):
+    high = value.astype(bf16)
+    rest = value - high.astype(f32)
+    middle = rest.astype(bf16)
+    low = (rest - middle.astype(f32)).astype(bf16)
+    return high.astype(f32), middle.astype(f32), low.astype(f32)
+
+
+def attend_kernel(
+    rows,
+    query,
     parents_in,
     table_in,
     lengths_in,
     prefix,
     pool,
     new_kv,
-    keys,
-    values,
-    tail_keys,
-    tail_values,
+    out,
+    wide,
+    stacks,
     bias,
-    scratch,
+    raw,
+    pairs,
+    sem,
     parents,
     table,
     lengths,
     meta_sem,
-):
-    sources, meta = (parents_in, table_in, lengths_in), (parents, table, lengths)
-    first_step = (pl.program_id(0) == 0) & (pl.program_id(1) == 0)
-
-    @pl.when(first_step)
-    def _():
-        load_meta(sources, meta, meta_sem)
-
-    for head in range(KVH):
-        split_kv(prefix.at[0], head, scratch.at[head], keys.at[0, head], values.at[0, head])
-
-    @pl.when(first_step)
-    def _():
-        for index, (from_ref, to_ref) in enumerate(zip(sources, meta)):
-            pltpu.make_async_copy(from_ref, to_ref, meta_sem.at[index]).wait()
-        me = lax.axis_index("ctx")
-        blocks, block_len = pool.shape[:2]
-        tokens = blocks * block_len
-        rows = new_kv.shape[0]
-        first = tokens - CAP * block_len
-        for head in range(KVH):
-            for block in range(blocks):
-                at = pl.ds(block * block_len, block_len)
-                split_kv(
-                    pool.at[block],
-                    head,
-                    scratch.at[head],
-                    tail_keys.at[head, at],
-                    tail_values.at[head, at],
-                )
-            at = pl.ds(first, CAP * block_len)
-            lanes = slice(head * HD, (head + 1) * HD)
-            slot = lax.broadcasted_iota(jnp.int32, (CAP * block_len, HD), 0)
-            key = tail_keys[head, at, :]
-            value = tail_values[head, at, :]
-            for row in range(rows):
-                key = jnp.where(slot == row, new_kv[row, 0:1, lanes], key)
-                value = jnp.where(slot == row, new_kv[row, 1:2, lanes], value)
-            tail_keys[head, at, :] = key
-            tail_values[head, at, :] = value
-
-        lane = lax.broadcasted_iota(jnp.int32, (1, tokens), 1)
-
-        def mask(row, carry):
-            parent = parents[row]
-            length = lengths[parent]
-            reach = jnp.zeros((1, tokens), jnp.int32)
-            for depth in range(table.shape[0]):
-                block = table[depth, parent] - me * blocks
-                reach = jnp.where(lane // block_len == block, length - depth * block_len, reach)
-            own = row - me * rows
-            own = jnp.where((own >= 0) & (own < rows), own + first, -1)
-            live = (lane % block_len < reach) | (lane == own)
-            bias[pl.ds(row, 1), :] = jnp.where(live, 0.0, masked_score)
-            return carry
-
-        lax.fori_loop(0, bias.shape[0], mask, 0)
-
-
-def unpack(meta, prefix_kv, pool, new_kv, row_total):
-    requests, length, _, width = prefix_kv.shape
-    blocks, block_len = pool.shape[:2]
-    tokens = blocks * block_len
-    step = min(256, length)
-    hbm = pl.BlockSpec(memory_space=pltpu.HBM)
-    whole = lambda shape: pl.BlockSpec(shape, lambda r, i: (0,) * len(shape))
-    return pl.pallas_call(
-        unpack_kernel,
-        name="unpack",
-        grid=(requests, length // step),
-        in_specs=[hbm] * 3
-        + [
-            pl.BlockSpec((1, step, 2, width), lambda r, i: (r, i, 0, 0)),
-            whole(pool.shape),
-            whole(new_kv.shape),
-        ],
-        out_specs=[pl.BlockSpec((1, KVH, step, HD), lambda r, i: (r, 0, i, 0))] * 2
-        + [whole((KVH, tokens, HD))] * 2
-        + [whole((row_total, tokens))],
-        out_shape=[pltpu.HBM((requests, KVH, length, HD), bf16)] * 2
-        + [jax.ShapeDtypeStruct((KVH, tokens, HD), bf16)] * 2
-        + [jax.ShapeDtypeStruct((row_total, tokens), f32)],
-        scratch_shapes=[pltpu.VMEM((KVH, 2 * step, HD), f32)] + meta_scratch(meta),
-        compiler_params=pltpu.CompilerParams(vmem_limit_bytes=VMEM_LIMIT),
-        cost_estimate=pl.CostEstimate(
-            flops=0, bytes_accessed=4 * prefix_kv.size, transcendentals=0
-        ),
-    )(*map(in_hbm, meta), in_hbm(prefix_kv), pool, new_kv)
-
-
-def pieces(value):
-    high = value.astype(bf16)
-    rest = value - high.astype(f32)
-    middle = rest.astype(bf16)
-    low = (rest - middle.astype(f32)).astype(bf16)
-    return high.astype(f32), middle.astype(f32), low.astype(f32)
-
-
-def attend_kernel(
-    query, keys, values, tail_keys, tail_values, bias, out, wide, stacks, key_buffer, value_buffer, sem
 ):
     groups = HQ // KVH
     targets = out.shape[0] // KVH
@@ -353,13 +241,30 @@
     factor = HD ** (-0.5) * math.log2(math.e)
     contract = (((1,), (1,)), ((), ()))
     request = pl.program_id(0)
+    length = prefix.shape[1]
+    blocks, block_len = pool.shape[:2]
+    tokens = blocks * block_len
+    old = tokens - CAP * block_len
+    me = lax.axis_index("ctx")
 
     def loads(head):
-        return (
-            pltpu.make_async_copy(keys.at[request, head], key_buffer.at[head], sem.at[0, head]),
-            pltpu.make_async_copy(values.at[request, head], value_buffer.at[head], sem.at[1, head]),
-        )
-
+        lanes = pl.ds(pl.multiple_of(head * HD, HD), HD)
+        flat = pool.reshape(tokens, 2, pool.shape[3])
+        spans = [
+            (prefix.at[request, :, :, lanes], 0, length),
+            (flat.at[pl.ds(0, old), :, lanes], length, old),
+            (new_kv.at[:, :, lanes], length + old, rows),
+            (flat.at[pl.ds(old + rows, tokens - old - rows), :, lanes], length + old + rows, 0),
+        ]
+        return [
+            pltpu.make_async_copy(
+                source, raw.at[head, pl.ds(first, source.shape[0])], sem.at[index, head]
+            )
+            for index, (source, first, _) in enumerate(spans)
+        ]
+
+    sources = (parents_in, table_in, lengths_in)
+    copies = load_meta(sources, (parents, table, lengths), meta_sem)
     for head in range(KVH):
         for copy in loads(head):
             copy.start()
@@ -369,14 +274,35 @@
         stacks[head * beams : (head + 1) * beams, :] = wide[pl.ds(head, beams, stride=HQ), :].astype(
             bf16
         )
-    mask = jnp.concatenate([bias[...]] * groups, axis=0)
+    for copy in copies:
+        copy.wait()
+    position = lax.broadcasted_iota(jnp.int32, (1, tokens), 1)
+    in_block, at_block = position % block_len, position // block_len
+
+    for beam in range(beams):
+        row = request * beams + beam
+        parent = parents[row]
+        tail = lengths[parent]
+        reach = jnp.zeros((1, tokens), jnp.int32)
+        for depth in range(table.shape[0]):
+            block = table[depth, parent] - me * blocks
+            reach = jnp.where(at_block == block, tail - depth * block_len, reach)
+        own = row - me * rows
+        own = jnp.where((own >= 0) & (own < rows), own + old, -1)
+        live = (in_block < reach) | (position == own)
+        bias[beam : beam + 1, :] = jnp.where(live, 0.0, masked_score)
+
     lane = lax.broadcasted_iota(jnp.int32, (count, HD), 1)
 
-    def one(head):
+    def one(head, slot):
         stacked = stacks[pl.ds(pl.multiple_of(head * count, count), count), :]
-        score = lax.dot_general(stacked, key_buffer[head], contract, preferred_element_type=f32)
-        tail = lax.dot_general(stacked, tail_keys[head], contract, preferred_element_type=f32)
-        tail = tail + mask
+        total_len = length + tokens
+        pairs[slot] = raw.at[head].reshape(2 * total_len, HD)[...].astype(f32)
+        keys = pairs[slot, pl.ds(0, total_len, stride=2), :].astype(bf16)
+        values = pairs[slot, pl.ds(1, total_len, stride=2), :].astype(bf16)
+        score = lax.dot_general(stacked, keys, contract, preferred_element_type=f32)
+        tail = score[:, length:] + jnp.concatenate([bias[...]] * groups, axis=0)
+        score = score[:, :length]
         top = jnp.maximum(
             jnp.max(score, axis=1, keepdims=True), jnp.max(tail, axis=1, keepdims=True)
         )
@@ -385,10 +311,8 @@
         total = jnp.sum(weight, axis=1, keepdims=True) + jnp.sum(
             tail_weight, axis=1, keepdims=True
         )
-        result = jnp.dot(weight.astype(bf16), value_buffer[head], preferred_element_type=f32)
-        result = result + jnp.dot(
-            tail_weight.astype(bf16), tail_values[head], preferred_element_type=f32
-        )
+        weight = jnp.concatenate([weight.astype(bf16), tail_weight.astype(bf16)], axis=1)
+        result = jnp.dot(weight, values, preferred_element_type=f32)
         packed = jnp.zeros((count, HD), f32)
         for at, term in enumerate(pieces(top) + pieces(total)):
             packed = jnp.where(lane == at, term, packed)
@@ -406,49 +330,44 @@
         for head in heads:
             for copy in loads(head):
                 copy.wait()
-        for head in heads:
-            one(head)
+        for slot, head in enumerate(heads):
+            one(head, slot)
         return carry
 
     lax.fori_loop(0, KVH // AT_ONCE, some, 0)
 
 
-def attend(everyone, keys, values, tail_keys, tail_values, bias, devices):
-    requests, _, length, _ = keys.shape
-    tokens = tail_keys.shape[1]
+def attend(everyone, meta, prefix_kv, pool, new_kv, devices):
+    requests, length = prefix_kv.shape[:2]
+    tokens = pool.shape[0] * pool.shape[1]
     beams = everyone.shape[0] // requests
     groups = HQ // KVH
     targets = devices // KVH
     rows = groups // targets * beams + STAT_ROWS
     hbm = pl.BlockSpec(memory_space=pltpu.HBM)
     return pl.pallas_call(
-        attend_kernel,
+        functools.partial(attend_kernel, new_kv.shape[0]),
         name="attend",
         grid=(requests,),
-        in_specs=[
-            pl.BlockSpec((beams, HQ, HD), lambda r: (r, 0, 0)),
-            hbm,
-            hbm,
-            pl.BlockSpec((KVH, tokens, HD), lambda r: (0, 0, 0)),
-            pl.BlockSpec((KVH, tokens, HD), lambda r: (0, 0, 0)),
-            pl.BlockSpec((beams, tokens), lambda r: (r, 0)),
-        ],
+        in_specs=[pl.BlockSpec((beams, HQ, HD), lambda r: (r, 0, 0))] + [hbm] * 6,
         out_specs=pl.BlockSpec((devices, 1, rows, HD), lambda r: (0, r, 0, 0)),
         out_shape=jax.ShapeDtypeStruct((devices, requests, rows, HD), bf16),
         scratch_shapes=[
             pltpu.VMEM((beams * HQ, HD), f32),
             pltpu.VMEM((beams * HQ, HD), bf16),
-            pltpu.VMEM((KVH, length, HD), bf16),
-            pltpu.VMEM((KVH, length, HD), bf16),
-            pltpu.SemaphoreType.DMA((2, KVH)),
-        ],
+            pltpu.VMEM((beams, tokens), f32),
+            pltpu.VMEM((KVH, length + tokens, 2, HD), bf16),
+            pltpu.VMEM((AT_ONCE, 2 * (length + tokens), HD), f32),
+            pltpu.SemaphoreType.DMA((4, KVH)),
+        ]
+        + meta_scratch(meta),
         compiler_params=pltpu.CompilerParams(vmem_limit_bytes=VMEM_LIMIT),
         cost_estimate=pl.CostEstimate(
             flops=4 * everyone.size * length,
-            bytes_accessed=4 * keys.size,
+            bytes_accessed=2 * prefix_kv.size,
             transcendentals=everyone.size * length // HD,
         ),
-    )(everyone, in_hbm(keys), in_hbm(values), tail_keys, tail_values, bias)
+    )(everyone, *map(in_hbm, meta), in_hbm(prefix_kv), in_hbm(pool), in_hbm(new_kv))
 
 
 def project_kernel(partial, weight, out, attended, scratch, buffer, sem):
@@ -543,14 +462,13 @@
             for at, block in enumerate(blocks)
         ]
 
-    wide, *blocks = ask(rounds[0], devices, queries, meta, pool)
+    wide = ask(queries, devices)
     everyone = exchange(wide).reshape(row_total, HQ, HD)
-    arrived = move(0, blocks)
-    tokens = unpack(meta, prefix_kv, pool, new_kv, row_total)
-    for index in range(1, len(rounds)):
+    arrived = []
+    for index in range(len(rounds)):
         blocks = pick(rounds[:index], rounds[index], devices, rows, meta, pool, arrived)
         arrived = arrived + move(index, blocks)
-    partial = attend(everyone, *tokens, devices)
+    partial = attend(everyone, meta, prefix_kv, pool, new_kv, devices)
     partial = exchange(partial)
     products = project(partial, out_weight, row_total)
     products = exchange(products.reshape(devices, rows * (width // HD), HD))

time: 85.3 us -> 83.5 us (0.979)
  blocking collectives: 17.5 us -> 31.4 us
  starting transfers between devices: 20 us -> 12.2 us
  Pallas kernels: 24.3 us -> 19.8 us
  local copies, waits for them, and re-layouts: 2.48 us -> 0.75 us
  waiting for transfers between devices: 18.9 us -> 17.4 us
    all_to_all x1 -> x2, blocking collectives: 17.5 us -> 31.4 us  [exchange(): return lax.all_to_all(array, 'ctx', split_axis=0, concat_axis=0, tiled=True)]
    all_to_all x2 -> x1, starting transfers between devices: 11.9 us -> 3.54 us  [exchange(): return lax.all_to_all(array, 'ctx', split_axis=0, concat_axis=0, tiled=True)]
    pallas_call x3 -> x2, Pallas kernels: 16.5 us -> 9.12 us  [the longest x1 9.08 us: attend(): pl.pallas_call(functools.partial(attend_kernel, new_kv.shape[0]), name='a...]
    pallas_call x1 -> x3, Pallas kernels: 1.14 us -> 4.03 us  [pick(): pl.pallas_call(functools.partial(pick_kernel, rounds, now, rows, len(arri...]
    unnamed x8 -> x4, local copies, waits for them, and re-layouts: 2.48 us -> 0.75 us
    ppermute x6 -> x5, waiting for transfers between devices: 18.9 us -> 17.4 us  [move(): lax.ppermute(block, 'ctx', [(i, i ^ at + 1 << first) for i in range(devic...]
    ppermute x6 -> x5, starting transfers between devices: 8.19 us -> 8.62 us  [move(): lax.ppermute(block, 'ctx', [(i, i ^ at + 1 << first) for i in range(devic...]
  transfers between devices with their start and end apart: 8 -> 6, of which waited for: 6 -> 5; matrix products, arithmetic and copies ran while one was open for 0% -> 0% of each run, Pallas kernels for 14% -> 7%
where the time goes in v4:
time: 83.5 us; the launch traced here: 82.9 us
  blocking collectives  31.4 us (38%)
  Pallas kernels  19.8 us (24%)
  waiting for transfers between devices  17.4 us (21%)
  starting transfers between devices  12.2 us (15%)
    all_to_all x2, blocking collectives, exchange(): return lax.all_to_all(array, 'ctx', split_axis=0, concat_axis=0, tiled=True)  31.4 us
    ppermute x5, waiting for transfers between devices, move(): lax.ppermute(block, 'ctx', [(i, i ^ at + 1 << first) for i in range(devic...  17.4 us
    pallas_call x1, Pallas kernels, attend(): pl.pallas_call(functools.partial(attend_kernel, new_kv.shape[0]), name='a...  9.08 us
    ppermute x5, starting transfers between devices, move(): lax.ppermute(block, 'ctx', [(i, i ^ at + 1 << first) for i in range(devic...  8.62 us
    pallas_call x1, Pallas kernels, project(): pl.pallas_call(project_kernel, name='project', in_specs=[pl.BlockSpec(mem...  4.48 us
    pallas_call x3, Pallas kernels, pick(): pl.pallas_call(functools.partial(pick_kernel, rounds, now, rows, len(arri...  4.03 us
    all_to_all x1, starting transfers between devices, exchange(): return lax.all_to_all(array, 'ctx', split_axis=0, concat_axis=0, tiled=True)  3.54 us
    pallas_call x1, Pallas kernels, place(): pl.pallas_call(functools.partial(place_kernel, rounds, rows), name='place...  2.16 us
  transfers between devices with their start and end apart: 6, of which 5 were waited for; matrix products, arithmetic and copies ran while one was open for 0% of the time, Pallas kernels for 7%

profile of v4, /device:TPU:0, one launch (start us, length us, event | category | flops | bytes accessed | tf_op | source)
XLA Modules:
  0.0 82.9 jit_solution(31400117593439707)
XLA Ops:
  0.6 0.0 copy-start
  0.6 0.7 copy-done
  1.4 18.0 %all_to_all.15 = bf16[16,1,64,128]{3,2,1,0:T(8,128)(2,1)S(1)} all-to-all(bf16[16,1,64,128]{3,2,1,0:T(8,128)(2,1)S(1)} %ask.1), channel_id=1, replica_groups=mesh['req'=2,'ctx'=16] {'ctx'}, dimensions={0} | all-to-all | bytes 524288 | tf_op jit(solution)/shard_map/all_to_all | solution.py:445
  19.4 0.0 copy-start.1
  19.5 9.1 %attend.1 = bf16[16,1,72,128]{3,2,1,0:T(8,128)(2,1)S(1)} custom-call(bf16[16,64,128]{2,1,0:T(8,128)(2,1)S(1)} %bitcast.3, s32[16]{0:T(128)} %parents_in.9, s32[4,16]{1,0:T(4,128)} %bitcast.4, s32[16]{0:T(128)} %lengths_in.9, bf16[1,1024,2,1024]{3,2,1,0:T(2,128)(2,1)} %prefix.1, bf16[8,16,2,1024]{3,2,1,0:T(2,128)(2,1)} %pool.9, bf16[1,2,1024]{2,1,0:T(2,128)(2,1)} %new_kv.3), custom_call_target="tpu_custom_call" | custom-call | flops 536870912 | bytes 4194304 | tf_op jit(solution)/shard_map/attend/pallas_call | solution.py:348
  28.5 13.4 %all_to_all.16.partial = bf16[16,1,72,128]{3,2,1,0:T(8,128)(2,1)S(1)} all-to-all(bf16[16,1,72,128]{3,2,1,0:T(8,128)(2,1)S(1)} %attend.1), channel_id=1, replica_groups=mesh['req'=2,'ctx'=16] {'ctx'}, dimensions={0} | all-to-all | bytes 589824 | tf_op jit(solution)/shard_map/all_to_all | solution.py:445
  42.0 4.5 %project.1 = bf16[16,64,128]{2,1,0:T(8,128)(2,1)} custom-call(bf16[16,1,72,128]{3,2,1,0:T(8,128)(2,1)S(1)} %all_to_all.16.partial, bf16[512,8192]{1,0:T(8,128)(2,1)} %weight.1), custom_call_target="tpu_custom_call" | custom-call | flops 134217728 | bytes 8388608 | tf_op jit(solution)/shard_map/project/pallas_call | solution.py:422
  46.5 3.5 %all-to-all-start.2 = ((bf16[16,64,128]{2,1,0:T(8,128)(2,1)}), bf16[16,64,128]{2,1,0:T(8,128)(2,1)S(1)}, u32[]{:S(2)}, u32[]{:S(2)}) async-start(bf16[16,64,128]{2,1,0:T(8,128)(2,1)} %project.1), calls=%async_computation.2 | async-start | bytes 524288 | tf_op jit(solution)/shard_map/all_to_all | solution.py:445
  50.0 2.1 %pick.3 = (bf16[4,16,2,1024]{3,2,1,0:T(2,128)(2,1)S(1)}, bf16[4,16,2,1024]{3,2,1,0:T(2,128)(2,1)S(1)}, bf16[4,16,2,1024]{3,2,1,0:T(2,128)(2,1)S(1)}) custom-call(s32[16]{0:T(128)} %parents_in.9, s32[4,16]{1,0:T(4,128)} %bitcast.5, s32[16]{0:T(128)} %lengths_in.9, bf16[8,16,2,1024]{3,2,1,0:T(2,128)(2,1)} %pool.9), custom_call_target="tpu_custom_call" | custom-call | bytes 4194304 | tf_op jit(solution)/shard_map/pick/pallas_call | solution.py:148
  52.1 1.9 %collective-permute-start = (bf16[4,16,2,1024]{3,2,1,0:T(2,128)(2,1)S(1)}, bf16[4,16,2,1024]{3,2,1,0:T(2,128)(2,1)S(1)}, u32[]{:S(2)}, u32[]{:S(2)}) collective-permute-start(bf16[4,16,2,1024]{3,2,1,0:T(2,128)(2,1)S(1)} %get-tuple-element.5), channel_id=1, source_target_pairs={{0,1},{1,0},{2,3},{3,2},{4,5},{5,4},{6,7},{7,6},{8,9},{9,8},{10,11... | collective-permute-start | bytes 786440 | tf_op jit(solution)/shard_map/ppermute | solution.py:461
  54.0 1.5 %collective-permute-start.1 = (bf16[4,16,2,1024]{3,2,1,0:T(2,128)(2,1)S(1)}, bf16[4,16,2,1024]{3,2,1,0:T(2,128)(2,1)S(1)}, u32[]{:S(2)}, u32[]{:S(2)}) collective-permute-start(bf16[4,16,2,1024]{3,2,1,0:T(2,128)(2,1)S(1)} %get-tuple-element.6), channel_id=1, source_target_pairs={{0,2},{1,3},{2,0},{3,1},{4,6},{5,7},{6,4},{7,5},{8,10},{9,11},{10,... | collective-permute-start | bytes 786440 | tf_op jit(solution)/shard_map/ppermute | solution.py:461
  55.5 0.2 collective-permute-start.2
  55.7 6.4 %collective-permute-done.refs_0_ = bf16[4,16,2,1024]{3,2,1,0:T(2,128)(2,1)S(1)} collective-permute-done((bf16[4,16,2,1024]{3,2,1,0:T(2,128)(2,1)S(1)}, bf16[4,16,2,1024]{3,2,1,0:T(2,128)(2,1)S(1)}, u32[]{:S(2)}, u32[]{:S(2)}) %collective-permute-start) | collective-permute-done | bytes 262176 | tf_op jit(solution)/shard_map/ppermute | solution.py:461
  62.1 4.1 %collective-permute-done.1.refs_1_ = bf16[4,16,2,1024]{3,2,1,0:T(2,128)(2,1)S(1)} collective-permute-done((bf16[4,16,2,1024]{3,2,1,0:T(2,128)(2,1)S(1)}, bf16[4,16,2,1024]{3,2,1,0:T(2,128)(2,1)S(1)}, u32[]{:S(2)}, u32[]{:S(2)}) %collective-permute-start.1) | collective-permute-done | bytes 262176 | tf_op jit(solution)/shard_map/ppermute | solution.py:461
  66.3 1.6 %collective-permute-done.2.refs_2_ = bf16[4,16,2,1024]{3,2,1,0:T(2,128)(2,1)S(1)} collective-permute-done((bf16[4,16,2,1024]{3,2,1,0:T(2,128)(2,1)S(1)}, bf16[4,16,2,1024]{3,2,1,0:T(2,128)(2,1)S(1)}, u32[]{:S(2)}, u32[]{:S(2)}) %collective-permute-start.2) | collective-permute-done | bytes 262176 | tf_op jit(solution)/shard_map/ppermute | solution.py:461
  67.8 1.0 %pick.4 = bf16[2,16,2,1024]{3,2,1,0:T(2,128)(2,1)S(1)} custom-call(s32[16]{0:T(128)} %parents_in.9, s32[4,16]{1,0:T(4,128)} %bitcast.6, s32[16]{0:T(128)} %lengths_in.9, bf16[8,16,2,1024]{3,2,1,0:T(2,128)(2,1)} %pool.9, bf16[4,16,2,1024]{3,2,1,0:T(2,128)(2,1)S(1)} %collective-permute-done.refs_0_, ...), custom_call_target="tpu_custom_call" | custom-call | bytes 4194304 | tf_op jit(solution)/shard_map/pick/pallas_call | solution.py:148
  68.9 2.1 %collective-permute-start.3 = (bf16[2,16,2,1024]{3,2,1,0:T(2,128)(2,1)S(1)}, bf16[2,16,2,1024]{3,2,1,0:T(2,128)(2,1)S(1)}, u32[]{:S(2)}, u32[]{:S(2)}) collective-permute-start(bf16[2,16,2,1024]{3,2,1,0:T(2,128)(2,1)S(1)} %pick.4), channel_id=1, source_target_pairs={{0,4},{1,5},{2,6},{3,7},{4,0},{5,1},{6,2},{7,3},{8,12},{9,13},{10,... | collective-permute-start | bytes 393224 | tf_op jit(solution)/shard_map/ppermute | solution.py:461
  71.0 2.9 %collective-permute-done.3.refs_3_ = bf16[2,16,2,1024]{3,2,1,0:T(2,128)(2,1)S(1)} collective-permute-done((bf16[2,16,2,1024]{3,2,1,0:T(2,128)(2,1)S(1)}, bf16[2,16,2,1024]{3,2,1,0:T(2,128)(2,1)S(1)}, u32[]{:S(2)}, u32[]{:S(2)}) %collective-permute-start.3) | collective-permute-done | bytes 131104 | tf_op jit(solution)/shard_map/ppermute | solution.py:461
  73.9 0.9 %pick.5 = bf16[1,16,2,1024]{3,2,1,0:T(2,128)(2,1)S(1)} custom-call(s32[16]{0:T(128)} %parents_in.9, s32[4,16]{1,0:T(4,128)} %bitcast.7, s32[16]{0:T(128)} %lengths_in.9, bf16[8,16,2,1024]{3,2,1,0:T(2,128)(2,1)} %pool.9, bf16[4,16,2,1024]{3,2,1,0:T(2,128)(2,1)S(1)} %collective-permute-done.refs_0_, ...), custom_call_target="tpu_custom_call" | custom-call | bytes 4194304 | tf_op jit(solution)/shard_map/pick/pallas_call | solution.py:148
  74.8 2.9 %collective-permute-start.4 = (bf16[1,16,2,1024]{3,2,1,0:T(2,128)(2,1)S(1)}, bf16[1,16,2,1024]{3,2,1,0:T(2,128)(2,1)S(1)}, u32[]{:S(2)}, u32[]{:S(2)}) collective-permute-start(bf16[1,16,2,1024]{3,2,1,0:T(2,128)(2,1)S(1)} %pick.5), channel_id=1, source_target_pairs={{0,8},{1,9},{2,10},{3,11},{4,12},{5,13},{6,14},{7,15},{8,0},{9,1},... | collective-permute-start | bytes 196616 | tf_op jit(solution)/shard_map/ppermute | solution.py:461
  77.8 2.3 %collective-permute-done.4.refs_4_ = bf16[1,16,2,1024]{3,2,1,0:T(2,128)(2,1)S(1)} collective-permute-done((bf16[1,16,2,1024]{3,2,1,0:T(2,128)(2,1)S(1)}, bf16[1,16,2,1024]{3,2,1,0:T(2,128)(2,1)S(1)}, u32[]{:S(2)}, u32[]{:S(2)}) %collective-permute-start.4) | collective-permute-done | bytes 65568 | tf_op jit(solution)/shard_map/ppermute | solution.py:461
  80.1 0.0 copy-done.1
  80.1 2.2 %place.1 = bf16[8,16,2,1024]{3,2,1,0:T(2,128)(2,1)} custom-call(s32[16]{0:T(128)} %parents_in.9, s32[4,16]{1,0:T(4,128)} %bitcast.8, s32[16]{0:T(128)} %lengths_in.9, s32[16]{0:T(128)} %fresh_in.1, bf16[1,2,1024]{2,1,0:T(2,128)(2,1)S(1)} %copy-done.1, bf16[8,16,2,1024]{3,2,1,0:T(2,128)(2,1)} %pool.9, ...), custom_call_target="tpu_custom_call" | custom-call | bytes 1048576 | tf_op jit(solution)/shard_map/place/pallas_call | solution.py:195
  82.2 0.0 all-to-all-done.2
  82.2 0.7 convert_reduce_fusion
  (1 shorter events, 0.0 us)
Async XLA Ops:
  0.6 0.8 copy-start
  19.4 60.6 %copy-start.1 = (bf16[1,2,1024]{2,1,0:T(2,128)(2,1)S(1)}, bf16[1,2,1024]{2,1,0:T(2,128)(2,1)}, u32[]{:S(2)}) copy-start(bf16[1,2,1024]{2,1,0:T(2,128)(2,1)} %new_kv.3) | copy-start | bytes 12292
  46.5 35.8 %all-to-all-start.2 = ((bf16[16,64,128]{2,1,0:T(8,128)(2,1)}), bf16[16,64,128]{2,1,0:T(8,128)(2,1)S(1)}, u32[]{:S(2)}, u32[]{:S(2)}) async-start(bf16[16,64,128]{2,1,0:T(8,128)(2,1)} %project.1), calls=%async_computation.2 | async-start | bytes 524288 | tf_op jit(solution)/shard_map/all_to_all | solution.py:445
  52.1 10.0 %collective-permute-start = (bf16[4,16,2,1024]{3,2,1,0:T(2,128)(2,1)S(1)}, bf16[4,16,2,1024]{3,2,1,0:T(2,128)(2,1)S(1)}, u32[]{:S(2)}, u32[]{:S(2)}) collective-permute-start(bf16[4,16,2,1024]{3,2,1,0:T(2,128)(2,1)S(1)} %get-tuple-element.5), channel_id=1, source_target_pairs={{0,1},{1,0},{2,3},{3,2},{4,5},{5,4},{6,7},{7,6},{8,9},{9,8},{10,11... | collective-permute-start | bytes 786440 | tf_op jit(solution)/shard_map/ppermute | solution.py:461
  54.0 12.3 %collective-permute-start.1 = (bf16[4,16,2,1024]{3,2,1,0:T(2,128)(2,1)S(1)}, bf16[4,16,2,1024]{3,2,1,0:T(2,128)(2,1)S(1)}, u32[]{:S(2)}, u32[]{:S(2)}) collective-permute-start(bf16[4,16,2,1024]{3,2,1,0:T(2,128)(2,1)S(1)} %get-tuple-element.6), channel_id=1, source_target_pairs={{0,2},{1,3},{2,0},{3,1},{4,6},{5,7},{6,4},{7,5},{8,10},{9,11},{10,... | collective-permute-start | bytes 786440 | tf_op jit(solution)/shard_map/ppermute | solution.py:461
  55.5 12.4 %collective-permute-start.2 = (bf16[4,16,2,1024]{3,2,1,0:T(2,128)(2,1)S(1)}, bf16[4,16,2,1024]{3,2,1,0:T(2,128)(2,1)S(1)}, u32[]{:S(2)}, u32[]{:S(2)}) collective-permute-start(bf16[4,16,2,1024]{3,2,1,0:T(2,128)(2,1)S(1)} %get-tuple-element.7), channel_id=1, source_target_pairs={{0,3},{1,2},{2,1},{3,0},{4,7},{5,6},{6,5},{7,4},{8,11},{9,10},{10,... | collective-permute-start | bytes 786440 | tf_op jit(solution)/shard_map/ppermute | solution.py:461
  68.9 5.1 %collective-permute-start.3 = (bf16[2,16,2,1024]{3,2,1,0:T(2,128)(2,1)S(1)}, bf16[2,16,2,1024]{3,2,1,0:T(2,128)(2,1)S(1)}, u32[]{:S(2)}, u32[]{:S(2)}) collective-permute-start(bf16[2,16,2,1024]{3,2,1,0:T(2,128)(2,1)S(1)} %pick.4), channel_id=1, source_target_pairs={{0,4},{1,5},{2,6},{3,7},{4,0},{5,1},{6,2},{7,3},{8,12},{9,13},{10,... | collective-permute-start | bytes 393224 | tf_op jit(solution)/shard_map/ppermute | solution.py:461
  74.8 5.2 %collective-permute-start.4 = (bf16[1,16,2,1024]{3,2,1,0:T(2,128)(2,1)S(1)}, bf16[1,16,2,1024]{3,2,1,0:T(2,128)(2,1)S(1)}, u32[]{:S(2)}, u32[]{:S(2)}) collective-permute-start(bf16[1,16,2,1024]{3,2,1,0:T(2,128)(2,1)S(1)} %pick.5), channel_id=1, source_target_pairs={{0,8},{1,9},{2,10},{3,11},{4,12},{5,13},{6,14},{7,15},{8,0},{9,1},... | collective-permute-start | bytes 196616 | tf_op jit(solution)/shard_map/ppermute | solution.py:461

commit v5 on v4

--- a/solution.py
+++ b/solution.py
@@ -212,162 +212,241 @@
     return high.astype(f32), middle.astype(f32), low.astype(f32)
 
 
-def attend_kernel(
+def tiles(array):
+    width = array.shape[-1]
+    split = array.reshape(-1, 2, width // HD, HD).transpose(0, 2, 1, 3)
+    return split.reshape(-1, HD)
+
+
+def unpack_kernel(
     rows,
-    query,
+    block_len,
     parents_in,
     table_in,
     lengths_in,
     prefix,
     pool,
     new_kv,
-    out,
-    wide,
-    stacks,
+    keys,
+    values,
     bias,
     raw,
-    pairs,
-    sem,
+    wide,
+    value_buffer,
+    in_sem,
+    tail_sem,
+    out_sem,
     parents,
     table,
     lengths,
     meta_sem,
 ):
+    requests = keys.shape[0]
+    per = 2 * KVH
+    size = raw.shape[1]
+    tokens = size // per
+    chunks = raw.shape[0] - 1
+    old = tokens - CAP * block_len
+    blocks = tokens // block_len
+    me = lax.axis_index("ctx")
+    metas = load_meta((parents_in, table_in, lengths_in), (parents, table, lengths), meta_sem)
+
+    first, last = old * per, (old + rows) * per
+    spans = [
+        (pool.at[pl.ds(0, first)], 0, first),
+        (new_kv, first, last - first),
+        (pool.at[pl.ds(last, size - last)], last, size - last),
+    ]
+    tails = [
+        pltpu.make_async_copy(source, raw.at[chunks, pl.ds(at, count)], tail_sem.at[index])
+        for index, (source, at, count) in enumerate(spans)
+    ]
+
+    def load(request, chunk):
+        at = pl.multiple_of((request * chunks + chunk) * size, size)
+        return pltpu.make_async_copy(prefix.at[pl.ds(at, size)], raw.at[chunk], in_sem.at[chunk])
+
+    def store(request, chunk):
+        span = pl.ds(pl.multiple_of(chunk * tokens, tokens), tokens)
+        return pltpu.make_async_copy(
+            value_buffer.at[:, span], values.at[request, :, span], out_sem.at[chunk]
+        )
+
+    def split(request, chunk):
+        slot = chunk % 2
+        wide[slot] = raw[chunk].astype(f32)
+        span = pl.ds(pl.multiple_of(chunk * tokens, tokens), tokens)
+        for head in range(KVH):
+            keys[request, head, span, :] = wide[
+                slot, pl.ds(2 * head, tokens, stride=per), :
+            ].astype(bf16)
+            value_buffer[head, span, :] = wide[
+                slot, pl.ds(2 * head + 1, tokens, stride=per), :
+            ].astype(bf16)
+        store(request, chunk).start()
+
+    for copy in tails:
+        copy.start()
+    for request in range(requests):
+        for chunk in range(chunks):
+            load(request, chunk).start()
+        if request == 0:
+            for copy in metas:
+                copy.wait()
+            position = lax.broadcasted_iota(jnp.int32, (1, tokens), 1)
+            in_block, at_block = position % block_len, position // block_len
+
+            def mask(row, carry):
+                parent = parents[row]
+                tail = lengths[parent]
+                reach = jnp.zeros((1, tokens), jnp.int32)
+                for depth in range(table.shape[0]):
+                    block = table[depth, parent] - me * blocks
+                    reach = jnp.where(at_block == block, tail - depth * block_len, reach)
+                own = row - me * rows
+                own = jnp.where((own >= 0) & (own < rows), own + old, -1)
+                live = (in_block < reach) | (position == own)
+                bias[pl.ds(row, 1), :] = jnp.where(live, 0.0, masked_score)
+                return carry
+
+            lax.fori_loop(0, bias.shape[0], mask, 0)
+            for copy in tails:
+                copy.wait()
+
+        def step(chunk, carry):
+            @pl.when(chunk < chunks)
+            def _():
+                load(request, chunk).wait()
+
+            split(request, chunk)
+            return carry
+
+        lax.fori_loop(0, chunks + 1, step, 0)
+        for chunk in range(chunks + 1):
+            store(request, chunk).wait()
+
+
+def unpack(meta, prefix_kv, pool, new_kv, row_total):
+    requests, length = prefix_kv.shape[:2]
+    blocks, block_len = pool.shape[:2]
+    tokens = blocks * block_len
+    chunks = length // tokens
+    size = 2 * KVH * tokens
+    whole = (KVH, length + tokens, HD)
+    hbm, vmem = pl.BlockSpec(memory_space=pltpu.HBM), pl.BlockSpec(memory_space=pltpu.VMEM)
+    arrays = tuple(map(tiles, (prefix_kv, pool, new_kv)))
+    return pl.pallas_call(
+        functools.partial(unpack_kernel, new_kv.shape[0], block_len),
+        name="unpack",
+        in_specs=[hbm] * 6,
+        out_specs=[vmem, hbm, vmem],
+        out_shape=[
+            jax.ShapeDtypeStruct((requests,) + whole, bf16),
+            pltpu.HBM((requests,) + whole, bf16),
+            jax.ShapeDtypeStruct((row_total, tokens), f32),
+        ],
+        scratch_shapes=[
+            pltpu.VMEM((chunks + 1, size, HD), bf16),
+            pltpu.VMEM((2, size, HD), f32),
+            pltpu.VMEM(whole, bf16),
+            pltpu.SemaphoreType.DMA((chunks,)),
+            pltpu.SemaphoreType.DMA((3,)),
+            pltpu.SemaphoreType.DMA((chunks + 1,)),
+        ]
+        + meta_scratch(meta),
+        compiler_params=pltpu.CompilerParams(vmem_limit_bytes=VMEM_LIMIT),
+        cost_estimate=pl.CostEstimate(
+            flops=0, bytes_accessed=3 * prefix_kv.size, transcendentals=0
+        ),
+    )(*map(in_hbm, meta + arrays))
+
+
+def attend_kernel(query, keys, values, bias, out, wide, stacks, value_buffer, sem):
     groups = HQ // KVH
+    requests = keys.shape[0]
     targets = out.shape[0] // KVH
-    beams = query.shape[0]
+    beams = query.shape[0] // requests
     count = groups * beams
     share = count // targets
+    tokens = bias.shape[1]
+    length = keys.shape[2] - tokens
     factor = HD ** (-0.5) * math.log2(math.e)
     contract = (((1,), (1,)), ((), ()))
-    request = pl.program_id(0)
-    length = prefix.shape[1]
-    blocks, block_len = pool.shape[:2]
-    tokens = blocks * block_len
-    old = tokens - CAP * block_len
-    me = lax.axis_index("ctx")
-
-    def loads(head):
-        lanes = pl.ds(pl.multiple_of(head * HD, HD), HD)
-        flat = pool.reshape(tokens, 2, pool.shape[3])
-        spans = [
-            (prefix.at[request, :, :, lanes], 0, length),
-            (flat.at[pl.ds(0, old), :, lanes], length, old),
-            (new_kv.at[:, :, lanes], length + old, rows),
-            (flat.at[pl.ds(old + rows, tokens - old - rows), :, lanes], length + old + rows, 0),
-        ]
-        return [
-            pltpu.make_async_copy(
-                source, raw.at[head, pl.ds(first, source.shape[0])], sem.at[index, head]
+    lane = lax.broadcasted_iota(jnp.int32, (count, HD), 1)
+
+    def load(request, head):
+        return pltpu.make_async_copy(values.at[request, head], value_buffer.at[head], sem.at[head])
+
+    for request in range(requests):
+        for head in range(KVH):
+            load(request, head).start()
+        span = pl.ds(request * beams, beams)
+        wide[...] = query[span].astype(f32).reshape(beams * HQ, HD)
+        for head in range(HQ):
+            stacks[head * beams : (head + 1) * beams, :] = wide[
+                pl.ds(head, beams, stride=HQ), :
+            ].astype(bf16)
+
+        def one(head):
+            stacked = stacks[pl.ds(pl.multiple_of(head * count, count), count), :]
+            score = lax.dot_general(
+                stacked, keys[request, head], contract, preferred_element_type=f32
             )
-            for index, (source, first, _) in enumerate(spans)
-        ]
-
-    sources = (parents_in, table_in, lengths_in)
-    copies = load_meta(sources, (parents, table, lengths), meta_sem)
-    for head in range(KVH):
-        for copy in loads(head):
-            copy.start()
-
-    wide[...] = query[...].astype(f32).reshape(beams * HQ, HD)
-    for head in range(HQ):
-        stacks[head * beams : (head + 1) * beams, :] = wide[pl.ds(head, beams, stride=HQ), :].astype(
-            bf16
-        )
-    for copy in copies:
-        copy.wait()
-    position = lax.broadcasted_iota(jnp.int32, (1, tokens), 1)
-    in_block, at_block = position % block_len, position // block_len
-
-    for beam in range(beams):
-        row = request * beams + beam
-        parent = parents[row]
-        tail = lengths[parent]
-        reach = jnp.zeros((1, tokens), jnp.int32)
-        for depth in range(table.shape[0]):
-            block = table[depth, parent] - me * blocks
-            reach = jnp.where(at_block == block, tail - depth * block_len, reach)
-        own = row - me * rows
-        own = jnp.where((own >= 0) & (own < rows), own + old, -1)
-        live = (in_block < reach) | (position == own)
-        bias[beam : beam + 1, :] = jnp.where(live, 0.0, masked_score)
-
-    lane = lax.broadcasted_iota(jnp.int32, (count, HD), 1)
-
-    def one(head, slot):
-        stacked = stacks[pl.ds(pl.multiple_of(head * count, count), count), :]
-        total_len = length + tokens
-        pairs[slot] = raw.at[head].reshape(2 * total_len, HD)[...].astype(f32)
-        keys = pairs[slot, pl.ds(0, total_len, stride=2), :].astype(bf16)
-        values = pairs[slot, pl.ds(1, total_len, stride=2), :].astype(bf16)
-        score = lax.dot_general(stacked, keys, contract, preferred_element_type=f32)
-        tail = score[:, length:] + jnp.concatenate([bias[...]] * groups, axis=0)
-        score = score[:, :length]
-        top = jnp.maximum(
-            jnp.max(score, axis=1, keepdims=True), jnp.max(tail, axis=1, keepdims=True)
-        )
-        weight = jnp.exp2((score - top) * factor)
-        tail_weight = jnp.exp2((tail - top) * factor)
-        total = jnp.sum(weight, axis=1, keepdims=True) + jnp.sum(
-            tail_weight, axis=1, keepdims=True
-        )
-        weight = jnp.concatenate([weight.astype(bf16), tail_weight.astype(bf16)], axis=1)
-        result = jnp.dot(weight, values, preferred_element_type=f32)
-        packed = jnp.zeros((count, HD), f32)
-        for at, term in enumerate(pieces(top) + pieces(total)):
-            packed = jnp.where(lane == at, term, packed)
-        if count < HD:
-            packed = jnp.concatenate([packed, jnp.zeros((HD - count, HD), f32)], axis=0)
-        stats = packed.T
-        for t in range(targets):
-            at = head * targets + t
-            out[at, 0, :share, :] = result[t * share : (t + 1) * share].astype(bf16)
-            mine = stats if t == 0 else pltpu.roll(stats, HD - t * share, 1)
-            out[at, 0, share : share + STAT_ROWS, :] = mine[:STAT_ROWS].astype(bf16)
-
-    def some(step, carry):
-        heads = [step * AT_ONCE + i for i in range(AT_ONCE)]
-        for head in heads:
-            for copy in loads(head):
-                copy.wait()
-        for slot, head in enumerate(heads):
-            one(head, slot)
-        return carry
-
-    lax.fori_loop(0, KVH // AT_ONCE, some, 0)
-
-
-def attend(everyone, meta, prefix_kv, pool, new_kv, devices):
-    requests, length = prefix_kv.shape[:2]
-    tokens = pool.shape[0] * pool.shape[1]
+            tail = score[:, length:] + jnp.concatenate([bias[span, :]] * groups, axis=0)
+            score = jnp.concatenate([score[:, :length], tail], axis=1)
+            top = jnp.max(score, axis=1, keepdims=True)
+            weight = jnp.exp2((score - top) * factor)
+            total = jnp.sum(weight, axis=1, keepdims=True)
+            result = jnp.dot(weight.astype(bf16), value_buffer[head], preferred_element_type=f32)
+            packed = jnp.zeros((count, HD), f32)
+            for at, term in enumerate(pieces(top) + pieces(total)):
+                packed = jnp.where(lane == at, term, packed)
+            if count < HD:
+                packed = jnp.concatenate([packed, jnp.zeros((HD - count, HD), f32)], axis=0)
+            stats = packed.T
+            for t in range(targets):
+                at = head * targets + t
+                out[at, request, :share, :] = result[t * share : (t + 1) * share].astype(bf16)
+                mine = stats if t == 0 else pltpu.roll(stats, HD - t * share, 1)
+                out[at, request, share : share + STAT_ROWS, :] = mine[:STAT_ROWS].astype(bf16)
+
+        def some(step, carry):
+            heads = [step * AT_ONCE + i for i in range(AT_ONCE)]
+            for head in heads:
+                load(request, head).wait()
+            for head in heads:
+                one(head)
+            return carry
+
+        lax.fori_loop(0, KVH // AT_ONCE, some, 0)
+
+
+def attend(everyone, keys, values, bias, devices):
+    requests, _, length, _ = keys.shape
     beams = everyone.shape[0] // requests
     groups = HQ // KVH
     targets = devices // KVH
     rows = groups // targets * beams + STAT_ROWS
-    hbm = pl.BlockSpec(memory_space=pltpu.HBM)
+    hbm, vmem = pl.BlockSpec(memory_space=pltpu.HBM), pl.BlockSpec(memory_space=pltpu.VMEM)
     return pl.pallas_call(
-        functools.partial(attend_kernel, new_kv.shape[0]),
+        attend_kernel,
         name="attend",
-        grid=(requests,),
-        in_specs=[pl.BlockSpec((beams, HQ, HD), lambda r: (r, 0, 0))] + [hbm] * 6,
-        out_specs=pl.BlockSpec((devices, 1, rows, HD), lambda r: (0, r, 0, 0)),
+        in_specs=[vmem, vmem, hbm, vmem],
+        out_specs=vmem,
         out_shape=jax.ShapeDtypeStruct((devices, requests, rows, HD), bf16),
         scratch_shapes=[
             pltpu.VMEM((beams * HQ, HD), f32),
             pltpu.VMEM((beams * HQ, HD), bf16),
-            pltpu.VMEM((beams, tokens), f32),
-            pltpu.VMEM((KVH, length + tokens, 2, HD), bf16),
-            pltpu.VMEM((AT_ONCE, 2 * (length + tokens), HD), f32),
-            pltpu.SemaphoreType.DMA((4, KVH)),
-        ]
-        + meta_scratch(meta),
+            pltpu.VMEM((KVH, length, HD), bf16),
+            pltpu.SemaphoreType.DMA((KVH,)),
+        ],
         compiler_params=pltpu.CompilerParams(vmem_limit_bytes=VMEM_LIMIT),
         cost_estimate=pl.CostEstimate(
             flops=4 * everyone.size * length,
-            bytes_accessed=2 * prefix_kv.size,
+            bytes_accessed=4 * keys.size,
             transcendentals=everyone.size * length // HD,
         ),
-    )(everyone, *map(in_hbm, meta), in_hbm(prefix_kv), in_hbm(pool), in_hbm(new_kv))
+    )(everyone, keys, in_hbm(values), bias)
 
 
 def project_kernel(partial, weight, out, attended, scratch, buffer, sem):
@@ -464,11 +543,12 @@
 
     wide = ask(queries, devices)
     everyone = exchange(wide).reshape(row_total, HQ, HD)
+    tokens = unpack(meta, prefix_kv, pool, new_kv, row_total)
     arrived = []
     for index in range(len(rounds)):
         blocks = pick(rounds[:index], rounds[index], devices, rows, meta, pool, arrived)
         arrived = arrived + move(index, blocks)
-    partial = attend(everyone, meta, prefix_kv, pool, new_kv, devices)
+    partial = attend(everyone, *tokens, devices)
     partial = exchange(partial)
     products = project(partial, out_weight, row_total)
     products = exchange(products.reshape(devices, rows * (width // HD), HD))

time: 83.5 us -> 80.5 us (0.964)
  blocking collectives: 31.4 us -> 13.4 us
  starting transfers between devices: 12.2 us -> 20.5 us
  waiting for transfers between devices: 17.4 us -> 21.6 us
  Pallas kernels: 19.8 us -> 22.2 us
    all_to_all x2 -> x1, blocking collectives: 31.4 us -> 13.4 us  [exchange(): return lax.all_to_all(array, 'ctx', split_axis=0, concat_axis=0, tiled=True)]
    all_to_all x1 -> x2, starting transfers between devices: 3.54 us -> 11.9 us  [exchange(): return lax.all_to_all(array, 'ctx', split_axis=0, concat_axis=0, tiled=True)]
    all_to_all x1 -> x2, waiting for transfers between devices: 0.01 us -> 4.23 us  [exchange(): return lax.all_to_all(array, 'ctx', split_axis=0, concat_axis=0, tiled=True)]
    pallas_call x1 -> x2, Pallas kernels: 9.08 us -> 10.8 us  [the longest x1 5.63 us: unpack(): pl.pallas_call(functools.partial(unpack_kernel, new_kv.shape[0], block_le...]
  transfers between devices with their start and end apart: 6 -> 7, of which waited for: 5 -> 6; matrix products, arithmetic and copies ran while one was open for 0% -> 0% of each run, Pallas kernels for 7% -> 15%
where the time goes in v5:
time: 80.5 us; the launch traced here: 79.9 us
  Pallas kernels  22.2 us (28%)
  waiting for transfers between devices  21.6 us (27%)
  starting transfers between devices  20.5 us (25%)
  blocking collectives  13.4 us (17%)
    ppermute x5, waiting for transfers between devices, move(): lax.ppermute(block, 'ctx', [(i, i ^ at + 1 << first) for i in range(devic...  17.4 us
    all_to_all x1, blocking collectives, exchange(): return lax.all_to_all(array, 'ctx', split_axis=0, concat_axis=0, tiled=True)  13.4 us
    all_to_all x2, starting transfers between devices, exchange(): return lax.all_to_all(array, 'ctx', split_axis=0, concat_axis=0, tiled=True)  11.9 us
    ppermute x5, starting transfers between devices, move(): lax.ppermute(block, 'ctx', [(i, i ^ at + 1 << first) for i in range(devic...  8.62 us
    pallas_call x1, Pallas kernels, unpack(): pl.pallas_call(functools.partial(unpack_kernel, new_kv.shape[0], block_le...  5.63 us
    pallas_call x1, Pallas kernels, attend(): pl.pallas_call(attend_kernel, name='attend', in_specs=[vmem, vmem, hbm, v...  5.14 us
    pallas_call x1, Pallas kernels, project(): pl.pallas_call(project_kernel, name='project', in_specs=[pl.BlockSpec(mem...  4.51 us
    all_to_all x2, waiting for transfers between devices, exchange(): return lax.all_to_all(array, 'ctx', split_axis=0, concat_axis=0, tiled=True)  4.23 us
  transfers between devices with their start and end apart: 7, of which 6 were waited for; matrix products, arithmetic and copies ran while one was open for 0% of the time, Pallas kernels for 15%

profile of v5, /device:TPU:0, one launch (start us, length us, event | category | flops | bytes accessed | tf_op | source)
XLA Modules:
  0.0 79.9 jit_solution(7197771256956464614)
XLA Ops:
  0.6 0.0 copy-start
  0.6 0.7 copy-done
  1.4 0.7 ask.1
  2.1 8.3 %all-to-all-start = ((bf16[16,1,64,128]{3,2,1,0:T(8,128)(2,1)}), bf16[16,1,64,128]{3,2,1,0:T(8,128)(2,1)S(1)}, u32[]{:S(2)}, u32[]{:S(2)}) async-start(bf16[16,1,64,128]{3,2,1,0:T(8,128)(2,1)} %ask.1), calls=%async_computation | async-start | bytes 524288 | tf_op jit(solution)/shard_map/all_to_all | solution.py:524
  10.5 5.6 %unpack.1 = (bf16[1,8,1152,128]{3,2,1,0:T(8,128)(2,1)S(1)}, bf16[1,8,1152,128]{3,2,1,0:T(8,128)(2,1)}, f32[16,128]{1,0:T(8,128)S(1)}) custom-call(s32[16]{0:T(128)} %parents_in.9, s32[4,16]{1,0:T(4,128)} %bitcast.22, s32[16]{0:T(128)} %lengths_in.9, bf16[16384,128]{1,0:T(8,128)(2,1)} %bitcast.21, bf16[2048,128]{1,0:T(8,128)(2,1)} %bitcast.20, ...), custom_call_target="tpu_custom_call" | custom-call | bytes 6291456 | tf_op jit(solution)/shard_map/unpack/pallas_call | solution.py:338
  16.1 4.2 %all-to-all-done = bf16[16,1,64,128]{3,2,1,0:T(8,128)(2,1)S(1)} async-done(((bf16[16,1,64,128]{3,2,1,0:T(8,128)(2,1)}), bf16[16,1,64,128]{3,2,1,0:T(8,128)(2,1)S(1)}, u32[]{:S(2)}, u32[]{:S(2)}) %all-to-all-start) | async-done | bytes 262176 | tf_op jit(solution)/shard_map/all_to_all | solution.py:524
  20.4 5.1 %attend.1 = bf16[16,1,72,128]{3,2,1,0:T(8,128)(2,1)S(1)} custom-call(bf16[16,64,128]{2,1,0:T(8,128)(2,1)S(1)} %bitcast.18, bf16[1,8,1152,128]{3,2,1,0:T(8,128)(2,1)S(1)} %get-tuple-element.8.keys, bf16[1,8,1152,128]{3,2,1,0:T(8,128)(2,1)} %get-tuple-element.9.values, f32[16,128]{1,0:T(8,128)S(1)} %get-tuple-element.10.bias), custom_call_target="tpu_custom_call" | custom-call | flops 603979776 | bytes 4718592 | tf_op jit(solution)/shard_map/attend/pallas_call | solution.py:431
  25.5 13.4 %all_to_all.15.partial = bf16[16,1,72,128]{3,2,1,0:T(8,128)(2,1)S(1)} all-to-all(bf16[16,1,72,128]{3,2,1,0:T(8,128)(2,1)S(1)} %attend.1), channel_id=1, replica_groups=mesh['req'=2,'ctx'=16] {'ctx'}, dimensions={0} | all-to-all | bytes 589824 | tf_op jit(solution)/shard_map/all_to_all | solution.py:524
  38.9 0.0 copy-start.1
  38.9 4.5 %project.1 = bf16[16,64,128]{2,1,0:T(8,128)(2,1)} custom-call(bf16[16,1,72,128]{3,2,1,0:T(8,128)(2,1)S(1)} %all_to_all.15.partial, bf16[512,8192]{1,0:T(8,128)(2,1)} %weight.1), custom_call_target="tpu_custom_call" | custom-call | flops 134217728 | bytes 8388608 | tf_op jit(solution)/shard_map/project/pallas_call | solution.py:501
  43.4 3.5 %all-to-all-start.2 = ((bf16[16,64,128]{2,1,0:T(8,128)(2,1)}), bf16[16,64,128]{2,1,0:T(8,128)(2,1)S(1)}, u32[]{:S(2)}, u32[]{:S(2)}) async-start(bf16[16,64,128]{2,1,0:T(8,128)(2,1)} %project.1), calls=%async_computation.2 | async-start | bytes 524288 | tf_op jit(solution)/shard_map/all_to_all | solution.py:524
  47.0 2.1 %pick.3 = (bf16[4,16,2,1024]{3,2,1,0:T(2,128)(2,1)S(1)}, bf16[4,16,2,1024]{3,2,1,0:T(2,128)(2,1)S(1)}, bf16[4,16,2,1024]{3,2,1,0:T(2,128)(2,1)S(1)}) custom-call(s32[16]{0:T(128)} %parents_in.9, s32[4,16]{1,0:T(4,128)} %bitcast.23, s32[16]{0:T(128)} %lengths_in.9, bf16[8,16,2,1024]{3,2,1,0:T(2,128)(2,1)} %pool.7), custom_call_target="tpu_custom_call" | custom-call | bytes 4194304 | tf_op jit(solution)/shard_map/pick/pallas_call | solution.py:148
  49.1 1.9 %collective-permute-start = (bf16[4,16,2,1024]{3,2,1,0:T(2,128)(2,1)S(1)}, bf16[4,16,2,1024]{3,2,1,0:T(2,128)(2,1)S(1)}, u32[]{:S(2)}, u32[]{:S(2)}) collective-permute-start(bf16[4,16,2,1024]{3,2,1,0:T(2,128)(2,1)S(1)} %get-tuple-element.11), channel_id=1, source_target_pairs={{0,1},{1,0},{2,3},{3,2},{4,5},{5,4},{6,7},{7,6},{8,9},{9,8},{10,11... | collective-permute-start | bytes 786440 | tf_op jit(solution)/shard_map/ppermute | solution.py:540
  51.0 1.5 %collective-permute-start.1 = (bf16[4,16,2,1024]{3,2,1,0:T(2,128)(2,1)S(1)}, bf16[4,16,2,1024]{3,2,1,0:T(2,128)(2,1)S(1)}, u32[]{:S(2)}, u32[]{:S(2)}) collective-permute-start(bf16[4,16,2,1024]{3,2,1,0:T(2,128)(2,1)S(1)} %get-tuple-element.12), channel_id=1, source_target_pairs={{0,2},{1,3},{2,0},{3,1},{4,6},{5,7},{6,4},{7,5},{8,10},{9,11},{10,... | collective-permute-start | bytes 786440 | tf_op jit(solution)/shard_map/ppermute | solution.py:540
  52.4 0.2 collective-permute-start.2
  52.7 6.4 %collective-permute-done.refs_0_ = bf16[4,16,2,1024]{3,2,1,0:T(2,128)(2,1)S(1)} collective-permute-done((bf16[4,16,2,1024]{3,2,1,0:T(2,128)(2,1)S(1)}, bf16[4,16,2,1024]{3,2,1,0:T(2,128)(2,1)S(1)}, u32[]{:S(2)}, u32[]{:S(2)}) %collective-permute-start) | collective-permute-done | bytes 262176 | tf_op jit(solution)/shard_map/ppermute | solution.py:540
  59.1 4.1 %collective-permute-done.1.refs_1_ = bf16[4,16,2,1024]{3,2,1,0:T(2,128)(2,1)S(1)} collective-permute-done((bf16[4,16,2,1024]{3,2,1,0:T(2,128)(2,1)S(1)}, bf16[4,16,2,1024]{3,2,1,0:T(2,128)(2,1)S(1)}, u32[]{:S(2)}, u32[]{:S(2)}) %collective-permute-start.1) | collective-permute-done | bytes 262176 | tf_op jit(solution)/shard_map/ppermute | solution.py:540
  63.2 1.6 %collective-permute-done.2.refs_2_ = bf16[4,16,2,1024]{3,2,1,0:T(2,128)(2,1)S(1)} collective-permute-done((bf16[4,16,2,1024]{3,2,1,0:T(2,128)(2,1)S(1)}, bf16[4,16,2,1024]{3,2,1,0:T(2,128)(2,1)S(1)}, u32[]{:S(2)}, u32[]{:S(2)}) %collective-permute-start.2) | collective-permute-done | bytes 262176 | tf_op jit(solution)/shard_map/ppermute | solution.py:540
  64.8 1.0 %pick.4 = bf16[2,16,2,1024]{3,2,1,0:T(2,128)(2,1)S(1)} custom-call(s32[16]{0:T(128)} %parents_in.9, s32[4,16]{1,0:T(4,128)} %bitcast.24, s32[16]{0:T(128)} %lengths_in.9, bf16[8,16,2,1024]{3,2,1,0:T(2,128)(2,1)} %pool.7, bf16[4,16,2,1024]{3,2,1,0:T(2,128)(2,1)S(1)} %collective-permute-done.refs_0_, ...), custom_call_target="tpu_custom_call" | custom-call | bytes 4194304 | tf_op jit(solution)/shard_map/pick/pallas_call | solution.py:148
  65.8 2.1 %collective-permute-start.3 = (bf16[2,16,2,1024]{3,2,1,0:T(2,128)(2,1)S(1)}, bf16[2,16,2,1024]{3,2,1,0:T(2,128)(2,1)S(1)}, u32[]{:S(2)}, u32[]{:S(2)}) collective-permute-start(bf16[2,16,2,1024]{3,2,1,0:T(2,128)(2,1)S(1)} %pick.4), channel_id=1, source_target_pairs={{0,4},{1,5},{2,6},{3,7},{4,0},{5,1},{6,2},{7,3},{8,12},{9,13},{10,... | collective-permute-start | bytes 393224 | tf_op jit(solution)/shard_map/ppermute | solution.py:540
  68.0 2.9 %collective-permute-done.3.refs_3_ = bf16[2,16,2,1024]{3,2,1,0:T(2,128)(2,1)S(1)} collective-permute-done((bf16[2,16,2,1024]{3,2,1,0:T(2,128)(2,1)S(1)}, bf16[2,16,2,1024]{3,2,1,0:T(2,128)(2,1)S(1)}, u32[]{:S(2)}, u32[]{:S(2)}) %collective-permute-start.3) | collective-permute-done | bytes 131104 | tf_op jit(solution)/shard_map/ppermute | solution.py:540
  70.9 0.9 %pick.5 = bf16[1,16,2,1024]{3,2,1,0:T(2,128)(2,1)S(1)} custom-call(s32[16]{0:T(128)} %parents_in.9, s32[4,16]{1,0:T(4,128)} %bitcast.25, s32[16]{0:T(128)} %lengths_in.9, bf16[8,16,2,1024]{3,2,1,0:T(2,128)(2,1)} %pool.7, bf16[4,16,2,1024]{3,2,1,0:T(2,128)(2,1)S(1)} %collective-permute-done.refs_0_, ...), custom_call_target="tpu_custom_call" | custom-call | bytes 4194304 | tf_op jit(solution)/shard_map/pick/pallas_call | solution.py:148
  71.8 2.9 %collective-permute-start.4 = (bf16[1,16,2,1024]{3,2,1,0:T(2,128)(2,1)S(1)}, bf16[1,16,2,1024]{3,2,1,0:T(2,128)(2,1)S(1)}, u32[]{:S(2)}, u32[]{:S(2)}) collective-permute-start(bf16[1,16,2,1024]{3,2,1,0:T(2,128)(2,1)S(1)} %pick.5), channel_id=1, source_target_pairs={{0,8},{1,9},{2,10},{3,11},{4,12},{5,13},{6,14},{7,15},{8,0},{9,1},... | collective-permute-start | bytes 196616 | tf_op jit(solution)/shard_map/ppermute | solution.py:540
  74.7 2.3 %collective-permute-done.4.refs_4_ = bf16[1,16,2,1024]{3,2,1,0:T(2,128)(2,1)S(1)} collective-permute-done((bf16[1,16,2,1024]{3,2,1,0:T(2,128)(2,1)S(1)}, bf16[1,16,2,1024]{3,2,1,0:T(2,128)(2,1)S(1)}, u32[]{:S(2)}, u32[]{:S(2)}) %collective-permute-start.4) | collective-permute-done | bytes 65568 | tf_op jit(solution)/shard_map/ppermute | solution.py:540
  77.0 0.0 copy-done.1
  77.0 2.2 %place.1 = bf16[8,16,2,1024]{3,2,1,0:T(2,128)(2,1)} custom-call(s32[16]{0:T(128)} %parents_in.9, s32[4,16]{1,0:T(4,128)} %bitcast.26, s32[16]{0:T(128)} %lengths_in.9, s32[16]{0:T(128)} %fresh_in.1, bf16[1,2,1024]{2,1,0:T(2,128)(2,1)S(1)} %copy-done.1, bf16[8,16,2,1024]{3,2,1,0:T(2,128)(2,1)} %pool.7, ...), custom_call_target="tpu_custom_call" | custom-call | bytes 1048576 | tf_op jit(solution)/shard_map/place/pallas_call | solution.py:195
  79.2 0.0 all-to-all-done.2
  79.2 0.7 convert_reduce_fusion
Async XLA Ops:
  0.6 0.8 copy-start
  2.1 18.2 %all-to-all-start = ((bf16[16,1,64,128]{3,2,1,0:T(8,128)(2,1)}), bf16[16,1,64,128]{3,2,1,0:T(8,128)(2,1)S(1)}, u32[]{:S(2)}, u32[]{:S(2)}) async-start(bf16[16,1,64,128]{3,2,1,0:T(8,128)(2,1)} %ask.1), calls=%async_computation | async-start | bytes 524288 | tf_op jit(solution)/shard_map/all_to_all | solution.py:524
  38.9 38.1 %copy-start.1 = (bf16[1,2,1024]{2,1,0:T(2,128)(2,1)S(1)}, bf16[1,2,1024]{2,1,0:T(2,128)(2,1)}, u32[]{:S(2)}) copy-start(bf16[1,2,1024]{2,1,0:T(2,128)(2,1)} %new_kv.1) | copy-start | bytes 12292
  43.4 35.8 %all-to-all-start.2 = ((bf16[16,64,128]{2,1,0:T(8,128)(2,1)}), bf16[16,64,128]{2,1,0:T(8,128)(2,1)S(1)}, u32[]{:S(2)}, u32[]{:S(2)}) async-start(bf16[16,64,128]{2,1,0:T(8,128)(2,1)} %project.1), calls=%async_computation.2 | async-start | bytes 524288 | tf_op jit(solution)/shard_map/all_to_all | solution.py:524
  49.1 10.0 %collective-permute-start = (bf16[4,16,2,1024]{3,2,1,0:T(2,128)(2,1)S(1)}, bf16[4,16,2,1024]{3,2,1,0:T(2,128)(2,1)S(1)}, u32[]{:S(2)}, u32[]{:S(2)}) collective-permute-start(bf16[4,16,2,1024]{3,2,1,0:T(2,128)(2,1)S(1)} %get-tuple-element.11), channel_id=1, source_target_pairs={{0,1},{1,0},{2,3},{3,2},{4,5},{5,4},{6,7},{7,6},{8,9},{9,8},{10,11... | collective-permute-start | bytes 786440 | tf_op jit(solution)/shard_map/ppermute | solution.py:540
  51.0 12.3 %collective-permute-start.1 = (bf16[4,16,2,1024]{3,2,1,0:T(2,128)(2,1)S(1)}, bf16[4,16,2,1024]{3,2,1,0:T(2,128)(2,1)S(1)}, u32[]{:S(2)}, u32[]{:S(2)}) collective-permute-start(bf16[4,16,2,1024]{3,2,1,0:T(2,128)(2,1)S(1)} %get-tuple-element.12), channel_id=1, source_target_pairs={{0,2},{1,3},{2,0},{3,1},{4,6},{5,7},{6,4},{7,5},{8,10},{9,11},{10,... | collective-permute-start | bytes 786440 | tf_op jit(solution)/shard_map/ppermute | solution.py:540
  52.4 12.4 %collective-permute-start.2 = (bf16[4,16,2,1024]{3,2,1,0:T(2,128)(2,1)S(1)}, bf16[4,16,2,1024]{3,2,1,0:T(2,128)(2,1)S(1)}, u32[]{:S(2)}, u32[]{:S(2)}) collective-permute-start(bf16[4,16,2,1024]{3,2,1,0:T(2,128)(2,1)S(1)} %get-tuple-element.13), channel_id=1, source_target_pairs={{0,3},{1,2},{2,1},{3,0},{4,7},{5,6},{6,5},{7,4},{8,11},{9,10},{10,... | collective-permute-start | bytes 786440 | tf_op jit(solution)/shard_map/ppermute | solution.py:540
  65.8 5.1 %collective-permute-start.3 = (bf16[2,16,2,1024]{3,2,1,0:T(2,128)(2,1)S(1)}, bf16[2,16,2,1024]{3,2,1,0:T(2,128)(2,1)S(1)}, u32[]{:S(2)}, u32[]{:S(2)}) collective-permute-start(bf16[2,16,2,1024]{3,2,1,0:T(2,128)(2,1)S(1)} %pick.4), channel_id=1, source_target_pairs={{0,4},{1,5},{2,6},{3,7},{4,0},{5,1},{6,2},{7,3},{8,12},{9,13},{10,... | collective-permute-start | bytes 393224 | tf_op jit(solution)/shard_map/ppermute | solution.py:540
  71.8 5.2 %collective-permute-start.4 = (bf16[1,16,2,1024]{3,2,1,0:T(2,128)(2,1)S(1)}, bf16[1,16,2,1024]{3,2,1,0:T(2,128)(2,1)S(1)}, u32[]{:S(2)}, u32[]{:S(2)}) collective-permute-start(bf16[1,16,2,1024]{3,2,1,0:T(2,128)(2,1)S(1)} %pick.5), channel_id=1, source_target_pairs={{0,8},{1,9},{2,10},{3,11},{4,12},{5,13},{6,14},{7,15},{8,0},{9,1},... | collective-permute-start | bytes 196616 | tf_op jit(solution)/shard_map/ppermute | solution.py:540

commit v6 on v5

--- a/solution.py
+++ b/solution.py
@@ -219,6 +219,7 @@
 
 
 def unpack_kernel(
+    now,
     rows,
     block_len,
     parents_in,
@@ -227,20 +228,16 @@
     prefix,
     pool,
     new_kv,
+    blocked,
     keys,
     values,
     bias,
-    raw,
-    wide,
-    value_buffer,
-    in_sem,
-    tail_sem,
-    out_sem,
-    parents,
-    table,
-    lengths,
-    meta_sem,
+    *refs,
 ):
+    partners = (1 << now[1]) - 1
+    chosen, refs = refs[:partners], refs[partners:]
+    raw, wide, value_buffer, in_sem, tail_sem, out_sem, pick_sem, *refs = refs
+    parents, table, lengths, meta_sem = refs
     requests = keys.shape[0]
     per = 2 * KVH
     size = raw.shape[1]
@@ -293,6 +290,8 @@
         if request == 0:
             for copy in metas:
                 copy.wait()
+            meta = (parents, table, lengths)
+            begin_picks([], now, rows, me, meta, blocked, [], chosen, pick_sem)
             position = lax.broadcasted_iota(jnp.int32, (1, tokens), 1)
             in_block, at_block = position % block_len, position // block_len
 
@@ -324,9 +323,12 @@
         lax.fori_loop(0, chunks + 1, step, 0)
         for chunk in range(chunks + 1):
             store(request, chunk).wait()
-
-
-def unpack(meta, prefix_kv, pool, new_kv, row_total):
+    end_picks(blocked, chosen, pick_sem)
+
+
+def unpack(now, devices, meta, prefix_kv, pool, new_kv):
+    rows = new_kv.shape[0]
+    row_total = rows * devices
     requests, length = prefix_kv.shape[:2]
     blocks, block_len = pool.shape[:2]
     tokens = blocks * block_len
@@ -334,17 +336,19 @@
     size = 2 * KVH * tokens
     whole = (KVH, length + tokens, HD)
     hbm, vmem = pl.BlockSpec(memory_space=pltpu.HBM), pl.BlockSpec(memory_space=pltpu.VMEM)
-    arrays = tuple(map(tiles, (prefix_kv, pool, new_kv)))
+    arrays = tuple(map(tiles, (prefix_kv, pool, new_kv))) + (pool,)
+    shapes, semaphores = pick_shapes(now, devices, rows, pool)
     return pl.pallas_call(
-        functools.partial(unpack_kernel, new_kv.shape[0], block_len),
+        functools.partial(unpack_kernel, now, rows, block_len),
         name="unpack",
-        in_specs=[hbm] * 6,
-        out_specs=[vmem, hbm, vmem],
+        in_specs=[hbm] * 7,
+        out_specs=[vmem, hbm] + [vmem] * (1 + len(shapes)),
         out_shape=[
             jax.ShapeDtypeStruct((requests,) + whole, bf16),
             pltpu.HBM((requests,) + whole, bf16),
             jax.ShapeDtypeStruct((row_total, tokens), f32),
-        ],
+        ]
+        + shapes,
         scratch_shapes=[
             pltpu.VMEM((chunks + 1, size, HD), bf16),
             pltpu.VMEM((2, size, HD), f32),
@@ -352,6 +356,7 @@
             pltpu.SemaphoreType.DMA((chunks,)),
             pltpu.SemaphoreType.DMA((3,)),
             pltpu.SemaphoreType.DMA((chunks + 1,)),
+            pltpu.SemaphoreType.DMA(semaphores),
         ]
         + meta_scratch(meta),
         compiler_params=pltpu.CompilerParams(vmem_limit_bytes=VMEM_LIMIT),
@@ -543,12 +548,14 @@
 
     wide = ask(queries, devices)
     everyone = exchange(wide).reshape(row_total, HQ, HD)
-    tokens = unpack(meta, prefix_kv, pool, new_kv, row_total)
-    arrived = []
-    for index in range(len(rounds)):
+    keys, values, bias, *blocks = unpack(
+        rounds[0], devices, meta, prefix_kv, pool, new_kv
+    )
+    arrived = move(0, blocks)
+    for index in range(1, len(rounds)):
         blocks = pick(rounds[:index], rounds[index], devices, rows, meta, pool, arrived)
         arrived = arrived + move(index, blocks)
-    partial = attend(everyone, *tokens, devices)
+    partial = attend(everyone, keys, values, bias, devices)
     partial = exchange(partial)
     products = project(partial, out_weight, row_total)
     products = exchange(products.reshape(devices, rows * (width // HD), HD))

time: 80.5 us -> 79.2 us (0.984)
  Pallas kernels: 22.2 us -> 20.3 us
    pallas_call x3 -> x2, Pallas kernels: 4.03 us -> 1.9 us  [pick(): pl.pallas_call(functools.partial(pick_kernel, rounds, now, rows, len(arri...]
  transfers between devices with their start and end apart: 7 -> 7, of which waited for: 6 -> 6; matrix products, arithmetic and copies ran while one was open for 0% -> 0% of each run, Pallas kernels for 15% -> 13%
where the time goes in v6:
time: 79.2 us; the launch traced here: 78.6 us
  waiting for transfers between devices  22 us (28%)
  starting transfers between devices  20.7 us (26%)
  Pallas kernels  20.3 us (26%)
  blocking collectives  13.4 us (17%)
    ppermute x5, waiting for transfers between devices, move(): lax.ppermute(block, 'ctx', [(i, i ^ at + 1 << first) for i in range(devic...  18 us
    all_to_all x1, blocking collectives, exchange(): return lax.all_to_all(array, 'ctx', split_axis=0, concat_axis=0, tiled=True)  13.4 us
    all_to_all x2, starting transfers between devices, exchange(): return lax.all_to_all(array, 'ctx', split_axis=0, concat_axis=0, tiled=True)  11.9 us
    ppermute x5, starting transfers between devices, move(): lax.ppermute(block, 'ctx', [(i, i ^ at + 1 << first) for i in range(devic...  8.85 us
    pallas_call x1, Pallas kernels, unpack(): pl.pallas_call(functools.partial(unpack_kernel, now, rows, block_len), na...  5.89 us
    pallas_call x1, Pallas kernels, attend(): pl.pallas_call(attend_kernel, name='attend', in_specs=[vmem, vmem, hbm, v...  5.14 us
    pallas_call x1, Pallas kernels, project(): pl.pallas_call(project_kernel, name='project', in_specs=[pl.BlockSpec(mem...  4.49 us
    all_to_all x2, waiting for transfers between devices, exchange(): return lax.all_to_all(array, 'ctx', split_axis=0, concat_axis=0, tiled=True)  3.97 us
  transfers between devices with their start and end apart: 7, of which 6 were waited for; matrix products, arithmetic and copies ran while one was open for 0% of the time, Pallas kernels for 13%

profile of v6, /device:TPU:0, one launch (start us, length us, event | category | flops | bytes accessed | tf_op | source)
XLA Modules:
  0.0 78.6 jit_solution(13365893691980275249)
XLA Ops:
  0.6 0.0 copy-start
  0.6 0.7 copy-done
  1.4 0.7 ask.1
  2.1 8.3 %all-to-all-start = ((bf16[16,1,64,128]{3,2,1,0:T(8,128)(2,1)}), bf16[16,1,64,128]{3,2,1,0:T(8,128)(2,1)S(1)}, u32[]{:S(2)}, u32[]{:S(2)}) async-start(bf16[16,1,64,128]{3,2,1,0:T(8,128)(2,1)} %ask.1), calls=%async_computation | async-start | bytes 524288 | tf_op jit(solution)/shard_map/all_to_all | solution.py:529
  10.5 5.9 %unpack.1 = (bf16[1,8,1152,128]{3,2,1,0:T(8,128)(2,1)S(1)}, bf16[1,8,1152,128]{3,2,1,0:T(8,128)(2,1)}, f32[16,128]{1,0:T(8,128)S(1)}, bf16[4,16,2,1024]{3,2,1,0:...) custom-call(s32[16]{0:T(128)} %parents_in.7, s32[4,16]{1,0:T(4,128)} %bitcast.22, ...), custom_call_target="tpu_custom_call" | custom-call | bytes 6291456 | tf_op jit(solution)/shard_map/unpack/pallas_call | solution.py:341
  16.4 4.0 %all-to-all-done = bf16[16,1,64,128]{3,2,1,0:T(8,128)(2,1)S(1)} async-done(((bf16[16,1,64,128]{3,2,1,0:T(8,128)(2,1)}), bf16[16,1,64,128]{3,2,1,0:T(8,128)(2,1)S(1)}, u32[]{:S(2)}, u32[]{:S(2)}) %all-to-all-start) | async-done | bytes 262176 | tf_op jit(solution)/shard_map/all_to_all | solution.py:529
  20.4 5.1 %attend.1 = bf16[16,1,72,128]{3,2,1,0:T(8,128)(2,1)S(1)} custom-call(bf16[16,64,128]{2,1,0:T(8,128)(2,1)S(1)} %bitcast.18, bf16[1,8,1152,128]{3,2,1,0:T(8,128)(2,1)S(1)} %get-tuple-element.8.keys, bf16[1,8,1152,128]{3,2,1,0:T(8,128)(2,1)} %get-tuple-element.9.values, f32[16,128]{1,0:T(8,128)S(1)} %get-tuple-element.10.bias), custom_call_target="tpu_custom_call" | custom-call | flops 603979776 | bytes 4718592 | tf_op jit(solution)/shard_map/attend/pallas_call | solution.py:436
  25.5 13.4 %all_to_all.15.partial = bf16[16,1,72,128]{3,2,1,0:T(8,128)(2,1)S(1)} all-to-all(bf16[16,1,72,128]{3,2,1,0:T(8,128)(2,1)S(1)} %attend.1), channel_id=1, replica_groups=mesh['req'=2,'ctx'=16] {'ctx'}, dimensions={0} | all-to-all | bytes 589824 | tf_op jit(solution)/shard_map/all_to_all | solution.py:529
  38.9 0.0 copy-start.1
  38.9 4.5 %project.1 = bf16[16,64,128]{2,1,0:T(8,128)(2,1)} custom-call(bf16[16,1,72,128]{3,2,1,0:T(8,128)(2,1)S(1)} %all_to_all.15.partial, bf16[512,8192]{1,0:T(8,128)(2,1)} %weight.1), custom_call_target="tpu_custom_call" | custom-call | flops 134217728 | bytes 8388608 | tf_op jit(solution)/shard_map/project/pallas_call | solution.py:506
  43.4 3.5 %all-to-all-start.2 = ((bf16[16,64,128]{2,1,0:T(8,128)(2,1)}), bf16[16,64,128]{2,1,0:T(8,128)(2,1)S(1)}, u32[]{:S(2)}, u32[]{:S(2)}) async-start(bf16[16,64,128]{2,1,0:T(8,128)(2,1)} %project.1), calls=%async_computation.2 | async-start | bytes 524288 | tf_op jit(solution)/shard_map/all_to_all | solution.py:529
  47.0 1.8 %collective-permute-start = (bf16[4,16,2,1024]{3,2,1,0:T(2,128)(2,1)S(1)}, bf16[4,16,2,1024]{3,2,1,0:T(2,128)(2,1)S(1)}, u32[]{:S(2)}, u32[]{:S(2)}) collective-permute-start(bf16[4,16,2,1024]{3,2,1,0:T(2,128)(2,1)S(1)} %get-tuple-element.11), channel_id=1, source_target_pairs={{0,1},{1,0},{2,3},{3,2},{4,5},{5,4},{6,7},{7,6},{8,9},{9,8},{10,11... | collective-permute-start | bytes 786440 | tf_op jit(solution)/shard_map/ppermute | solution.py:545
  48.8 1.5 %collective-permute-start.1 = (bf16[4,16,2,1024]{3,2,1,0:T(2,128)(2,1)S(1)}, bf16[4,16,2,1024]{3,2,1,0:T(2,128)(2,1)S(1)}, u32[]{:S(2)}, u32[]{:S(2)}) collective-permute-start(bf16[4,16,2,1024]{3,2,1,0:T(2,128)(2,1)S(1)} %get-tuple-element.12), channel_id=1, source_target_pairs={{0,2},{1,3},{2,0},{3,1},{4,6},{5,7},{6,4},{7,5},{8,10},{9,11},{10,... | collective-permute-start | bytes 786440 | tf_op jit(solution)/shard_map/ppermute | solution.py:545
  50.3 0.3 collective-permute-start.2
  50.5 8.1 %collective-permute-done.refs_0_ = bf16[4,16,2,1024]{3,2,1,0:T(2,128)(2,1)S(1)} collective-permute-done((bf16[4,16,2,1024]{3,2,1,0:T(2,128)(2,1)S(1)}, bf16[4,16,2,1024]{3,2,1,0:T(2,128)(2,1)S(1)}, u32[]{:S(2)}, u32[]{:S(2)}) %collective-permute-start) | collective-permute-done | bytes 262176 | tf_op jit(solution)/shard_map/ppermute | solution.py:545
  58.6 3.2 %collective-permute-done.1.refs_1_ = bf16[4,16,2,1024]{3,2,1,0:T(2,128)(2,1)S(1)} collective-permute-done((bf16[4,16,2,1024]{3,2,1,0:T(2,128)(2,1)S(1)}, bf16[4,16,2,1024]{3,2,1,0:T(2,128)(2,1)S(1)}, u32[]{:S(2)}, u32[]{:S(2)}) %collective-permute-start.1) | collective-permute-done | bytes 262176 | tf_op jit(solution)/shard_map/ppermute | solution.py:545
  61.9 1.5 %collective-permute-done.2.refs_2_ = bf16[4,16,2,1024]{3,2,1,0:T(2,128)(2,1)S(1)} collective-permute-done((bf16[4,16,2,1024]{3,2,1,0:T(2,128)(2,1)S(1)}, bf16[4,16,2,1024]{3,2,1,0:T(2,128)(2,1)S(1)}, u32[]{:S(2)}, u32[]{:S(2)}) %collective-permute-start.2) | collective-permute-done | bytes 262176 | tf_op jit(solution)/shard_map/ppermute | solution.py:545
  63.4 1.0 %pick.2 = bf16[2,16,2,1024]{3,2,1,0:T(2,128)(2,1)S(1)} custom-call(s32[16]{0:T(128)} %parents_in.7, s32[4,16]{1,0:T(4,128)} %bitcast.23, s32[16]{0:T(128)} %lengths_in.7, bf16[8,16,2,1024]{3,2,1,0:T(2,128)(2,1)} %pool.5, bf16[4,16,2,1024]{3,2,1,0:T(2,128)(2,1)S(1)} %collective-permute-done.refs_0_, ...), custom_call_target="tpu_custom_call" | custom-call | bytes 4194304 | tf_op jit(solution)/shard_map/pick/pallas_call | solution.py:148
  64.4 2.1 %collective-permute-start.3 = (bf16[2,16,2,1024]{3,2,1,0:T(2,128)(2,1)S(1)}, bf16[2,16,2,1024]{3,2,1,0:T(2,128)(2,1)S(1)}, u32[]{:S(2)}, u32[]{:S(2)}) collective-permute-start(bf16[2,16,2,1024]{3,2,1,0:T(2,128)(2,1)S(1)} %pick.2), channel_id=1, source_target_pairs={{0,4},{1,5},{2,6},{3,7},{4,0},{5,1},{6,2},{7,3},{8,12},{9,13},{10,... | collective-permute-start | bytes 393224 | tf_op jit(solution)/shard_map/ppermute | solution.py:545
  66.5 2.9 %collective-permute-done.3.refs_3_ = bf16[2,16,2,1024]{3,2,1,0:T(2,128)(2,1)S(1)} collective-permute-done((bf16[2,16,2,1024]{3,2,1,0:T(2,128)(2,1)S(1)}, bf16[2,16,2,1024]{3,2,1,0:T(2,128)(2,1)S(1)}, u32[]{:S(2)}, u32[]{:S(2)}) %collective-permute-start.3) | collective-permute-done | bytes 131104 | tf_op jit(solution)/shard_map/ppermute | solution.py:545
  69.5 0.9 %pick.3 = bf16[1,16,2,1024]{3,2,1,0:T(2,128)(2,1)S(1)} custom-call(s32[16]{0:T(128)} %parents_in.7, s32[4,16]{1,0:T(4,128)} %bitcast.24, s32[16]{0:T(128)} %lengths_in.7, bf16[8,16,2,1024]{3,2,1,0:T(2,128)(2,1)} %pool.5, bf16[4,16,2,1024]{3,2,1,0:T(2,128)(2,1)S(1)} %collective-permute-done.refs_0_, ...), custom_call_target="tpu_custom_call" | custom-call | bytes 4194304 | tf_op jit(solution)/shard_map/pick/pallas_call | solution.py:148
  70.4 3.2 %collective-permute-start.4 = (bf16[1,16,2,1024]{3,2,1,0:T(2,128)(2,1)S(1)}, bf16[1,16,2,1024]{3,2,1,0:T(2,128)(2,1)S(1)}, u32[]{:S(2)}, u32[]{:S(2)}) collective-permute-start(bf16[1,16,2,1024]{3,2,1,0:T(2,128)(2,1)S(1)} %pick.3), channel_id=1, source_target_pairs={{0,8},{1,9},{2,10},{3,11},{4,12},{5,13},{6,14},{7,15},{8,0},{9,1},... | collective-permute-start | bytes 196616 | tf_op jit(solution)/shard_map/ppermute | solution.py:545
  73.5 2.2 %collective-permute-done.4.refs_4_ = bf16[1,16,2,1024]{3,2,1,0:T(2,128)(2,1)S(1)} collective-permute-done((bf16[1,16,2,1024]{3,2,1,0:T(2,128)(2,1)S(1)}, bf16[1,16,2,1024]{3,2,1,0:T(2,128)(2,1)S(1)}, u32[]{:S(2)}, u32[]{:S(2)}) %collective-permute-start.4) | collective-permute-done | bytes 65568 | tf_op jit(solution)/shard_map/ppermute | solution.py:545
  75.8 0.0 copy-done.1
  75.8 2.2 %place.1 = bf16[8,16,2,1024]{3,2,1,0:T(2,128)(2,1)} custom-call(s32[16]{0:T(128)} %parents_in.7, s32[4,16]{1,0:T(4,128)} %bitcast.25, s32[16]{0:T(128)} %lengths_in.7, s32[16]{0:T(128)} %fresh_in.1, bf16[1,2,1024]{2,1,0:T(2,128)(2,1)S(1)} %copy-done.1, bf16[8,16,2,1024]{3,2,1,0:T(2,128)(2,1)} %pool.5, ...), custom_call_target="tpu_custom_call" | custom-call | bytes 1048576 | tf_op jit(solution)/shard_map/place/pallas_call | solution.py:195
  77.9 0.0 all-to-all-done.2
  78.0 0.7 convert_reduce_fusion
Async XLA Ops:
  0.6 0.8 copy-start
  2.1 18.2 %all-to-all-start = ((bf16[16,1,64,128]{3,2,1,0:T(8,128)(2,1)}), bf16[16,1,64,128]{3,2,1,0:T(8,128)(2,1)S(1)}, u32[]{:S(2)}, u32[]{:S(2)}) async-start(bf16[16,1,64,128]{3,2,1,0:T(8,128)(2,1)} %ask.1), calls=%async_computation | async-start | bytes 524288 | tf_op jit(solution)/shard_map/all_to_all | solution.py:529
  38.9 36.9 %copy-start.1 = (bf16[1,2,1024]{2,1,0:T(2,128)(2,1)S(1)}, bf16[1,2,1024]{2,1,0:T(2,128)(2,1)}, u32[]{:S(2)}) copy-start(bf16[1,2,1024]{2,1,0:T(2,128)(2,1)} %new_kv.1) | copy-start | bytes 12292
  43.4 34.5 %all-to-all-start.2 = ((bf16[16,64,128]{2,1,0:T(8,128)(2,1)}), bf16[16,64,128]{2,1,0:T(8,128)(2,1)S(1)}, u32[]{:S(2)}, u32[]{:S(2)}) async-start(bf16[16,64,128]{2,1,0:T(8,128)(2,1)} %project.1), calls=%async_computation.2 | async-start | bytes 524288 | tf_op jit(solution)/shard_map/all_to_all | solution.py:529
  47.0 11.6 %collective-permute-start = (bf16[4,16,2,1024]{3,2,1,0:T(2,128)(2,1)S(1)}, bf16[4,16,2,1024]{3,2,1,0:T(2,128)(2,1)S(1)}, u32[]{:S(2)}, u32[]{:S(2)}) collective-permute-start(bf16[4,16,2,1024]{3,2,1,0:T(2,128)(2,1)S(1)} %get-tuple-element.11), channel_id=1, source_target_pairs={{0,1},{1,0},{2,3},{3,2},{4,5},{5,4},{6,7},{7,6},{8,9},{9,8},{10,11... | collective-permute-start | bytes 786440 | tf_op jit(solution)/shard_map/ppermute | solution.py:545
  48.8 13.1 %collective-permute-start.1 = (bf16[4,16,2,1024]{3,2,1,0:T(2,128)(2,1)S(1)}, bf16[4,16,2,1024]{3,2,1,0:T(2,128)(2,1)S(1)}, u32[]{:S(2)}, u32[]{:S(2)}) collective-permute-start(bf16[4,16,2,1024]{3,2,1,0:T(2,128)(2,1)S(1)} %get-tuple-element.12), channel_id=1, source_target_pairs={{0,2},{1,3},{2,0},{3,1},{4,6},{5,7},{6,4},{7,5},{8,10},{9,11},{10,... | collective-permute-start | bytes 786440 | tf_op jit(solution)/shard_map/ppermute | solution.py:545
  50.3 13.1 %collective-permute-start.2 = (bf16[4,16,2,1024]{3,2,1,0:T(2,128)(2,1)S(1)}, bf16[4,16,2,1024]{3,2,1,0:T(2,128)(2,1)S(1)}, u32[]{:S(2)}, u32[]{:S(2)}) collective-permute-start(bf16[4,16,2,1024]{3,2,1,0:T(2,128)(2,1)S(1)} %get-tuple-element.13), channel_id=1, source_target_pairs={{0,3},{1,2},{2,1},{3,0},{4,7},{5,6},{6,5},{7,4},{8,11},{9,10},{10,... | collective-permute-start | bytes 786440 | tf_op jit(solution)/shard_map/ppermute | solution.py:545
  64.4 5.1 %collective-permute-start.3 = (bf16[2,16,2,1024]{3,2,1,0:T(2,128)(2,1)S(1)}, bf16[2,16,2,1024]{3,2,1,0:T(2,128)(2,1)S(1)}, u32[]{:S(2)}, u32[]{:S(2)}) collective-permute-start(bf16[2,16,2,1024]{3,2,1,0:T(2,128)(2,1)S(1)} %pick.2), channel_id=1, source_target_pairs={{0,4},{1,5},{2,6},{3,7},{4,0},{5,1},{6,2},{7,3},{8,12},{9,13},{10,... | collective-permute-start | bytes 393224 | tf_op jit(solution)/shard_map/ppermute | solution.py:545
  70.4 5.4 %collective-permute-start.4 = (bf16[1,16,2,1024]{3,2,1,0:T(2,128)(2,1)S(1)}, bf16[1,16,2,1024]{3,2,1,0:T(2,128)(2,1)S(1)}, u32[]{:S(2)}, u32[]{:S(2)}) collective-permute-start(bf16[1,16,2,1024]{3,2,1,0:T(2,128)(2,1)S(1)} %pick.3), channel_id=1, source_target_pairs={{0,8},{1,9},{2,10},{3,11},{4,12},{5,13},{6,14},{7,15},{8,0},{9,1},... | collective-permute-start | bytes 196616 | tf_op jit(solution)/shard_map/ppermute | solution.py:545

commit v7 on v6

--- a/solution.py
+++ b/solution.py
@@ -15,7 +15,7 @@
 CAP = 2
 
 STAT_ROWS = 8
-AT_ONCE = 2
+AT_ONCE = 8
 VMEM_LIMIT = 20 << 20
 masked_score = -1e30
 bf16 = jnp.bfloat16
@@ -236,8 +236,9 @@
 ):
     partners = (1 << now[1]) - 1
     chosen, refs = refs[:partners], refs[partners:]
-    raw, wide, value_buffer, in_sem, tail_sem, out_sem, pick_sem, *refs = refs
-    parents, table, lengths, meta_sem = refs
+    raw, wide, value_buffer, in_sem, tail_sem, out_sem, *refs = refs
+    buffers, refs = refs[:partners], refs[partners:]
+    pick_sem, sent_sem, parents, table, lengths, meta_sem = refs
     requests = keys.shape[0]
     per = 2 * KVH
     size = raw.shape[1]
@@ -282,48 +283,55 @@
             ].astype(bf16)
         store(request, chunk).start()
 
-    for copy in tails:
-        copy.start()
+    def mask(row, carry):
+        parent = parents[row]
+        tail = lengths[parent]
+        reach = jnp.zeros((1, tokens), jnp.int32)
+        for depth in range(table.shape[0]):
+            block = table[depth, parent] - me * blocks
+            reach = jnp.where(at_block == block, tail - depth * block_len, reach)
+        own = row - me * rows
+        own = jnp.where((own >= 0) & (own < rows), own + old, -1)
+        live = (in_block < reach) | (position == own)
+        bias[pl.ds(row, 1), :] = jnp.where(live, 0.0, masked_score)
+        return carry
+
+    position = lax.broadcasted_iota(jnp.int32, (1, tokens), 1)
+    in_block, at_block = position % block_len, position // block_len
     for request in range(requests):
         for chunk in range(chunks):
             load(request, chunk).start()
         if request == 0:
+            for copy in tails:
+                copy.start()
             for copy in metas:
                 copy.wait()
             meta = (parents, table, lengths)
-            begin_picks([], now, rows, me, meta, blocked, [], chosen, pick_sem)
-            position = lax.broadcasted_iota(jnp.int32, (1, tokens), 1)
-            in_block, at_block = position % block_len, position // block_len
-
-            def mask(row, carry):
-                parent = parents[row]
-                tail = lengths[parent]
-                reach = jnp.zeros((1, tokens), jnp.int32)
-                for depth in range(table.shape[0]):
-                    block = table[depth, parent] - me * blocks
-                    reach = jnp.where(at_block == block, tail - depth * block_len, reach)
-                own = row - me * rows
-                own = jnp.where((own >= 0) & (own < rows), own + old, -1)
-                live = (in_block < reach) | (position == own)
-                bias[pl.ds(row, 1), :] = jnp.where(live, 0.0, masked_score)
-                return carry
-
-            lax.fori_loop(0, bias.shape[0], mask, 0)
+            begin_picks([], now, rows, me, meta, blocked, [], buffers, pick_sem)
+
+        def step(chunk, carry):
+            load(request, chunk).wait()
+            split(request, chunk)
+            return carry
+
+        lax.fori_loop(0, chunks, step, 0)
+        if request == 0:
             for copy in tails:
                 copy.wait()
-
-        def step(chunk, carry):
-            @pl.when(chunk < chunks)
-            def _():
-                load(request, chunk).wait()
-
-            split(request, chunk)
-            return carry
-
-        lax.fori_loop(0, chunks + 1, step, 0)
+        split(request, chunks)
+        if request == 0:
+            end_picks(blocked, buffers, pick_sem)
+            sends = [
+                pltpu.make_async_copy(source, target, sent_sem.at[index])
+                for index, (source, target) in enumerate(zip(buffers, chosen))
+            ]
+            for copy in sends:
+                copy.start()
+            lax.fori_loop(0, bias.shape[0], mask, 0)
         for chunk in range(chunks + 1):
             store(request, chunk).wait()
-    end_picks(blocked, chosen, pick_sem)
+    for copy in sends:
+        copy.wait()
 
 
 def unpack(now, devices, meta, prefix_kv, pool, new_kv):
@@ -342,13 +350,13 @@
         functools.partial(unpack_kernel, now, rows, block_len),
         name="unpack",
         in_specs=[hbm] * 7,
-        out_specs=[vmem, hbm] + [vmem] * (1 + len(shapes)),
+        out_specs=[vmem, hbm, vmem] + [hbm] * len(shapes),
         out_shape=[
             jax.ShapeDtypeStruct((requests,) + whole, bf16),
             pltpu.HBM((requests,) + whole, bf16),
             jax.ShapeDtypeStruct((row_total, tokens), f32),
         ]
-        + shapes,
+        + [pltpu.HBM(shape.shape, shape.dtype) for shape in shapes],
         scratch_shapes=[
             pltpu.VMEM((chunks + 1, size, HD), bf16),
             pltpu.VMEM((2, size, HD), f32),
@@ -356,8 +364,9 @@
             pltpu.SemaphoreType.DMA((chunks,)),
             pltpu.SemaphoreType.DMA((3,)),
             pltpu.SemaphoreType.DMA((chunks + 1,)),
-            pltpu.SemaphoreType.DMA(semaphores),
         ]
+        + [pltpu.VMEM(shape.shape, shape.dtype) for shape in shapes]
+        + [pltpu.SemaphoreType.DMA(semaphores), pltpu.SemaphoreType.DMA((len(shapes),))]
         + meta_scratch(meta),
         compiler_params=pltpu.CompilerParams(vmem_limit_bytes=VMEM_LIMIT),
         cost_estimate=pl.CostEstimate(
@@ -378,6 +387,7 @@
     factor = HD ** (-0.5) * math.log2(math.e)
     contract = (((1,), (1,)), ((), ()))
     lane = lax.broadcasted_iota(jnp.int32, (count, HD), 1)
+    stat_row = lax.broadcasted_iota(jnp.int32, (STAT_ROWS, HD), 0)
 
     def load(request, head):
         return pltpu.make_async_copy(values.at[request, head], value_buffer.at[head], sem.at[head])
@@ -386,41 +396,45 @@
         for head in range(KVH):
             load(request, head).start()
         span = pl.ds(request * beams, beams)
-        wide[...] = query[span].astype(f32).reshape(beams * HQ, HD)
-        for head in range(HQ):
-            stacks[head * beams : (head + 1) * beams, :] = wide[
-                pl.ds(head, beams, stride=HQ), :
-            ].astype(bf16)
-
-        def one(head):
+        stacks[...] = pltpu.einshape("bhd->hbd", query[span]).reshape(HQ * beams, HD)
+
+        def scores(head):
             stacked = stacks[pl.ds(pl.multiple_of(head * count, count), count), :]
             score = lax.dot_general(
                 stacked, keys[request, head], contract, preferred_element_type=f32
             )
             tail = score[:, length:] + jnp.concatenate([bias[span, :]] * groups, axis=0)
-            score = jnp.concatenate([score[:, :length], tail], axis=1)
+            return jnp.concatenate([score[:, :length], tail], axis=1)
+
+        def softmax(score):
             top = jnp.max(score, axis=1, keepdims=True)
             weight = jnp.exp2((score - top) * factor)
-            total = jnp.sum(weight, axis=1, keepdims=True)
-            result = jnp.dot(weight.astype(bf16), value_buffer[head], preferred_element_type=f32)
-            packed = jnp.zeros((count, HD), f32)
-            for at, term in enumerate(pieces(top) + pieces(total)):
-                packed = jnp.where(lane == at, term, packed)
+            return weight.astype(bf16), top, jnp.sum(weight, axis=1, keepdims=True)
+
+        def finish(head, weight, top, total):
+            result = jnp.dot(weight, value_buffer[head], preferred_element_type=f32)
+            packed = jnp.where(lane == 0, top, total)
             if count < HD:
                 packed = jnp.concatenate([packed, jnp.zeros((HD - count, HD), f32)], axis=0)
-            stats = packed.T
+            flat = packed.T
+            stats = jnp.zeros((STAT_ROWS, HD), f32)
+            for at, term in enumerate(pieces(flat[0:1]) + pieces(flat[1:2])):
+                stats = jnp.where(stat_row == at, term, stats)
             for t in range(targets):
                 at = head * targets + t
                 out[at, request, :share, :] = result[t * share : (t + 1) * share].astype(bf16)
                 mine = stats if t == 0 else pltpu.roll(stats, HD - t * share, 1)
-                out[at, request, share : share + STAT_ROWS, :] = mine[:STAT_ROWS].astype(bf16)
+                out[at, request, share : share + STAT_ROWS, :] = mine.astype(bf16)
 
         def some(step, carry):
             heads = [step * AT_ONCE + i for i in range(AT_ONCE)]
+            ready = softmax(scores(heads[0]))
             for head in heads:
                 load(request, head).wait()
-            for head in heads:
-                one(head)
+            for index, head in enumerate(heads):
+                ahead = scores(heads[index + 1]) if index + 1 < AT_ONCE else None
+                finish(head, *ready)
+                ready = ahead if ahead is None else softmax(ahead)
             return carry
 
         lax.fori_loop(0, KVH // AT_ONCE, some, 0)

time: 79.2 us -> 78 us (0.985)
  Pallas kernels: 20.3 us -> 19.2 us
    pallas_call x1, Pallas kernels: 5.14 us -> 3.88 us  [attend(): pl.pallas_call(attend_kernel, name='attend', in_specs=[vmem, vmem, hbm, v...]
where the time goes in v7:
time: 78 us; the launch traced here: 77.4 us
  waiting for transfers between devices  21.9 us (28%)
  starting transfers between devices  20.7 us (27%)
  Pallas kernels  19.2 us (25%)
  blocking collectives  13.4 us (17%)
    ppermute x5, waiting for transfers between devices, move(): lax.ppermute(block, 'ctx', [(i, i ^ at + 1 << first) for i in range(devic...  18 us
    all_to_all x1, blocking collectives, exchange(): return lax.all_to_all(array, 'ctx', split_axis=0, concat_axis=0, tiled=True)  13.4 us
    all_to_all x2, starting transfers between devices, exchange(): return lax.all_to_all(array, 'ctx', split_axis=0, concat_axis=0, tiled=True)  11.9 us
    ppermute x5, starting transfers between devices, move(): lax.ppermute(block, 'ctx', [(i, i ^ at + 1 << first) for i in range(devic...  8.85 us
    pallas_call x1, Pallas kernels, unpack(): pl.pallas_call(functools.partial(unpack_kernel, now, rows, block_len), na...  5.98 us
    pallas_call x1, Pallas kernels, project(): pl.pallas_call(project_kernel, name='project', in_specs=[pl.BlockSpec(mem...  4.56 us
    all_to_all x2, waiting for transfers between devices, exchange(): return lax.all_to_all(array, 'ctx', split_axis=0, concat_axis=0, tiled=True)  3.89 us
    pallas_call x1, Pallas kernels, attend(): pl.pallas_call(attend_kernel, name='attend', in_specs=[vmem, vmem, hbm, v...  3.88 us
  transfers between devices with their start and end apart: 7, of which 6 were waited for; matrix products, arithmetic and copies ran while one was open for 0% of the time, Pallas kernels for 13%

profile of v7, /device:TPU:0, one launch (start us, length us, event | category | flops | bytes accessed | tf_op | source)
XLA Modules:
  0.0 77.4 jit_solution(13483582444639399288)
XLA Ops:
  0.6 0.0 copy-start
  0.6 0.7 copy-done
  1.4 0.7 ask.1
  2.1 8.3 %all-to-all-start = ((bf16[16,1,64,128]{3,2,1,0:T(8,128)(2,1)}), bf16[16,1,64,128]{3,2,1,0:T(8,128)(2,1)S(1)}, u32[]{:S(2)}, u32[]{:S(2)}) async-start(bf16[16,1,64,128]{3,2,1,0:T(8,128)(2,1)} %ask.1), calls=%async_computation | async-start | bytes 524288 | tf_op jit(solution)/shard_map/all_to_all | solution.py:543
  10.5 6.0 %unpack.1 = (bf16[1,8,1152,128]{3,2,1,0:T(8,128)(2,1)S(1)}, bf16[1,8,1152,128]{3,2,1,0:T(8,128)(2,1)}, f32[16,128]{1,0:T(8,128)S(1)}, bf16[4,16,2,1024]{3,2,1,0:...) custom-call(s32[16]{0:T(128)} %parents_in.7, s32[4,16]{1,0:T(4,128)} %bitcast.22, ...), custom_call_target="tpu_custom_call" | custom-call | bytes 6291456 | tf_op jit(solution)/shard_map/unpack/pallas_call | solution.py:349
  16.5 3.9 %all-to-all-done = bf16[16,1,64,128]{3,2,1,0:T(8,128)(2,1)S(1)} async-done(((bf16[16,1,64,128]{3,2,1,0:T(8,128)(2,1)}), bf16[16,1,64,128]{3,2,1,0:T(8,128)(2,1)S(1)}, u32[]{:S(2)}, u32[]{:S(2)}) %all-to-all-start) | async-done | bytes 262176 | tf_op jit(solution)/shard_map/all_to_all | solution.py:543
  20.4 3.9 %attend.1 = bf16[16,1,72,128]{3,2,1,0:T(8,128)(2,1)S(1)} custom-call(bf16[16,64,128]{2,1,0:T(8,128)(2,1)S(1)} %bitcast.18, bf16[1,8,1152,128]{3,2,1,0:T(8,128)(2,1)S(1)} %get-tuple-element.8.keys, bf16[1,8,1152,128]{3,2,1,0:T(8,128)(2,1)} %get-tuple-element.9.values, f32[16,128]{1,0:T(8,128)S(1)} %get-tuple-element.10.bias), custom_call_target="tpu_custom_call" | custom-call | flops 603979776 | bytes 4718592 | tf_op jit(solution)/shard_map/attend/pallas_call | solution.py:450
  24.2 13.4 %all_to_all.15.partial = bf16[16,1,72,128]{3,2,1,0:T(8,128)(2,1)S(1)} all-to-all(bf16[16,1,72,128]{3,2,1,0:T(8,128)(2,1)S(1)} %attend.1), channel_id=1, replica_groups=mesh['req'=2,'ctx'=16] {'ctx'}, dimensions={0} | all-to-all | bytes 589824 | tf_op jit(solution)/shard_map/all_to_all | solution.py:543
  37.7 0.0 copy-start.4
  37.7 0.0 copy-start.3
  37.7 0.0 copy-start.2
  37.7 0.0 copy-start.1
  37.7 4.6 %project.1 = bf16[16,64,128]{2,1,0:T(8,128)(2,1)} custom-call(bf16[16,1,72,128]{3,2,1,0:T(8,128)(2,1)S(1)} %all_to_all.15.partial, bf16[512,8192]{1,0:T(8,128)(2,1)} %weight.1), custom_call_target="tpu_custom_call" | custom-call | flops 134217728 | bytes 8388608 | tf_op jit(solution)/shard_map/project/pallas_call | solution.py:520
  42.2 3.5 %all-to-all-start.2 = ((bf16[16,64,128]{2,1,0:T(8,128)(2,1)}), bf16[16,64,128]{2,1,0:T(8,128)(2,1)S(1)}, u32[]{:S(2)}, u32[]{:S(2)}) async-start(bf16[16,64,128]{2,1,0:T(8,128)(2,1)} %project.1), calls=%async_computation.2 | async-start | bytes 524288 | tf_op jit(solution)/shard_map/all_to_all | solution.py:543
  45.8 0.0 copy-done.4
  45.8 1.9 %collective-permute-start = (bf16[4,16,2,1024]{3,2,1,0:T(2,128)(2,1)S(1)}, bf16[4,16,2,1024]{3,2,1,0:T(2,128)(2,1)S(1)}, u32[]{:S(2)}, u32[]{:S(2)}) collective-permute-start(bf16[4,16,2,1024]{3,2,1,0:T(2,128)(2,1)S(1)} %copy-done.4), channel_id=1, source_target_pairs={{0,1},{1,0},{2,3},{3,2},{4,5},{5,4},{6,7},{7,6},{8,9},{9,8},{10,11... | collective-permute-start | bytes 786440 | tf_op jit(solution)/shard_map/ppermute | solution.py:559
  47.7 0.0 copy-done.3
  47.7 1.5 %collective-permute-start.1 = (bf16[4,16,2,1024]{3,2,1,0:T(2,128)(2,1)S(1)}, bf16[4,16,2,1024]{3,2,1,0:T(2,128)(2,1)S(1)}, u32[]{:S(2)}, u32[]{:S(2)}) collective-permute-start(bf16[4,16,2,1024]{3,2,1,0:T(2,128)(2,1)S(1)} %copy-done.3), channel_id=1, source_target_pairs={{0,2},{1,3},{2,0},{3,1},{4,6},{5,7},{6,4},{7,5},{8,10},{9,11},{10,... | collective-permute-start | bytes 786440 | tf_op jit(solution)/shard_map/ppermute | solution.py:559
  49.2 0.0 copy-done.2
  49.2 0.2 collective-permute-start.2
  49.4 8.1 %collective-permute-done.refs_0_ = bf16[4,16,2,1024]{3,2,1,0:T(2,128)(2,1)S(1)} collective-permute-done((bf16[4,16,2,1024]{3,2,1,0:T(2,128)(2,1)S(1)}, bf16[4,16,2,1024]{3,2,1,0:T(2,128)(2,1)S(1)}, u32[]{:S(2)}, u32[]{:S(2)}) %collective-permute-start) | collective-permute-done | bytes 262176 | tf_op jit(solution)/shard_map/ppermute | solution.py:559
  57.4 3.3 %collective-permute-done.1.refs_1_ = bf16[4,16,2,1024]{3,2,1,0:T(2,128)(2,1)S(1)} collective-permute-done((bf16[4,16,2,1024]{3,2,1,0:T(2,128)(2,1)S(1)}, bf16[4,16,2,1024]{3,2,1,0:T(2,128)(2,1)S(1)}, u32[]{:S(2)}, u32[]{:S(2)}) %collective-permute-start.1) | collective-permute-done | bytes 262176 | tf_op jit(solution)/shard_map/ppermute | solution.py:559
  60.8 1.4 %collective-permute-done.2.refs_2_ = bf16[4,16,2,1024]{3,2,1,0:T(2,128)(2,1)S(1)} collective-permute-done((bf16[4,16,2,1024]{3,2,1,0:T(2,128)(2,1)S(1)}, bf16[4,16,2,1024]{3,2,1,0:T(2,128)(2,1)S(1)}, u32[]{:S(2)}, u32[]{:S(2)}) %collective-permute-start.2) | collective-permute-done | bytes 262176 | tf_op jit(solution)/shard_map/ppermute | solution.py:559
  62.2 1.0 %pick.2 = bf16[2,16,2,1024]{3,2,1,0:T(2,128)(2,1)S(1)} custom-call(s32[16]{0:T(128)} %parents_in.7, s32[4,16]{1,0:T(4,128)} %bitcast.23, s32[16]{0:T(128)} %lengths_in.7, bf16[8,16,2,1024]{3,2,1,0:T(2,128)(2,1)} %pool.5, bf16[4,16,2,1024]{3,2,1,0:T(2,128)(2,1)S(1)} %collective-permute-done.refs_0_, ...), custom_call_target="tpu_custom_call" | custom-call | bytes 4194304 | tf_op jit(solution)/shard_map/pick/pallas_call | solution.py:148
  63.2 2.1 %collective-permute-start.3 = (bf16[2,16,2,1024]{3,2,1,0:T(2,128)(2,1)S(1)}, bf16[2,16,2,1024]{3,2,1,0:T(2,128)(2,1)S(1)}, u32[]{:S(2)}, u32[]{:S(2)}) collective-permute-start(bf16[2,16,2,1024]{3,2,1,0:T(2,128)(2,1)S(1)} %pick.2), channel_id=1, source_target_pairs={{0,4},{1,5},{2,6},{3,7},{4,0},{5,1},{6,2},{7,3},{8,12},{9,13},{10,... | collective-permute-start | bytes 393224 | tf_op jit(solution)/shard_map/ppermute | solution.py:559
  65.4 2.9 %collective-permute-done.3.refs_3_ = bf16[2,16,2,1024]{3,2,1,0:T(2,128)(2,1)S(1)} collective-permute-done((bf16[2,16,2,1024]{3,2,1,0:T(2,128)(2,1)S(1)}, bf16[2,16,2,1024]{3,2,1,0:T(2,128)(2,1)S(1)}, u32[]{:S(2)}, u32[]{:S(2)}) %collective-permute-start.3) | collective-permute-done | bytes 131104 | tf_op jit(solution)/shard_map/ppermute | solution.py:559
  68.3 0.9 %pick.3 = bf16[1,16,2,1024]{3,2,1,0:T(2,128)(2,1)S(1)} custom-call(s32[16]{0:T(128)} %parents_in.7, s32[4,16]{1,0:T(4,128)} %bitcast.24, s32[16]{0:T(128)} %lengths_in.7, bf16[8,16,2,1024]{3,2,1,0:T(2,128)(2,1)} %pool.5, bf16[4,16,2,1024]{3,2,1,0:T(2,128)(2,1)S(1)} %collective-permute-done.refs_0_, ...), custom_call_target="tpu_custom_call" | custom-call | bytes 4194304 | tf_op jit(solution)/shard_map/pick/pallas_call | solution.py:148
  69.2 3.2 %collective-permute-start.4 = (bf16[1,16,2,1024]{3,2,1,0:T(2,128)(2,1)S(1)}, bf16[1,16,2,1024]{3,2,1,0:T(2,128)(2,1)S(1)}, u32[]{:S(2)}, u32[]{:S(2)}) collective-permute-start(bf16[1,16,2,1024]{3,2,1,0:T(2,128)(2,1)S(1)} %pick.3), channel_id=1, source_target_pairs={{0,8},{1,9},{2,10},{3,11},{4,12},{5,13},{6,14},{7,15},{8,0},{9,1},... | collective-permute-start | bytes 196616 | tf_op jit(solution)/shard_map/ppermute | solution.py:559
  72.4 2.2 %collective-permute-done.4.refs_4_ = bf16[1,16,2,1024]{3,2,1,0:T(2,128)(2,1)S(1)} collective-permute-done((bf16[1,16,2,1024]{3,2,1,0:T(2,128)(2,1)S(1)}, bf16[1,16,2,1024]{3,2,1,0:T(2,128)(2,1)S(1)}, u32[]{:S(2)}, u32[]{:S(2)}) %collective-permute-start.4) | collective-permute-done | bytes 65568 | tf_op jit(solution)/shard_map/ppermute | solution.py:559
  74.6 0.0 copy-done.1
  74.6 2.2 %place.1 = bf16[8,16,2,1024]{3,2,1,0:T(2,128)(2,1)} custom-call(s32[16]{0:T(128)} %parents_in.7, s32[4,16]{1,0:T(4,128)} %bitcast.25, s32[16]{0:T(128)} %lengths_in.7, s32[16]{0:T(128)} %fresh_in.1, bf16[1,2,1024]{2,1,0:T(2,128)(2,1)S(1)} %copy-done.1, bf16[8,16,2,1024]{3,2,1,0:T(2,128)(2,1)} %pool.5, ...), custom_call_target="tpu_custom_call" | custom-call | bytes 1048576 | tf_op jit(solution)/shard_map/place/pallas_call | solution.py:195
  76.8 0.0 all-to-all-done.2
  76.8 0.7 convert_reduce_fusion
Async XLA Ops:
  0.6 0.8 copy-start
  2.1 18.2 %all-to-all-start = ((bf16[16,1,64,128]{3,2,1,0:T(8,128)(2,1)}), bf16[16,1,64,128]{3,2,1,0:T(8,128)(2,1)S(1)}, u32[]{:S(2)}, u32[]{:S(2)}) async-start(bf16[16,1,64,128]{3,2,1,0:T(8,128)(2,1)} %ask.1), calls=%async_computation | async-start | bytes 524288 | tf_op jit(solution)/shard_map/all_to_all | solution.py:543
  37.7 8.1 %copy-start.4 = (bf16[4,16,2,1024]{3,2,1,0:T(2,128)(2,1)S(1)}, bf16[4,16,2,1024]{3,2,1,0:T(2,128)(2,1)}, u32[]{:S(2)}) copy-start(bf16[4,16,2,1024]{3,2,1,0:T(2,128)(2,1)} %get-tuple-element.11) | copy-start | bytes 786436
  37.7 10.0 %copy-start.3 = (bf16[4,16,2,1024]{3,2,1,0:T(2,128)(2,1)S(1)}, bf16[4,16,2,1024]{3,2,1,0:T(2,128)(2,1)}, u32[]{:S(2)}) copy-start(bf16[4,16,2,1024]{3,2,1,0:T(2,128)(2,1)} %get-tuple-element.12) | copy-start | bytes 786436
  37.7 11.5 %copy-start.2 = (bf16[4,16,2,1024]{3,2,1,0:T(2,128)(2,1)S(1)}, bf16[4,16,2,1024]{3,2,1,0:T(2,128)(2,1)}, u32[]{:S(2)}) copy-start(bf16[4,16,2,1024]{3,2,1,0:T(2,128)(2,1)} %get-tuple-element.13) | copy-start | bytes 786436
  37.7 36.9 %copy-start.1 = (bf16[1,2,1024]{2,1,0:T(2,128)(2,1)S(1)}, bf16[1,2,1024]{2,1,0:T(2,128)(2,1)}, u32[]{:S(2)}) copy-start(bf16[1,2,1024]{2,1,0:T(2,128)(2,1)} %new_kv.1) | copy-start | bytes 12292
  42.2 34.5 %all-to-all-start.2 = ((bf16[16,64,128]{2,1,0:T(8,128)(2,1)}), bf16[16,64,128]{2,1,0:T(8,128)(2,1)S(1)}, u32[]{:S(2)}, u32[]{:S(2)}) async-start(bf16[16,64,128]{2,1,0:T(8,128)(2,1)} %project.1), calls=%async_computation.2 | async-start | bytes 524288 | tf_op jit(solution)/shard_map/all_to_all | solution.py:543
  45.8 11.6 %collective-permute-start = (bf16[4,16,2,1024]{3,2,1,0:T(2,128)(2,1)S(1)}, bf16[4,16,2,1024]{3,2,1,0:T(2,128)(2,1)S(1)}, u32[]{:S(2)}, u32[]{:S(2)}) collective-permute-start(bf16[4,16,2,1024]{3,2,1,0:T(2,128)(2,1)S(1)} %copy-done.4), channel_id=1, source_target_pairs={{0,1},{1,0},{2,3},{3,2},{4,5},{5,4},{6,7},{7,6},{8,9},{9,8},{10,11... | collective-permute-start | bytes 786440 | tf_op jit(solution)/shard_map/ppermute | solution.py:559
  47.7 13.1 %collective-permute-start.1 = (bf16[4,16,2,1024]{3,2,1,0:T(2,128)(2,1)S(1)}, bf16[4,16,2,1024]{3,2,1,0:T(2,128)(2,1)S(1)}, u32[]{:S(2)}, u32[]{:S(2)}) collective-permute-start(bf16[4,16,2,1024]{3,2,1,0:T(2,128)(2,1)S(1)} %copy-done.3), channel_id=1, source_target_pairs={{0,2},{1,3},{2,0},{3,1},{4,6},{5,7},{6,4},{7,5},{8,10},{9,11},{10,... | collective-permute-start | bytes 786440 | tf_op jit(solution)/shard_map/ppermute | solution.py:559
  49.2 13.0 %collective-permute-start.2 = (bf16[4,16,2,1024]{3,2,1,0:T(2,128)(2,1)S(1)}, bf16[4,16,2,1024]{3,2,1,0:T(2,128)(2,1)S(1)}, u32[]{:S(2)}, u32[]{:S(2)}) collective-permute-start(bf16[4,16,2,1024]{3,2,1,0:T(2,128)(2,1)S(1)} %copy-done.2), channel_id=1, source_target_pairs={{0,3},{1,2},{2,1},{3,0},{4,7},{5,6},{6,5},{7,4},{8,11},{9,10},{10,... | collective-permute-start | bytes 786440 | tf_op jit(solution)/shard_map/ppermute | solution.py:559
  63.2 5.1 %collective-permute-start.3 = (bf16[2,16,2,1024]{3,2,1,0:T(2,128)(2,1)S(1)}, bf16[2,16,2,1024]{3,2,1,0:T(2,128)(2,1)S(1)}, u32[]{:S(2)}, u32[]{:S(2)}) collective-permute-start(bf16[2,16,2,1024]{3,2,1,0:T(2,128)(2,1)S(1)} %pick.2), channel_id=1, source_target_pairs={{0,4},{1,5},{2,6},{3,7},{4,0},{5,1},{6,2},{7,3},{8,12},{9,13},{10,... | collective-permute-start | bytes 393224 | tf_op jit(solution)/shard_map/ppermute | solution.py:559
  69.2 5.4 %collective-permute-start.4 = (bf16[1,16,2,1024]{3,2,1,0:T(2,128)(2,1)S(1)}, bf16[1,16,2,1024]{3,2,1,0:T(2,128)(2,1)S(1)}, u32[]{:S(2)}, u32[]{:S(2)}) collective-permute-start(bf16[1,16,2,1024]{3,2,1,0:T(2,128)(2,1)S(1)} %pick.3), channel_id=1, source_target_pairs={{0,8},{1,9},{2,10},{3,11},{4,12},{5,13},{6,14},{7,15},{8,0},{9,1},... | collective-permute-start | bytes 196616 | tf_op jit(solution)/shard_map/ppermute | solution.py:559

commit v8 on v7

--- a/solution.py
+++ b/solution.py
@@ -15,6 +15,8 @@
 CAP = 2
 
 STAT_ROWS = 8
+PARTS = 8
+WARM = 2
 AT_ONCE = 8
 VMEM_LIMIT = 20 << 20
 masked_score = -1e30
@@ -157,51 +159,111 @@
     )(*map(in_hbm, meta), in_hbm(pool), *arrived)
 
 
-def place_kernel(rounds, rows, parents_in, table_in, lengths_in, fresh_in, new_kv, pool, *refs):
-    channels = len(channels_of(rounds))
-    arrived, (out, parents, table, lengths, fresh, meta_sem, sem) = refs[:channels], refs[channels:]
+def base_kernel(
+    rounds, rows, parents_in, table_in, lengths_in, fresh_in, new_in, pool, *refs
+):
+    channels = len(channels_of(rounds)) - 1
+    arrived, (whole, tail, mask, *refs) = refs[:channels], refs[channels:]
+    old_blocks, new_kv, parents, table, lengths, fresh, meta_sem, sems = refs
     me = lax.axis_index("ctx")
     pool_dev, block_len = pool.shape[:2]
-    whole = pltpu.make_async_copy(pool, out, sem)
-    whole.start()
+    old = pool_dev - CAP
+    zero = jnp.zeros(mask.shape[3:], bf16)
+    one = jnp.ones(mask.shape[3:], bf16)
+    first = pltpu.make_async_copy(pool.at[pl.ds(0, old)], old_blocks, sems.at[0])
+    last = pltpu.make_async_copy(pool.at[pl.ds(old, CAP)], tail, sems.at[1])
+    token_copy = pltpu.make_async_copy(new_in, new_kv, sems.at[2])
     sources = (parents_in, table_in, lengths_in, fresh_in)
-    for copy in load_meta(sources, (parents, table, lengths, fresh), meta_sem):
+    metas = load_meta(sources, (parents, table, lengths, fresh), meta_sem)
+    for copy in (first, last, token_copy):
+        copy.start()
+    mask[...] = jnp.zeros(mask.shape, bf16)
+    for copy in metas:
         copy.wait()
-    whole.wait()
+    token_copy.wait()
+    last.wait()
+    first.wait()
+    send = pltpu.make_async_copy(old_blocks, whole.at[pl.ds(0, old)], sems.at[0])
+    send.start()
+    bit = rounds[-1][0]
     for part in range(rows):
         row = me * rows + part
         length, source = source_of(row, parents, table, lengths, block_len)
-        slot = fresh[row] - me * pool_dev
-        fetch_block(rounds, me, source, me, part, rows, pool, arrived, out.at[slot], sem)
-        pltpu.make_async_copy(pool.at[0], out.at[slot], sem).wait()
+        slot = fresh[row] - me * pool_dev - old
+        fetch_block(
+            rounds[:-1], me, source, me, part, rows, pool, arrived, tail.at[slot], sems.at[1]
+        )
+        pltpu.make_async_copy(pool.at[0], tail.at[slot], sems.at[1]).wait()
         offset = length % block_len
+        awaited = (((source // pool_dev) ^ me) >> bit) & 1
 
         def token(at, carry):
+            @pl.when((at < offset) & (awaited == 1))
+            def _():
+                mask[part, slot, at] = one
+
             @pl.when(at == offset)
             def _():
-                out[slot, at] = new_kv[part]
+                tail[slot, at] = new_kv[part]
 
             @pl.when(at > offset)
             def _():
-                out[slot, at] = jnp.zeros(out.shape[2:], bf16)
+                tail[slot, at] = zero
 
             return carry
 
         lax.fori_loop(0, block_len, token, 0)
-
-
-def place(rounds, rows, meta, new_kv, pool, arrived):
+    send.wait()
+
+
+def base(rounds, rows, meta, new_kv, pool, arrived):
     vmem, hbm = pl.BlockSpec(memory_space=pltpu.VMEM), pl.BlockSpec(memory_space=pltpu.HBM)
-    return pl.pallas_call(
-        functools.partial(place_kernel, rounds, rows),
+    block = pool.shape[1:]
+    return pl.pallas_call(
+        functools.partial(base_kernel, rounds, rows),
+        name="base",
+        in_specs=[hbm] * 6 + [pl.BlockSpec(memory_space=pl.ANY)] * len(arrived),
+        out_specs=[hbm, vmem, vmem],
+        out_shape=[
+            pltpu.HBM(pool.shape, bf16),
+            jax.ShapeDtypeStruct((CAP,) + block, bf16),
+            jax.ShapeDtypeStruct((rows, CAP) + block, bf16),
+        ],
+        scratch_shapes=[
+            pltpu.VMEM((pool.shape[0] - CAP,) + block, bf16),
+            pltpu.VMEM(new_kv.shape, bf16),
+        ]
+        + meta_scratch(meta)
+        + [pltpu.SemaphoreType.DMA((3,))],
+        compiler_params=pltpu.CompilerParams(vmem_limit_bytes=VMEM_LIMIT),
+        cost_estimate=pl.CostEstimate(flops=0, bytes_accessed=4 * pool.size, transcendentals=0),
+    )(*map(in_hbm, meta + (new_kv, pool)), *arrived)
+
+
+def place_kernel(whole, tail, mask, last, out, merged, sem):
+    old = out.shape[0] - CAP
+    block = tail[...]
+    for part in range(mask.shape[0]):
+        block = jnp.where(mask[part] != 0, last[part][None], block)
+    merged[...] = block
+    copy = pltpu.make_async_copy(merged, out.at[pl.ds(old, CAP)], sem)
+    copy.start()
+    copy.wait()
+
+
+def place(whole, tail, mask, last):
+    vmem, hbm = pl.BlockSpec(memory_space=pltpu.VMEM), pl.BlockSpec(memory_space=pltpu.HBM)
+    return pl.pallas_call(
+        place_kernel,
         name="place",
-        in_specs=[hbm] * 4 + [vmem, hbm] + [pl.BlockSpec(memory_space=pl.ANY)] * len(arrived),
-        out_specs=vmem,
-        out_shape=jax.ShapeDtypeStruct(pool.shape, bf16),
-        scratch_shapes=meta_scratch(meta) + [pltpu.SemaphoreType.DMA],
-        compiler_params=pltpu.CompilerParams(vmem_limit_bytes=VMEM_LIMIT),
-        cost_estimate=pl.CostEstimate(flops=0, bytes_accessed=4 * pool.size, transcendentals=0),
-    )(*map(in_hbm, meta), new_kv, in_hbm(pool), *arrived)
+        in_specs=[hbm, vmem, vmem, vmem],
+        out_specs=hbm,
+        out_shape=pltpu.HBM(whole.shape, bf16),
+        input_output_aliases={0: 0},
+        scratch_shapes=[pltpu.VMEM(tail.shape, bf16), pltpu.SemaphoreType.DMA],
+        compiler_params=pltpu.CompilerParams(vmem_limit_bytes=VMEM_LIMIT),
+        cost_estimate=pl.CostEstimate(flops=0, bytes_accessed=4 * tail.size, transcendentals=0),
+    )(whole, tail, mask, last)
 
 
 def pieces(value):
@@ -468,22 +530,24 @@
     )(everyone, keys, in_hbm(values), bias)
 
 
-def project_kernel(partial, weight, out, attended, scratch, buffer, sem):
+def project_kernel(partial, warmed, weight, out, attended, scratch, buffer, sem):
     devices, requests, rows, _ = partial.shape
     share = rows - STAT_ROWS
     row_total = out.shape[0]
     beams = row_total // requests
     own = share // beams
     chunks = out.shape[1]
-    parts = sem.shape[0]
-    step = weight.shape[1] // parts
+    ready = warmed.shape[0]
+    step = warmed.shape[2]
+    parts = ready + sem.shape[0]
     factor = HD ** (-0.5) * math.log2(math.e)
 
     def load(part):
         lanes = pl.ds(part * step, step)
-        return pltpu.make_async_copy(weight.at[:, lanes], buffer.at[part], sem.at[part])
-
-    for part in range(parts):
+        at = part - ready
+        return pltpu.make_async_copy(weight.at[:, lanes], buffer.at[at], sem.at[at])
+
+    for part in range(ready, parts):
         load(part).start()
 
     for r in range(requests):
@@ -504,8 +568,10 @@
             ].astype(bf16)
 
     for part in range(parts):
-        load(part).wait()
-        product = jnp.dot(attended[...], buffer[part], preferred_element_type=f32)
+        if part >= ready:
+            load(part).wait()
+        block = warmed[part] if part < ready else buffer[part - ready]
+        product = jnp.dot(attended[...], block, preferred_element_type=f32)
         for c in range(step // HD):
             scratch[pl.ds(part * (step // HD) + c, row_total, stride=chunks), :] = product[
                 :, c * HD : (c + 1) * HD
@@ -514,29 +580,56 @@
         out[row] = scratch[row * chunks : (row + 1) * chunks, :].astype(bf16)
 
 
-def project(partial, weight, row_total):
+def warm_kernel(weight, out, sem):
+    parts, _, step = out.shape
+    copies = [
+        pltpu.make_async_copy(weight.at[:, pl.ds(i * step, step)], out.at[i], sem.at[i])
+        for i in range(parts)
+    ]
+    for copy in copies:
+        copy.start()
+    for copy in copies:
+        copy.wait()
+
+
+def warm(weight):
     depth, width = weight.shape
-    parts = max(1, width // 1024)
+    step = width // PARTS
+    return pl.pallas_call(
+        warm_kernel,
+        name="warm",
+        in_specs=[pl.BlockSpec(memory_space=pltpu.HBM)],
+        out_specs=pl.BlockSpec(memory_space=pltpu.VMEM),
+        out_shape=jax.ShapeDtypeStruct((WARM, depth, step), bf16),
+        scratch_shapes=[pltpu.SemaphoreType.DMA((WARM,))],
+        compiler_params=pltpu.CompilerParams(vmem_limit_bytes=VMEM_LIMIT),
+        cost_estimate=pl.CostEstimate(
+            flops=0, bytes_accessed=4 * WARM * depth * step, transcendentals=0
+        ),
+    )(in_hbm(weight))
+
+
+def project(partial, warmed, weight, row_total):
+    depth, width = weight.shape
+    cold = PARTS - WARM
+    vmem, hbm = pl.BlockSpec(memory_space=pltpu.VMEM), pl.BlockSpec(memory_space=pltpu.HBM)
     return pl.pallas_call(
         project_kernel,
         name="project",
-        in_specs=[
-            pl.BlockSpec(memory_space=pltpu.VMEM),
-            pl.BlockSpec(memory_space=pltpu.HBM),
-        ],
-        out_specs=pl.BlockSpec(memory_space=pltpu.VMEM),
+        in_specs=[vmem, vmem, hbm],
+        out_specs=vmem,
         out_shape=jax.ShapeDtypeStruct((row_total, width // HD, HD), bf16),
         scratch_shapes=[
             pltpu.VMEM((row_total, depth), bf16),
             pltpu.VMEM((row_total * (width // HD), HD), f32),
-            pltpu.VMEM((parts, depth, width // parts), bf16),
-            pltpu.SemaphoreType.DMA((parts,)),
+            pltpu.VMEM((cold, depth, width // PARTS), bf16),
+            pltpu.SemaphoreType.DMA((cold,)),
         ],
         compiler_params=pltpu.CompilerParams(vmem_limit_bytes=VMEM_LIMIT),
         cost_estimate=pl.CostEstimate(
             flops=2 * row_total * depth * width, bytes_accessed=2 * weight.size, transcendentals=0
         ),
-    )(partial, in_hbm(weight))
+    )(partial, warmed, in_hbm(weight))
 
 
 def exchange(array):
@@ -571,10 +664,12 @@
         arrived = arrived + move(index, blocks)
     partial = attend(everyone, keys, values, bias, devices)
     partial = exchange(partial)
-    products = project(partial, out_weight, row_total)
+    warmed = warm(out_weight)
+    products = project(partial, warmed, out_weight, row_total)
     products = exchange(products.reshape(devices, rows * (width // HD), HD))
     result = jnp.sum(products.astype(f32), axis=0).reshape(rows, width)
-    new_pool = place(rounds, rows, meta + (fresh_slots,), new_kv, pool, arrived)
+    parts = base(rounds, rows, meta + (fresh_slots,), new_kv, pool, arrived[:-1])
+    new_pool = place(*parts, arrived[-1])
     return (result, new_pool)
 
 

time: 78 us -> 77 us (0.987)
  blocking collectives: 13.4 us -> 0 us
  waiting for transfers between devices: 21.9 us -> 28.2 us
  starting transfers between devices: 20.7 us -> 24.3 us
  Pallas kernels: 19.2 us -> 21.6 us
    all_to_all x1 -> x0, blocking collectives: 13.4 us -> none  [exchange(): return lax.all_to_all(array, 'ctx', split_axis=0, concat_axis=0, tiled=True)]
    all_to_all x2 -> x3, waiting for transfers between devices: 3.89 us -> 12.4 us  [exchange(): return lax.all_to_all(array, 'ctx', split_axis=0, concat_axis=0, tiled=True)]
    all_to_all x2 -> x3, starting transfers between devices: 11.9 us -> 15.4 us  [exchange(): return lax.all_to_all(array, 'ctx', split_axis=0, concat_axis=0, tiled=True)]
    ppermute x5, waiting for transfers between devices: 18 us -> 15.9 us  [move(): lax.ppermute(block, 'ctx', [(i, i ^ at + 1 << first) for i in range(devic...]
    pallas_call x2 -> x4, Pallas kernels: 6.72 us -> 8.38 us  [the longest x1 4.01 us: project(): pl.pallas_call(project_kernel, name='project', in_specs=[vmem, vmem, hbm]...]
  transfers between devices with their start and end apart: 7 -> 8, of which waited for: 6 -> 7; matrix products, arithmetic and copies ran while one was open for 0% -> 0% of each run, Pallas kernels for 13% -> 16%
where the time goes in v8:
time: 77 us; the launch traced here: 76.4 us
  waiting for transfers between devices  28.2 us (37%)
  starting transfers between devices  24.3 us (32%)
  Pallas kernels  21.6 us (28%)
  between operations  0.77 us (1%)
    ppermute x5, waiting for transfers between devices, move(): lax.ppermute(block, 'ctx', [(i, i ^ at + 1 << first) for i in range(devic...  15.9 us
    all_to_all x3, starting transfers between devices, exchange(): return lax.all_to_all(array, 'ctx', split_axis=0, concat_axis=0, tiled=True)  15.4 us
    all_to_all x3, waiting for transfers between devices, exchange(): return lax.all_to_all(array, 'ctx', split_axis=0, concat_axis=0, tiled=True)  12.4 us
    ppermute x5, starting transfers between devices, move(): lax.ppermute(block, 'ctx', [(i, i ^ at + 1 << first) for i in range(devic...  8.85 us
    pallas_call x1, Pallas kernels, unpack(): pl.pallas_call(functools.partial(unpack_kernel, now, rows, block_len), na...  5.98 us
    pallas_call x1, Pallas kernels, attend(): pl.pallas_call(attend_kernel, name='attend', in_specs=[vmem, vmem, hbm, v...  4.64 us
    pallas_call x1, Pallas kernels, project(): pl.pallas_call(project_kernel, name='project', in_specs=[vmem, vmem, hbm]...  4.01 us
    pallas_call x1, Pallas kernels, base(): pl.pallas_call(functools.partial(base_kernel, rounds, rows), name='base',...  2.13 us
  transfers between devices with their start and end apart: 8, of which 7 were waited for; matrix products, arithmetic and copies ran while one was open for 0% of the time, Pallas kernels for 16%

profile of v8, /device:TPU:0, one launch (start us, length us, event | category | flops | bytes accessed | tf_op | source)
XLA Modules:
  0.0 76.4 jit_solution(12347989520363378675)
XLA Ops:
  0.6 0.0 copy-start
  0.6 0.7 copy-done
  1.4 0.7 ask.1
  2.1 8.3 %all-to-all-start = ((bf16[16,1,64,128]{3,2,1,0:T(8,128)(2,1)}), bf16[16,1,64,128]{3,2,1,0:T(8,128)(2,1)S(1)}, u32[]{:S(2)}, u32[]{:S(2)}) async-start(bf16[16,1,64,128]{3,2,1,0:T(8,128)(2,1)} %ask.1), calls=%async_computation | async-start | bytes 524288 | tf_op jit(solution)/shard_map/all_to_all | solution.py:636
  10.5 6.0 %unpack.1 = (bf16[1,8,1152,128]{3,2,1,0:T(8,128)(2,1)S(1)}, bf16[1,8,1152,128]{3,2,1,0:T(8,128)(2,1)}, f32[16,128]{1,0:T(8,128)S(1)}, bf16[4,16,2,1024]{3,2,1,0:...) custom-call(s32[16]{0:T(128)} %parents_in.7, s32[4,16]{1,0:T(4,128)} %bitcast.21, ...), custom_call_target="tpu_custom_call" | custom-call | bytes 6291456 | tf_op jit(solution)/shard_map/unpack/pallas_call | solution.py:411
  16.5 3.9 %all-to-all-done = bf16[16,1,64,128]{3,2,1,0:T(8,128)(2,1)S(1)} async-done(((bf16[16,1,64,128]{3,2,1,0:T(8,128)(2,1)}), bf16[16,1,64,128]{3,2,1,0:T(8,128)(2,1)S(1)}, u32[]{:S(2)}, u32[]{:S(2)}) %all-to-all-start) | async-done | bytes 262176 | tf_op jit(solution)/shard_map/all_to_all | solution.py:636
  20.4 4.6 %attend.1 = bf16[16,1,72,128]{3,2,1,0:T(8,128)(2,1)} custom-call(bf16[16,64,128]{2,1,0:T(8,128)(2,1)S(1)} %bitcast.18, bf16[1,8,1152,128]{3,2,1,0:T(8,128)(2,1)S(1)} %get-tuple-element.11.keys, bf16[1,8,1152,128]{3,2,1,0:T(8,128)(2,1)} %get-tuple-element.12.values, f32[16,128]{1,0:T(8,128)S(1)} %get-tuple-element.13.bias), custom_call_target="tpu_custom_call" | custom-call | flops 603979776 | bytes 4718592 | tf_op jit(solution)/shard_map/attend/pallas_call | solution.py:512
  25.0 3.6 %all-to-all-start.1 = ((bf16[16,1,72,128]{3,2,1,0:T(8,128)(2,1)}), bf16[16,1,72,128]{3,2,1,0:T(8,128)(2,1)S(1)}, u32[]{:S(2)}, u32[]{:S(2)}) async-start(bf16[16,1,72,128]{3,2,1,0:T(8,128)(2,1)} %attend.1), calls=%async_computation.1 | async-start | bytes 589824 | tf_op jit(solution)/shard_map/all_to_all | solution.py:636
  28.6 1.6 %warm.1.warmed = bf16[2,512,1024]{2,1,0:T(8,128)(2,1)S(1)} custom-call(bf16[512,8192]{1,0:T(8,128)(2,1)} %weight.3), custom_call_target="tpu_custom_call" | custom-call | bytes 4194304 | tf_op jit(solution)/shard_map/warm/pallas_call | solution.py:598
  30.1 0.0 copy-start.3
  30.2 0.0 copy-start.2
  30.2 0.0 copy-start.1
  30.2 8.5 %all-to-all-done.1.partial = bf16[16,1,72,128]{3,2,1,0:T(8,128)(2,1)S(1)} async-done(((bf16[16,1,72,128]{3,2,1,0:T(8,128)(2,1)}), bf16[16,1,72,128]{3,2,1,0:T(8,128)(2,1)S(1)}, u32[]{:S(2)}, u32[]{:S(2)}) %all-to-all-start.1) | async-done | bytes 294944 | tf_op jit(solution)/shard_map/all_to_all | solution.py:636
  38.6 4.0 %project.1 = bf16[16,64,128]{2,1,0:T(8,128)(2,1)} custom-call(bf16[16,1,72,128]{3,2,1,0:T(8,128)(2,1)S(1)} %all-to-all-done.1.partial, bf16[2,512,1024]{2,1,0:T(8,128)(2,1)S(1)} %warm.1.warmed, bf16[512,8192]{1,0:T(8,128)(2,1)} %weight.3), custom_call_target="tpu_custom_call" | custom-call | flops 134217728 | bytes 8388608 | tf_op jit(solution)/shard_map/project/pallas_call | solution.py:616
  42.7 3.5 %all-to-all-start.2 = ((bf16[16,64,128]{2,1,0:T(8,128)(2,1)}), bf16[16,64,128]{2,1,0:T(8,128)(2,1)S(1)}, u32[]{:S(2)}, u32[]{:S(2)}) async-start(bf16[16,64,128]{2,1,0:T(8,128)(2,1)} %project.1), calls=%async_computation.2 | async-start | bytes 524288 | tf_op jit(solution)/shard_map/all_to_all | solution.py:636
  46.2 0.0 copy-done.3
  46.2 1.9 %collective-permute-start = (bf16[4,16,2,1024]{3,2,1,0:T(2,128)(2,1)S(1)}, bf16[4,16,2,1024]{3,2,1,0:T(2,128)(2,1)S(1)}, u32[]{:S(2)}, u32[]{:S(2)}) collective-permute-start(bf16[4,16,2,1024]{3,2,1,0:T(2,128)(2,1)S(1)} %copy-done.3), channel_id=1, source_target_pairs={{0,1},{1,0},{2,3},{3,2},{4,5},{5,4},{6,7},{7,6},{8,9},{9,8},{10,11... | collective-permute-start | bytes 786440 | tf_op jit(solution)/shard_map/ppermute | solution.py:652
  48.1 0.0 copy-done.2
  48.1 1.5 %collective-permute-start.1 = (bf16[4,16,2,1024]{3,2,1,0:T(2,128)(2,1)S(1)}, bf16[4,16,2,1024]{3,2,1,0:T(2,128)(2,1)S(1)}, u32[]{:S(2)}, u32[]{:S(2)}) collective-permute-start(bf16[4,16,2,1024]{3,2,1,0:T(2,128)(2,1)S(1)} %copy-done.2), channel_id=1, source_target_pairs={{0,2},{1,3},{2,0},{3,1},{4,6},{5,7},{6,4},{7,5},{8,10},{9,11},{10,... | collective-permute-start | bytes 786440 | tf_op jit(solution)/shard_map/ppermute | solution.py:652
  49.6 0.0 copy-done.1
  49.6 0.2 collective-permute-start.2
  49.8 8.1 %collective-permute-done.refs_0_ = bf16[4,16,2,1024]{3,2,1,0:T(2,128)(2,1)S(1)} collective-permute-done((bf16[4,16,2,1024]{3,2,1,0:T(2,128)(2,1)S(1)}, bf16[4,16,2,1024]{3,2,1,0:T(2,128)(2,1)S(1)}, u32[]{:S(2)}, u32[]{:S(2)}) %collective-permute-start) | collective-permute-done | bytes 262176 | tf_op jit(solution)/shard_map/ppermute | solution.py:652
  57.9 3.3 %collective-permute-done.1.refs_1_ = bf16[4,16,2,1024]{3,2,1,0:T(2,128)(2,1)S(1)} collective-permute-done((bf16[4,16,2,1024]{3,2,1,0:T(2,128)(2,1)S(1)}, bf16[4,16,2,1024]{3,2,1,0:T(2,128)(2,1)S(1)}, u32[]{:S(2)}, u32[]{:S(2)}) %collective-permute-start.1) | collective-permute-done | bytes 262176 | tf_op jit(solution)/shard_map/ppermute | solution.py:652
  61.2 1.4 %collective-permute-done.2.refs_2_ = bf16[4,16,2,1024]{3,2,1,0:T(2,128)(2,1)S(1)} collective-permute-done((bf16[4,16,2,1024]{3,2,1,0:T(2,128)(2,1)S(1)}, bf16[4,16,2,1024]{3,2,1,0:T(2,128)(2,1)S(1)}, u32[]{:S(2)}, u32[]{:S(2)}) %collective-permute-start.2) | collective-permute-done | bytes 262176 | tf_op jit(solution)/shard_map/ppermute | solution.py:652
  62.6 1.0 %pick.2 = bf16[2,16,2,1024]{3,2,1,0:T(2,128)(2,1)S(1)} custom-call(s32[16]{0:T(128)} %parents_in.7, s32[4,16]{1,0:T(4,128)} %bitcast.22, s32[16]{0:T(128)} %lengths_in.7, bf16[8,16,2,1024]{3,2,1,0:T(2,128)(2,1)} %pool.5, bf16[4,16,2,1024]{3,2,1,0:T(2,128)(2,1)S(1)} %collective-permute-done.refs_0_, ...), custom_call_target="tpu_custom_call" | custom-call | bytes 4194304 | tf_op jit(solution)/shard_map/pick/pallas_call | solution.py:150
  63.6 2.1 %collective-permute-start.3 = (bf16[2,16,2,1024]{3,2,1,0:T(2,128)(2,1)S(1)}, bf16[2,16,2,1024]{3,2,1,0:T(2,128)(2,1)S(1)}, u32[]{:S(2)}, u32[]{:S(2)}) collective-permute-start(bf16[2,16,2,1024]{3,2,1,0:T(2,128)(2,1)S(1)} %pick.2), channel_id=1, source_target_pairs={{0,4},{1,5},{2,6},{3,7},{4,0},{5,1},{6,2},{7,3},{8,12},{9,13},{10,... | collective-permute-start | bytes 393224 | tf_op jit(solution)/shard_map/ppermute | solution.py:652
  65.8 2.9 %collective-permute-done.3.refs_3_ = bf16[2,16,2,1024]{3,2,1,0:T(2,128)(2,1)S(1)} collective-permute-done((bf16[2,16,2,1024]{3,2,1,0:T(2,128)(2,1)S(1)}, bf16[2,16,2,1024]{3,2,1,0:T(2,128)(2,1)S(1)}, u32[]{:S(2)}, u32[]{:S(2)}) %collective-permute-start.3) | collective-permute-done | bytes 131104 | tf_op jit(solution)/shard_map/ppermute | solution.py:652
  68.7 0.9 %pick.3 = bf16[1,16,2,1024]{3,2,1,0:T(2,128)(2,1)S(1)} custom-call(s32[16]{0:T(128)} %parents_in.7, s32[4,16]{1,0:T(4,128)} %bitcast.23, s32[16]{0:T(128)} %lengths_in.7, bf16[8,16,2,1024]{3,2,1,0:T(2,128)(2,1)} %pool.5, bf16[4,16,2,1024]{3,2,1,0:T(2,128)(2,1)S(1)} %collective-permute-done.refs_0_, ...), custom_call_target="tpu_custom_call" | custom-call | bytes 4194304 | tf_op jit(solution)/shard_map/pick/pallas_call | solution.py:150
  69.6 3.2 %collective-permute-start.4 = (bf16[1,16,2,1024]{3,2,1,0:T(2,128)(2,1)S(1)}, bf16[1,16,2,1024]{3,2,1,0:T(2,128)(2,1)S(1)}, u32[]{:S(2)}, u32[]{:S(2)}) collective-permute-start(bf16[1,16,2,1024]{3,2,1,0:T(2,128)(2,1)S(1)} %pick.3), channel_id=1, source_target_pairs={{0,8},{1,9},{2,10},{3,11},{4,12},{5,13},{6,14},{7,15},{8,0},{9,1},... | collective-permute-start | bytes 196616 | tf_op jit(solution)/shard_map/ppermute | solution.py:652
  72.8 2.1 %base.1 = (bf16[8,16,2,1024]{3,2,1,0:T(2,128)(2,1)}, bf16[2,16,2,1024]{3,2,1,0:T(2,128)(2,1)S(1)}, bf16[1,2,16,2,1024]{4,3,2,1,0:T(2,128)(2,1)S(1)}) custom-call(s32[16]{0:T(128)} %parents_in.7, s32[4,16]{1,0:T(4,128)} %bitcast.24, s32[16]{0:T(128)} %lengths_in.7, s32[16]{0:T(128)} %fresh_in.1, bf16[1,2,1024]{2,1,0:T(2,128)(2,1)} %new_in.1, ...), custom_call_target="tpu_custom_call" | custom-call | bytes 1048576 | tf_op jit(solution)/shard_map/base/pallas_call | solution.py:222
  74.9 0.1 collective-permute-done.4.last
  75.0 0.7 place.1
  75.7 0.0 all-to-all-done.2
  75.7 0.7 convert_reduce_fusion
Async XLA Ops:
  0.6 0.8 copy-start
  2.1 18.2 %all-to-all-start = ((bf16[16,1,64,128]{3,2,1,0:T(8,128)(2,1)}), bf16[16,1,64,128]{3,2,1,0:T(8,128)(2,1)S(1)}, u32[]{:S(2)}, u32[]{:S(2)}) async-start(bf16[16,1,64,128]{3,2,1,0:T(8,128)(2,1)} %ask.1), calls=%async_computation | async-start | bytes 524288 | tf_op jit(solution)/shard_map/all_to_all | solution.py:636
  25.0 13.6 %all-to-all-start.1 = ((bf16[16,1,72,128]{3,2,1,0:T(8,128)(2,1)}), bf16[16,1,72,128]{3,2,1,0:T(8,128)(2,1)S(1)}, u32[]{:S(2)}, u32[]{:S(2)}) async-start(bf16[16,1,72,128]{3,2,1,0:T(8,128)(2,1)} %attend.1), calls=%async_computation.1 | async-start | bytes 589824 | tf_op jit(solution)/shard_map/all_to_all | solution.py:636
  30.1 16.1 %copy-start.3 = (bf16[4,16,2,1024]{3,2,1,0:T(2,128)(2,1)S(1)}, bf16[4,16,2,1024]{3,2,1,0:T(2,128)(2,1)}, u32[]{:S(2)}) copy-start(bf16[4,16,2,1024]{3,2,1,0:T(2,128)(2,1)} %get-tuple-element.14) | copy-start | bytes 786436
  30.2 18.0 %copy-start.2 = (bf16[4,16,2,1024]{3,2,1,0:T(2,128)(2,1)S(1)}, bf16[4,16,2,1024]{3,2,1,0:T(2,128)(2,1)}, u32[]{:S(2)}) copy-start(bf16[4,16,2,1024]{3,2,1,0:T(2,128)(2,1)} %get-tuple-element.15) | copy-start | bytes 786436
  30.2 19.4 %copy-start.1 = (bf16[4,16,2,1024]{3,2,1,0:T(2,128)(2,1)S(1)}, bf16[4,16,2,1024]{3,2,1,0:T(2,128)(2,1)}, u32[]{:S(2)}) copy-start(bf16[4,16,2,1024]{3,2,1,0:T(2,128)(2,1)} %get-tuple-element.16) | copy-start | bytes 786436
  42.7 33.0 %all-to-all-start.2 = ((bf16[16,64,128]{2,1,0:T(8,128)(2,1)}), bf16[16,64,128]{2,1,0:T(8,128)(2,1)S(1)}, u32[]{:S(2)}, u32[]{:S(2)}) async-start(bf16[16,64,128]{2,1,0:T(8,128)(2,1)} %project.1), calls=%async_computation.2 | async-start | bytes 524288 | tf_op jit(solution)/shard_map/all_to_all | solution.py:636
  46.2 11.6 %collective-permute-start = (bf16[4,16,2,1024]{3,2,1,0:T(2,128)(2,1)S(1)}, bf16[4,16,2,1024]{3,2,1,0:T(2,128)(2,1)S(1)}, u32[]{:S(2)}, u32[]{:S(2)}) collective-permute-start(bf16[4,16,2,1024]{3,2,1,0:T(2,128)(2,1)S(1)} %copy-done.3), channel_id=1, source_target_pairs={{0,1},{1,0},{2,3},{3,2},{4,5},{5,4},{6,7},{7,6},{8,9},{9,8},{10,11... | collective-permute-start | bytes 786440 | tf_op jit(solution)/shard_map/ppermute | solution.py:652
  48.1 13.1 %collective-permute-start.1 = (bf16[4,16,2,1024]{3,2,1,0:T(2,128)(2,1)S(1)}, bf16[4,16,2,1024]{3,2,1,0:T(2,128)(2,1)S(1)}, u32[]{:S(2)}, u32[]{:S(2)}) collective-permute-start(bf16[4,16,2,1024]{3,2,1,0:T(2,128)(2,1)S(1)} %copy-done.2), channel_id=1, source_target_pairs={{0,2},{1,3},{2,0},{3,1},{4,6},{5,7},{6,4},{7,5},{8,10},{9,11},{10,... | collective-permute-start | bytes 786440 | tf_op jit(solution)/shard_map/ppermute | solution.py:652
  49.6 13.0 %collective-permute-start.2 = (bf16[4,16,2,1024]{3,2,1,0:T(2,128)(2,1)S(1)}, bf16[4,16,2,1024]{3,2,1,0:T(2,128)(2,1)S(1)}, u32[]{:S(2)}, u32[]{:S(2)}) collective-permute-start(bf16[4,16,2,1024]{3,2,1,0:T(2,128)(2,1)S(1)} %copy-done.1), channel_id=1, source_target_pairs={{0,3},{1,2},{2,1},{3,0},{4,7},{5,6},{6,5},{7,4},{8,11},{9,10},{10,... | collective-permute-start | bytes 786440 | tf_op jit(solution)/shard_map/ppermute | solution.py:652
  63.6 5.1 %collective-permute-start.3 = (bf16[2,16,2,1024]{3,2,1,0:T(2,128)(2,1)S(1)}, bf16[2,16,2,1024]{3,2,1,0:T(2,128)(2,1)S(1)}, u32[]{:S(2)}, u32[]{:S(2)}) collective-permute-start(bf16[2,16,2,1024]{3,2,1,0:T(2,128)(2,1)S(1)} %pick.2), channel_id=1, source_target_pairs={{0,4},{1,5},{2,6},{3,7},{4,0},{5,1},{6,2},{7,3},{8,12},{9,13},{10,... | collective-permute-start | bytes 393224 | tf_op jit(solution)/shard_map/ppermute | solution.py:652
  69.6 5.4 %collective-permute-start.4 = (bf16[1,16,2,1024]{3,2,1,0:T(2,128)(2,1)S(1)}, bf16[1,16,2,1024]{3,2,1,0:T(2,128)(2,1)S(1)}, u32[]{:S(2)}, u32[]{:S(2)}) collective-permute-start(bf16[1,16,2,1024]{3,2,1,0:T(2,128)(2,1)S(1)} %pick.3), channel_id=1, source_target_pairs={{0,8},{1,9},{2,10},{3,11},{4,12},{5,13},{6,14},{7,15},{8,0},{9,1},... | collective-permute-start | bytes 196616 | tf_op jit(solution)/shard_map/ppermute | solution.py:652

commit v9 on v8

--- a/solution.py
+++ b/solution.py
@@ -28,6 +28,22 @@
     return pltpu.with_memory_space_constraint(array, pltpu.HBM)
 
 
+def div(value, size):
+    return value >> (size.bit_length() - 1) if size & (size - 1) == 0 else lax.div(value, size)
+
+
+def rem(value, size):
+    return value & (size - 1) if size & (size - 1) == 0 else lax.rem(value, size)
+
+
+def each(count, body):
+    if count <= 4:
+        for at in range(count):
+            body(at, 0)
+    else:
+        lax.fori_loop(0, count, body, 0)
+
+
 def rounds_of(devices):
     total = devices.bit_length() - 1
     return [(0, 2)] + [(bit, 1) for bit in range(2, total)]
@@ -51,17 +67,21 @@
 def source_of(row, parents, table, lengths, block_len):
     parent = parents[row]
     length = lengths[parent]
-    return length, table[length // block_len, parent]
+    return length, table[div(length, block_len), parent]
 
 
 def fetch_block(rounds, me, source, dest, part, rows, pool, arrived, target, sem):
     pool_dev = pool.shape[0]
     done = sum(bits for _, bits in rounds)
-    moved = (source // pool_dev ^ me) & ((1 << done) - 1)
+    moved = (div(source, pool_dev) ^ me) & ((1 << done) - 1)
+
+    if not rounds:
+        pltpu.make_async_copy(pool.at[rem(source, pool_dev)], target, sem).start()
+        return
 
     @pl.when(moved == 0)
     def _():
-        pltpu.make_async_copy(pool.at[source % pool_dev], target, sem).start()
+        pltpu.make_async_copy(pool.at[rem(source, pool_dev)], target, sem).start()
 
     for (first, mask), ref in zip(channels_of(rounds), arrived):
         bits = dict(rounds)[first]
@@ -79,15 +99,15 @@
         low = (me & ((1 << (first + bits)) - 1)) ^ (mask << first)
 
         def begin(at, carry):
-            dest = (at // rows << (first + bits)) | low
-            part = at % rows
+            dest = (at << (first + bits)) | low if rows == 1 else (at // rows << (first + bits)) | low
+            part = 0 if rows == 1 else at % rows
             _, source = source_of(dest * rows + part, *meta, pool.shape[1])
             fetch_block(
                 rounds, me, source, dest, part, rows, pool, arrived, out.at[at], sem.at[mask - 1, at]
             )
             return carry
 
-        lax.fori_loop(0, out.shape[0], begin, 0)
+        each(out.shape[0], begin)
 
 
 def end_picks(pool, outs, sem):
@@ -97,7 +117,7 @@
             pltpu.make_async_copy(pool.at[0], out.at[at], sem.at[index, at]).wait()
             return carry
 
-        lax.fori_loop(0, out.shape[0], finish, 0)
+        each(out.shape[0], finish)
 
 
 def ask_kernel(query, out, wide):
@@ -194,8 +214,8 @@
             rounds[:-1], me, source, me, part, rows, pool, arrived, tail.at[slot], sems.at[1]
         )
         pltpu.make_async_copy(pool.at[0], tail.at[slot], sems.at[1]).wait()
-        offset = length % block_len
-        awaited = (((source // pool_dev) ^ me) >> bit) & 1
+        offset = rem(length, block_len)
+        awaited = ((div(source, pool_dev) ^ me) >> bit) & 1
 
         def token(at, carry):
             @pl.when((at < offset) & (awaited == 1))
@@ -240,7 +260,7 @@
     )(*map(in_hbm, meta + (new_kv, pool)), *arrived)
 
 
-def place_kernel(whole, tail, mask, last, out, merged, sem):
+def place_kernel(whole, tail, mask, last, products, out, result, merged, sem):
     old = out.shape[0] - CAP
     block = tail[...]
     for part in range(mask.shape[0]):
@@ -248,22 +268,29 @@
     merged[...] = block
     copy = pltpu.make_async_copy(merged, out.at[pl.ds(old, CAP)], sem)
     copy.start()
+    total = products[0].astype(f32)
+    for device in range(1, products.shape[0]):
+        total = total + products[device].astype(f32)
+    result[...] = total
     copy.wait()
 
 
-def place(whole, tail, mask, last):
+def place(whole, tail, mask, last, products):
     vmem, hbm = pl.BlockSpec(memory_space=pltpu.VMEM), pl.BlockSpec(memory_space=pltpu.HBM)
     return pl.pallas_call(
         place_kernel,
         name="place",
-        in_specs=[hbm, vmem, vmem, vmem],
-        out_specs=hbm,
-        out_shape=pltpu.HBM(whole.shape, bf16),
+        in_specs=[hbm, vmem, vmem, vmem, vmem],
+        out_specs=[hbm, vmem],
+        out_shape=[
+            pltpu.HBM(whole.shape, bf16),
+            jax.ShapeDtypeStruct(products.shape[1:], f32),
+        ],
         input_output_aliases={0: 0},
         scratch_shapes=[pltpu.VMEM(tail.shape, bf16), pltpu.SemaphoreType.DMA],
         compiler_params=pltpu.CompilerParams(vmem_limit_bytes=VMEM_LIMIT),
         cost_estimate=pl.CostEstimate(flops=0, bytes_accessed=4 * tail.size, transcendentals=0),
-    )(whole, tail, mask, last)
+    )(whole, tail, mask, last, products)
 
 
 def pieces(value):
@@ -359,7 +386,7 @@
         return carry
 
     position = lax.broadcasted_iota(jnp.int32, (1, tokens), 1)
-    in_block, at_block = position % block_len, position // block_len
+    in_block, at_block = rem(position, block_len), div(position, block_len)
     for request in range(requests):
         for chunk in range(chunks):
             load(request, chunk).start()
@@ -667,10 +694,9 @@
     warmed = warm(out_weight)
     products = project(partial, warmed, out_weight, row_total)
     products = exchange(products.reshape(devices, rows * (width // HD), HD))
-    result = jnp.sum(products.astype(f32), axis=0).reshape(rows, width)
     parts = base(rounds, rows, meta + (fresh_slots,), new_kv, pool, arrived[:-1])
-    new_pool = place(*parts, arrived[-1])
-    return (result, new_pool)
+    new_pool, result = place(*parts, arrived[-1], products)
+    return (result.reshape(rows, width), new_pool)
 
 
 def solution(mesh):

time: 77 us -> 77 us (level)
  transfers between devices with their start and end apart: 8 -> 8, of which waited for: 7 -> 7; matrix products, arithmetic and copies ran while one was open for 0% -> 0% of each run, Pallas kernels for 16% -> 15%
where the time goes in v9:
time: 77 us; the launch traced here: 76.3 us
  waiting for transfers between devices  28.4 us (37%)
  starting transfers between devices  24.3 us (32%)
  Pallas kernels  22.1 us (29%)
    ppermute x5, waiting for transfers between devices, move(): lax.ppermute(block, 'ctx', [(i, i ^ at + 1 << first) for i in range(devic...  15.9 us
    all_to_all x3, starting transfers between devices, exchange(): return lax.all_to_all(array, 'ctx', split_axis=0, concat_axis=0, tiled=True)  15.4 us
    all_to_all x3, waiting for transfers between devices, exchange(): return lax.all_to_all(array, 'ctx', split_axis=0, concat_axis=0, tiled=True)  12.5 us
    ppermute x5, starting transfers between devices, move(): lax.ppermute(block, 'ctx', [(i, i ^ at + 1 << first) for i in range(devic...  8.88 us
    pallas_call x1, Pallas kernels, unpack(): pl.pallas_call(functools.partial(unpack_kernel, now, rows, block_len), na...  5.87 us
    pallas_call x1, Pallas kernels, attend(): pl.pallas_call(attend_kernel, name='attend', in_specs=[vmem, vmem, hbm, v...  4.64 us
    pallas_call x1, Pallas kernels, project(): pl.pallas_call(project_kernel, name='project', in_specs=[vmem, vmem, hbm]...  3.99 us
    pallas_call x1, Pallas kernels, base(): pl.pallas_call(functools.partial(base_kernel, rounds, rows), name='base',...  2.13 us
  transfers between devices with their start and end apart: 8, of which 7 were waited for; matrix products, arithmetic and copies ran while one was open for 0% of the time, Pallas kernels for 15%

profile of v9, /device:TPU:0, one launch (start us, length us, event | category | flops | bytes accessed | tf_op | source)
XLA Modules:
  0.0 76.3 jit_solution(944820753987256613)
XLA Ops:
  0.6 0.0 copy-start
  0.6 0.7 copy-done
  1.4 0.7 ask.1
  2.1 8.3 %all-to-all-start = ((bf16[16,1,64,128]{3,2,1,0:T(8,128)(2,1)}), bf16[16,1,64,128]{3,2,1,0:T(8,128)(2,1)S(1)}, u32[]{:S(2)}, u32[]{:S(2)}) async-start(bf16[16,1,64,128]{3,2,1,0:T(8,128)(2,1)} %ask.1), calls=%async_computation | async-start | bytes 524288 | tf_op jit(solution)/shard_map/all_to_all | solution.py:663
  10.5 5.9 %unpack.1 = (bf16[1,8,1152,128]{3,2,1,0:T(8,128)(2,1)S(1)}, bf16[1,8,1152,128]{3,2,1,0:T(8,128)(2,1)}, f32[16,128]{1,0:T(8,128)S(1)}, bf16[4,16,2,1024]{3,2,1,0:...) custom-call(s32[16]{0:T(128)} %parents_in.7, s32[4,16]{1,0:T(4,128)} %bitcast.21, ...), custom_call_target="tpu_custom_call" | custom-call | bytes 6291456 | tf_op jit(solution)/shard_map/unpack/pallas_call | solution.py:438
  16.4 4.0 %all-to-all-done = bf16[16,1,64,128]{3,2,1,0:T(8,128)(2,1)S(1)} async-done(((bf16[16,1,64,128]{3,2,1,0:T(8,128)(2,1)}), bf16[16,1,64,128]{3,2,1,0:T(8,128)(2,1)S(1)}, u32[]{:S(2)}, u32[]{:S(2)}) %all-to-all-start) | async-done | bytes 262176 | tf_op jit(solution)/shard_map/all_to_all | solution.py:663
  20.4 4.6 %attend.1 = bf16[16,1,72,128]{3,2,1,0:T(8,128)(2,1)} custom-call(bf16[16,64,128]{2,1,0:T(8,128)(2,1)S(1)} %bitcast.18, bf16[1,8,1152,128]{3,2,1,0:T(8,128)(2,1)S(1)} %get-tuple-element.19.keys, bf16[1,8,1152,128]{3,2,1,0:T(8,128)(2,1)} %get-tuple-element.20.values, f32[16,128]{1,0:T(8,128)S(1)} %get-tuple-element.21.bias), custom_call_target="tpu_custom_call" | custom-call | flops 603979776 | bytes 4718592 | tf_op jit(solution)/shard_map/attend/pallas_call | solution.py:539
  25.0 3.6 %all-to-all-start.1 = ((bf16[16,1,72,128]{3,2,1,0:T(8,128)(2,1)}), bf16[16,1,72,128]{3,2,1,0:T(8,128)(2,1)S(1)}, u32[]{:S(2)}, u32[]{:S(2)}) async-start(bf16[16,1,72,128]{3,2,1,0:T(8,128)(2,1)} %attend.1), calls=%async_computation.1 | async-start | bytes 589824 | tf_op jit(solution)/shard_map/all_to_all | solution.py:663
  28.6 1.6 %warm.1.warmed = bf16[2,512,1024]{2,1,0:T(8,128)(2,1)S(1)} custom-call(bf16[512,8192]{1,0:T(8,128)(2,1)} %weight.3), custom_call_target="tpu_custom_call" | custom-call | bytes 4194304 | tf_op jit(solution)/shard_map/warm/pallas_call | solution.py:625
  30.1 0.0 copy-start.3
  30.2 0.0 copy-start.2
  30.2 0.0 copy-start.1
  30.2 8.5 %all-to-all-done.1.partial = bf16[16,1,72,128]{3,2,1,0:T(8,128)(2,1)S(1)} async-done(((bf16[16,1,72,128]{3,2,1,0:T(8,128)(2,1)}), bf16[16,1,72,128]{3,2,1,0:T(8,128)(2,1)S(1)}, u32[]{:S(2)}, u32[]{:S(2)}) %all-to-all-start.1) | async-done | bytes 294944 | tf_op jit(solution)/shard_map/all_to_all | solution.py:663
  38.6 4.0 %project.1 = bf16[16,64,128]{2,1,0:T(8,128)(2,1)} custom-call(bf16[16,1,72,128]{3,2,1,0:T(8,128)(2,1)S(1)} %all-to-all-done.1.partial, bf16[2,512,1024]{2,1,0:T(8,128)(2,1)S(1)} %warm.1.warmed, bf16[512,8192]{1,0:T(8,128)(2,1)} %weight.3), custom_call_target="tpu_custom_call" | custom-call | flops 134217728 | bytes 8388608 | tf_op jit(solution)/shard_map/project/pallas_call | solution.py:643
  42.6 3.5 %all-to-all-start.2 = ((bf16[16,64,128]{2,1,0:T(8,128)(2,1)}), bf16[16,64,128]{2,1,0:T(8,128)(2,1)S(1)}, u32[]{:S(2)}, u32[]{:S(2)}) async-start(bf16[16,64,128]{2,1,0:T(8,128)(2,1)} %project.1), calls=%async_computation.2 | async-start | bytes 524288 | tf_op jit(solution)/shard_map/all_to_all | solution.py:663
  46.2 0.0 copy-done.3
  46.2 1.9 %collective-permute-start = (bf16[4,16,2,1024]{3,2,1,0:T(2,128)(2,1)S(1)}, bf16[4,16,2,1024]{3,2,1,0:T(2,128)(2,1)S(1)}, u32[]{:S(2)}, u32[]{:S(2)}) collective-permute-start(bf16[4,16,2,1024]{3,2,1,0:T(2,128)(2,1)S(1)} %copy-done.3), channel_id=1, source_target_pairs={{0,1},{1,0},{2,3},{3,2},{4,5},{5,4},{6,7},{7,6},{8,9},{9,8},{10,11... | collective-permute-start | bytes 786440 | tf_op jit(solution)/shard_map/ppermute | solution.py:679
  48.1 0.0 copy-done.2
  48.1 1.5 %collective-permute-start.1 = (bf16[4,16,2,1024]{3,2,1,0:T(2,128)(2,1)S(1)}, bf16[4,16,2,1024]{3,2,1,0:T(2,128)(2,1)S(1)}, u32[]{:S(2)}, u32[]{:S(2)}) collective-permute-start(bf16[4,16,2,1024]{3,2,1,0:T(2,128)(2,1)S(1)} %copy-done.2), channel_id=1, source_target_pairs={{0,2},{1,3},{2,0},{3,1},{4,6},{5,7},{6,4},{7,5},{8,10},{9,11},{10,... | collective-permute-start | bytes 786440 | tf_op jit(solution)/shard_map/ppermute | solution.py:679
  49.6 0.0 copy-done.1
  49.6 0.2 collective-permute-start.2
  49.8 8.1 %collective-permute-done.refs_0_ = bf16[4,16,2,1024]{3,2,1,0:T(2,128)(2,1)S(1)} collective-permute-done((bf16[4,16,2,1024]{3,2,1,0:T(2,128)(2,1)S(1)}, bf16[4,16,2,1024]{3,2,1,0:T(2,128)(2,1)S(1)}, u32[]{:S(2)}, u32[]{:S(2)}) %collective-permute-start) | collective-permute-done | bytes 262176 | tf_op jit(solution)/shard_map/ppermute | solution.py:679
  57.8 3.3 %collective-permute-done.1.refs_1_ = bf16[4,16,2,1024]{3,2,1,0:T(2,128)(2,1)S(1)} collective-permute-done((bf16[4,16,2,1024]{3,2,1,0:T(2,128)(2,1)S(1)}, bf16[4,16,2,1024]{3,2,1,0:T(2,128)(2,1)S(1)}, u32[]{:S(2)}, u32[]{:S(2)}) %collective-permute-start.1) | collective-permute-done | bytes 262176 | tf_op jit(solution)/shard_map/ppermute | solution.py:679
  61.2 1.4 %collective-permute-done.2.refs_2_ = bf16[4,16,2,1024]{3,2,1,0:T(2,128)(2,1)S(1)} collective-permute-done((bf16[4,16,2,1024]{3,2,1,0:T(2,128)(2,1)S(1)}, bf16[4,16,2,1024]{3,2,1,0:T(2,128)(2,1)S(1)}, u32[]{:S(2)}, u32[]{:S(2)}) %collective-permute-start.2) | collective-permute-done | bytes 262176 | tf_op jit(solution)/shard_map/ppermute | solution.py:679
  62.6 1.0 %pick.2 = bf16[2,16,2,1024]{3,2,1,0:T(2,128)(2,1)S(1)} custom-call(s32[16]{0:T(128)} %parents_in.7, s32[4,16]{1,0:T(4,128)} %bitcast.22, s32[16]{0:T(128)} %lengths_in.7, bf16[8,16,2,1024]{3,2,1,0:T(2,128)(2,1)} %pool.5, bf16[4,16,2,1024]{3,2,1,0:T(2,128)(2,1)S(1)} %collective-permute-done.refs_0_, ...), custom_call_target="tpu_custom_call" | custom-call | bytes 4194304 | tf_op jit(solution)/shard_map/pick/pallas_call | solution.py:170
  63.6 2.2 %collective-permute-start.3 = (bf16[2,16,2,1024]{3,2,1,0:T(2,128)(2,1)S(1)}, bf16[2,16,2,1024]{3,2,1,0:T(2,128)(2,1)S(1)}, u32[]{:S(2)}, u32[]{:S(2)}) collective-permute-start(bf16[2,16,2,1024]{3,2,1,0:T(2,128)(2,1)S(1)} %pick.2), channel_id=1, source_target_pairs={{0,4},{1,5},{2,6},{3,7},{4,0},{5,1},{6,2},{7,3},{8,12},{9,13},{10,... | collective-permute-start | bytes 393224 | tf_op jit(solution)/shard_map/ppermute | solution.py:679
  65.7 2.9 %collective-permute-done.3.refs_3_ = bf16[2,16,2,1024]{3,2,1,0:T(2,128)(2,1)S(1)} collective-permute-done((bf16[2,16,2,1024]{3,2,1,0:T(2,128)(2,1)S(1)}, bf16[2,16,2,1024]{3,2,1,0:T(2,128)(2,1)S(1)}, u32[]{:S(2)}, u32[]{:S(2)}) %collective-permute-start.3) | collective-permute-done | bytes 131104 | tf_op jit(solution)/shard_map/ppermute | solution.py:679
  68.7 0.9 %pick.3 = bf16[1,16,2,1024]{3,2,1,0:T(2,128)(2,1)S(1)} custom-call(s32[16]{0:T(128)} %parents_in.7, s32[4,16]{1,0:T(4,128)} %bitcast.23, s32[16]{0:T(128)} %lengths_in.7, bf16[8,16,2,1024]{3,2,1,0:T(2,128)(2,1)} %pool.5, bf16[4,16,2,1024]{3,2,1,0:T(2,128)(2,1)S(1)} %collective-permute-done.refs_0_, ...), custom_call_target="tpu_custom_call" | custom-call | bytes 4194304 | tf_op jit(solution)/shard_map/pick/pallas_call | solution.py:170
  69.6 3.2 %collective-permute-start.4 = (bf16[1,16,2,1024]{3,2,1,0:T(2,128)(2,1)S(1)}, bf16[1,16,2,1024]{3,2,1,0:T(2,128)(2,1)S(1)}, u32[]{:S(2)}, u32[]{:S(2)}) collective-permute-start(bf16[1,16,2,1024]{3,2,1,0:T(2,128)(2,1)S(1)} %pick.3), channel_id=1, source_target_pairs={{0,8},{1,9},{2,10},{3,11},{4,12},{5,13},{6,14},{7,15},{8,0},{9,1},... | collective-permute-start | bytes 196616 | tf_op jit(solution)/shard_map/ppermute | solution.py:679
  72.7 2.1 %base.1 = (bf16[8,16,2,1024]{3,2,1,0:T(2,128)(2,1)}, bf16[2,16,2,1024]{3,2,1,0:T(2,128)(2,1)S(1)}, bf16[1,2,16,2,1024]{4,3,2,1,0:T(2,128)(2,1)S(1)}) custom-call(s32[16]{0:T(128)} %parents_in.7, s32[4,16]{1,0:T(4,128)} %bitcast.24, s32[16]{0:T(128)} %lengths_in.7, s32[16]{0:T(128)} %fresh_in.1, bf16[1,2,1024]{2,1,0:T(2,128)(2,1)} %new_in.1, ...), custom_call_target="tpu_custom_call" | custom-call | bytes 1048576 | tf_op jit(solution)/shard_map/base/pallas_call | solution.py:242
  74.9 0.1 collective-permute-done.4.last
  75.0 0.0 all-to-all-done.2.products
  75.0 1.3 %place.1 = (bf16[8,16,2,1024]{3,2,1,0:T(2,128)(2,1)}, f32[64,128]{1,0:T(8,128)}) custom-call(bf16[8,16,2,1024]{3,2,1,0:T(2,128)(2,1)} %get-tuple-element.16.whole, bf16[2,16,2,1024]{3,2,1,0:T(2,128)(2,1)S(1)} %get-tuple-element.17.tail, bf16[1,2,16,2,1024]{4,3,2,1,0:T(2,128)(2,1)S(1)} %get-tuple-element.18.mask, ...), custom_call_target="tpu_custom_call", output_to_operand_aliasing={{0}: (0, {})} | custom-call | bytes 262144 | tf_op jit(solution)/shard_map/place/pallas_call | solution.py:280
Async XLA Ops:
  0.6 0.8 copy-start
  2.1 18.2 %all-to-all-start = ((bf16[16,1,64,128]{3,2,1,0:T(8,128)(2,1)}), bf16[16,1,64,128]{3,2,1,0:T(8,128)(2,1)S(1)}, u32[]{:S(2)}, u32[]{:S(2)}) async-start(bf16[16,1,64,128]{3,2,1,0:T(8,128)(2,1)} %ask.1), calls=%async_computation | async-start | bytes 524288 | tf_op jit(solution)/shard_map/all_to_all | solution.py:663
  25.0 13.6 %all-to-all-start.1 = ((bf16[16,1,72,128]{3,2,1,0:T(8,128)(2,1)}), bf16[16,1,72,128]{3,2,1,0:T(8,128)(2,1)S(1)}, u32[]{:S(2)}, u32[]{:S(2)}) async-start(bf16[16,1,72,128]{3,2,1,0:T(8,128)(2,1)} %attend.1), calls=%async_computation.1 | async-start | bytes 589824 | tf_op jit(solution)/shard_map/all_to_all | solution.py:663
  30.1 16.1 %copy-start.3 = (bf16[4,16,2,1024]{3,2,1,0:T(2,128)(2,1)S(1)}, bf16[4,16,2,1024]{3,2,1,0:T(2,128)(2,1)}, u32[]{:S(2)}) copy-start(bf16[4,16,2,1024]{3,2,1,0:T(2,128)(2,1)} %get-tuple-element.13) | copy-start | bytes 786436
  30.2 17.9 %copy-start.2 = (bf16[4,16,2,1024]{3,2,1,0:T(2,128)(2,1)S(1)}, bf16[4,16,2,1024]{3,2,1,0:T(2,128)(2,1)}, u32[]{:S(2)}) copy-start(bf16[4,16,2,1024]{3,2,1,0:T(2,128)(2,1)} %get-tuple-element.14) | copy-start | bytes 786436
  30.2 19.4 %copy-start.1 = (bf16[4,16,2,1024]{3,2,1,0:T(2,128)(2,1)S(1)}, bf16[4,16,2,1024]{3,2,1,0:T(2,128)(2,1)}, u32[]{:S(2)}) copy-start(bf16[4,16,2,1024]{3,2,1,0:T(2,128)(2,1)} %get-tuple-element.15) | copy-start | bytes 786436
  42.6 32.3 %all-to-all-start.2 = ((bf16[16,64,128]{2,1,0:T(8,128)(2,1)}), bf16[16,64,128]{2,1,0:T(8,128)(2,1)S(1)}, u32[]{:S(2)}, u32[]{:S(2)}) async-start(bf16[16,64,128]{2,1,0:T(8,128)(2,1)} %project.1), calls=%async_computation.2 | async-start | bytes 524288 | tf_op jit(solution)/shard_map/all_to_all | solution.py:663
  46.2 11.6 %collective-permute-start = (bf16[4,16,2,1024]{3,2,1,0:T(2,128)(2,1)S(1)}, bf16[4,16,2,1024]{3,2,1,0:T(2,128)(2,1)S(1)}, u32[]{:S(2)}, u32[]{:S(2)}) collective-permute-start(bf16[4,16,2,1024]{3,2,1,0:T(2,128)(2,1)S(1)} %copy-done.3), channel_id=1, source_target_pairs={{0,1},{1,0},{2,3},{3,2},{4,5},{5,4},{6,7},{7,6},{8,9},{9,8},{10,11... | collective-permute-start | bytes 786440 | tf_op jit(solution)/shard_map/ppermute | solution.py:679
  48.1 13.1 %collective-permute-start.1 = (bf16[4,16,2,1024]{3,2,1,0:T(2,128)(2,1)S(1)}, bf16[4,16,2,1024]{3,2,1,0:T(2,128)(2,1)S(1)}, u32[]{:S(2)}, u32[]{:S(2)}) collective-permute-start(bf16[4,16,2,1024]{3,2,1,0:T(2,128)(2,1)S(1)} %copy-done.2), channel_id=1, source_target_pairs={{0,2},{1,3},{2,0},{3,1},{4,6},{5,7},{6,4},{7,5},{8,10},{9,11},{10,... | collective-permute-start | bytes 786440 | tf_op jit(solution)/shard_map/ppermute | solution.py:679
  49.6 13.0 %collective-permute-start.2 = (bf16[4,16,2,1024]{3,2,1,0:T(2,128)(2,1)S(1)}, bf16[4,16,2,1024]{3,2,1,0:T(2,128)(2,1)S(1)}, u32[]{:S(2)}, u32[]{:S(2)}) collective-permute-start(bf16[4,16,2,1024]{3,2,1,0:T(2,128)(2,1)S(1)} %copy-done.1), channel_id=1, source_target_pairs={{0,3},{1,2},{2,1},{3,0},{4,7},{5,6},{6,5},{7,4},{8,11},{9,10},{10,... | collective-permute-start | bytes 786440 | tf_op jit(solution)/shard_map/ppermute | solution.py:679
  63.6 5.1 %collective-permute-start.3 = (bf16[2,16,2,1024]{3,2,1,0:T(2,128)(2,1)S(1)}, bf16[2,16,2,1024]{3,2,1,0:T(2,128)(2,1)S(1)}, u32[]{:S(2)}, u32[]{:S(2)}) collective-permute-start(bf16[2,16,2,1024]{3,2,1,0:T(2,128)(2,1)S(1)} %pick.2), channel_id=1, source_target_pairs={{0,4},{1,5},{2,6},{3,7},{4,0},{5,1},{6,2},{7,3},{8,12},{9,13},{10,... | collective-permute-start | bytes 393224 | tf_op jit(solution)/shard_map/ppermute | solution.py:679
  69.6 5.4 %collective-permute-start.4 = (bf16[1,16,2,1024]{3,2,1,0:T(2,128)(2,1)S(1)}, bf16[1,16,2,1024]{3,2,1,0:T(2,128)(2,1)S(1)}, u32[]{:S(2)}, u32[]{:S(2)}) collective-permute-start(bf16[1,16,2,1024]{3,2,1,0:T(2,128)(2,1)S(1)} %pick.3), channel_id=1, source_target_pairs={{0,8},{1,9},{2,10},{3,11},{4,12},{5,13},{6,14},{7,15},{8,0},{9,1},... | collective-permute-start | bytes 196616 | tf_op jit(solution)/shard_map/ppermute | solution.py:679
